TPU v7x, 32 devices: a whole 2x2x4 slice. The times are simulated.
32 devices in a mesh: dom: 8 (over z, core), seg: 4 (over y, x).
Axes of the slice: x: 2, y: 2, z: 4, core: 2. Of those that a mesh axis runs over, the one named last changes fastest.
Arguments:
- state: float32 [256, 9, 64], P(('dom', 'seg'))
- counts: int32 [256], P(('dom', 'seg')), may hold values from 16 to 64
- neighbours: int32 [256, 26], P(('dom', 'seg')), may hold values from 0 to 95, as said below
- new_place: int32 [256], P(('dom', 'seg')), may hold values from 0 to 31, as said below
Outputs:
- moved_state: float32 [256, 9, 64], P(('dom', 'seg'))
- moved_density: float32 [256, 64], P(('dom', 'seg'))
Inputs may be any that keep to these rules, and one draw needn't show every extreme that they name: `neighbours`: each row lists 26 distinct region indices in 0 to 95, never the block's own index 32 + k. `new_place`: within each domain range the 32 values are a permutation.
All inputs are finite; a program needn't handle non-finite values.
Results may differ from a plain program's by a relative error of at most 0.00002.
Values sent between devices are 32-bit elements; how exact they have to be, the bound alone decides.
No kernel may reach another device: no remote copies, remote signals or barrier semaphores. Data moves between devices by JAX's collectives and lax.ppermute only.
A program may use at most 64 MiB of HBM per device.

v0:
```python
import math

import jax
import jax.numpy as jnp
from jax import lax
from jax.sharding import PartitionSpec as P

SIGMA = 21.0 / (16.0 * math.pi)
GAMMA_LESS = 2.0 / 3.0
STEP_DT = 0.1


def with_halo(block, sides, width):
    for axis, dim in sides:
        count = lax.axis_size(axis)
        forward = [(i, i + 1) for i in range(count - 1)]
        backward = [(target, source) for source, target in forward]
        low = lax.ppermute(
            lax.slice_in_dim(block, block.shape[dim] - width, None, axis=dim), axis, forward
        )
        high = lax.ppermute(lax.slice_in_dim(block, 0, width, axis=dim), axis, backward)
        block = jnp.concatenate([low, block, high], axis=dim)
    return block


def offsets(own_pos, far_pos):
    return own_pos[:, :, None] - far_pos[:, None, :]


def density_tile(own, far):
    diff = offsets(own[0:3], far[0:3])
    dist = jnp.sqrt(jnp.sum(diff * diff, axis=0))
    smooth = own[7][:, None]
    ratio = dist / smooth
    shell = jnp.maximum(1.0 - 0.5 * ratio, 0.0)
    kernel = SIGMA / smooth**3 * shell**4 * (1.0 + 2.0 * ratio)
    return jnp.sum(kernel * far[6][None, :], axis=1)


def slope(own, far):
    diff = offsets(own[0:3], far[0:3])
    dist = jnp.sqrt(jnp.sum(diff * diff, axis=0))
    smooth = 0.5 * (own[7][:, None] + far[7][None, :])
    ratio = dist / smooth
    shell = jnp.maximum(1.0 - 0.5 * ratio, 0.0)
    factor = -5.0 * SIGMA / smooth**5 * shell**3
    return (diff, factor)


def tensor_tile(own, far, far_vol):
    diff, factor = slope(own, far)
    weight = -factor * far_vol[None, :]
    pairs = ((0, 0), (1, 1), (2, 2), (0, 1), (0, 2), (1, 2))
    return jnp.stack([jnp.sum(weight * diff[a] * diff[b], axis=1) for a, b in pairs])


def corrected(tensor):
    return jnp.stack(
        [2.0 - tensor[0], 2.0 - tensor[1], 2.0 - tensor[2], -tensor[3], -tensor[4], -tensor[5]]
    )


def apply_sym(sym, vec):
    first = sym[0] * vec[0] + sym[3] * vec[1] + sym[4] * vec[2]
    second = sym[3] * vec[0] + sym[1] * vec[1] + sym[5] * vec[2]
    third = sym[4] * vec[0] + sym[5] * vec[1] + sym[2] * vec[2]
    return jnp.stack([first, second, third])


def momentum_tile(own, own_corr, own_press, far, far_corr, far_press):
    diff, factor = slope(own, far)
    scaled = diff * factor[None]
    grad_own = apply_sym(own_corr[:, :, None], scaled)
    grad_far = apply_sym(far_corr[:, None, :], scaled)
    mass_far = far[6][None, :]
    accel = -jnp.sum(
        mass_far[None]
        * (own_press[None, :, None] * grad_own + far_press[None, None, :] * grad_far),
        axis=2,
    )
    dvel = own[3:6][:, :, None] - far[3:6][:, None, :]
    heat = own_press * jnp.sum(mass_far * jnp.sum(dvel * grad_own, axis=0), axis=1)
    return (accel, heat)


def tile_of(region, index):
    tile = jnp.take(region, index, axis=0)
    if tile.ndim == 3:
        return jnp.moveaxis(tile, 0, 1).reshape(tile.shape[1], -1)
    return tile.reshape(-1)


def spread(values, slab):
    whole = lax.all_gather(values, "seg", axis=0, tiled=True)
    return with_halo(whole, (("dom", 0),), slab)


def local(state, counts, neighbours, new_place):
    blocks = state.shape[0]
    width = state.shape[2]
    groups = lax.axis_size("seg")
    slab = blocks * groups
    seg_index = lax.axis_index("seg")
    live = (jnp.arange(width, dtype=jnp.int32)[None, :] < counts[:, None]).astype(jnp.float32)
    base = jnp.concatenate([state[:, 0:6], (state[:, 6] * live)[:, None], state[:, 7:9]], axis=1)
    own_rows = seg_index * blocks + jnp.arange(blocks, dtype=jnp.int32)
    lists = jnp.concatenate([(slab + own_rows)[:, None], neighbours], axis=1)
    block_ids = jnp.arange(blocks, dtype=jnp.int32)
    region_state = spread(base, slab)

    def first(b):
        return density_tile(base[b], tile_of(region_state, lists[b]))

    rho = lax.map(first, block_ids) + (1.0 - live)
    vol = base[:, 6] / rho
    region_vol = spread(vol, slab)

    def second(b):
        return tensor_tile(base[b], tile_of(region_state, lists[b]), tile_of(region_vol, lists[b]))

    corr = jnp.moveaxis(corrected(jnp.moveaxis(lax.map(second, block_ids), 1, 0)), 0, 1)
    press = GAMMA_LESS * base[:, 8] / rho
    extra = jnp.concatenate([corr, press[:, None]], axis=1)
    region_extra = spread(extra, slab)

    def third(b):
        far_extra = tile_of(region_extra, lists[b])
        return momentum_tile(
            base[b],
            corr[b],
            press[b],
            tile_of(region_state, lists[b]),
            far_extra[0:6],
            far_extra[6],
        )

    accel, heat = lax.map(third, block_ids)
    accel = accel * live[:, None]
    heat = heat * live
    velocity = state[:, 3:6] + STEP_DT * accel
    position = state[:, 0:3] + STEP_DT * velocity
    energy = state[:, 8] + STEP_DT * heat
    updated = jnp.concatenate([position, velocity, state[:, 6:8], energy[:, None]], axis=1)
    place_float = new_place.astype(jnp.float32)
    all_state, all_rho, all_place = (
        lax.all_gather(updated, "seg", axis=0, tiled=True),
        lax.all_gather(rho, "seg", axis=0, tiled=True),
        lax.all_gather(place_float, "seg", axis=0, tiled=True),
    )
    wanted = all_place.astype(jnp.int32)
    source = jnp.sum(
        jnp.where(
            wanted[None, :] == own_rows[:, None], jnp.arange(slab, dtype=jnp.int32)[None, :], 0
        ),
        axis=1,
    )
    return (jnp.take(all_state, source, axis=0), jnp.take(all_rho, source, axis=0))


def solution(mesh):
    return jax.shard_map(
        local,
        mesh=mesh,
        in_specs=(
            P(("dom", "seg"), None, None),
            P(("dom", "seg")),
            P(("dom", "seg"), None),
            P(("dom", "seg")),
        ),
        out_specs=(P(("dom", "seg"), None, None), P(("dom", "seg"), None)),
        check_vma=False,
    )
```

profile of v0, /device:TPU:1, one launch (start us, length us, event | category | flops | bytes accessed | tf_op | source)
XLA Modules:
  0.0 215.6 jit_solution(7203631403740827378)
XLA Ops:
  0.6 0.8 fusion.34
  1.4 0.7 slice.211
  2.1 0.8 fusion.30
  2.9 7.9 %all_gather.19 = f32[32,9,64]{2,0,1:T(8,128)S(1)} all-gather(f32[8,9,64]{2,0,1:T(8,128)S(1)} %pad_maximum_fusion.4), channel_id=1, replica_groups=mesh['dom'=8,'seg'=4] {'seg'}, dimensions={0}, use_global_device_ids=true | all-gather | bytes 92160 | tf_op jit(solution)/shard_map/all_gather | solution.py:94
  10.8 4.6 %collective-permute-start.1 = (f32[32,9,64]{2,0,1:T(8,128)S(1)}, f32[32,9,64]{2,0,1:T(8,128)S(1)}, u32[]{:S(2)}, u32[]{:S(2)}) collective-permute-start(f32[32,9,64]{2,0,1:T(8,128)S(1)} %all_gather.19), channel_id=1, source_target_pairs={{4,0},{8,4},{12,8},{16,12},{20,16},{24,20},{28,24},{5,1},{9,5},{13... | collective-permute-start | bytes 221192 | tf_op jit(solution)/shard_map/ppermute | solution.py:21
  15.4 3.1 %collective-permute-start = (f32[32,9,64]{2,0,1:T(8,128)S(1)}, f32[32,9,64]{2,0,1:T(8,128)S(1)}, u32[]{:S(2)}, u32[]{:S(2)}) collective-permute-start(f32[32,9,64]{2,0,1:T(8,128)S(1)} %all_gather.19), channel_id=1, source_target_pairs={{0,4},{4,8},{8,12},{12,16},{16,20},{20,24},{24,28},{1,5},{5,9},{9,... | collective-permute-start | bytes 221192 | tf_op jit(solution)/shard_map/ppermute | solution.py:18
  18.6 1.2 dynamic-slice
  20.4 0.8 convert_dynamic-update-slice_fusion
  21.1 7.0 %all-reduce = f32[32]{0:T(128)S(1)} all-reduce(f32[32]{0:T(128)S(1)} %convert_dynamic-update-slice_fusion), channel_id=1, replica_groups=mesh['dom'=8,'seg'=4] {'seg'}, use_global_device_ids=true, to_apply=%add | all-reduce | flops 32 | bytes 256
  28.3 0.7 fusion.29
  29.3 0.8 pad_add_fusion
  31.1 31.5 %while.32 = (s32[]{:T(128)}, f32[8,64]{1,0:T(8,128)S(1)}, s32[8]{0:T(128)S(1)}, f32[8,9,64]{2,1,0:T(8,128)S(1)}, s32[8,27]{1,0:T(8,128)S(1)}, /*index=5*/f32[96,...) while((s32[]{:T(128)}, f32[8,64]{1,0:T(8,128)S(1)}, s32[8]{0:T(128)S(1)}, ...), condition=%wide.region_4.6_spmd, body=%wide.region_1.5_spmd.sunk | while | flops 2228712 | bytes 1322401 | solution.py:114
  62.7 6.1 %all_gather.20 = f32[32,64]{1,0:T(8,128)S(1)} all-gather(f32[8,64]{1,0:T(8,128)S(1)} %get-tuple-element.254), channel_id=1, replica_groups=mesh['dom'=8,'seg'=4] {'seg'}, dimensions={0}, use_global_device_ids=true | all-gather | bytes 10240 | tf_op jit(solution)/shard_map/all_gather | solution.py:94
  68.8 5.2 %collective-permute-start.3 = (f32[32,64]{1,0:T(8,128)S(1)}, f32[32,64]{1,0:T(8,128)S(1)}, u32[]{:S(2)}, u32[]{:S(2)}) collective-permute-start(f32[32,64]{1,0:T(8,128)S(1)} %all_gather.20), channel_id=1, source_target_pairs={{4,0},{8,4},{12,8},{16,12},{20,16},{24,20},{28,24},{5,1},{9,5},{13... | collective-permute-start | bytes 24584 | tf_op jit(solution)/shard_map/ppermute | solution.py:21
  74.0 3.1 %collective-permute-start.2 = (f32[32,64]{1,0:T(8,128)S(1)}, f32[32,64]{1,0:T(8,128)S(1)}, u32[]{:S(2)}, u32[]{:S(2)}) collective-permute-start(f32[32,64]{1,0:T(8,128)S(1)} %all_gather.20), channel_id=1, source_target_pairs={{0,4},{4,8},{8,12},{12,16},{16,20},{20,24},{24,28},{1,5},{5,9},{9,... | collective-permute-start | bytes 24584 | tf_op jit(solution)/shard_map/ppermute | solution.py:18
  77.1 5.2 %all_gather.23 = f32[32,64]{1,0:T(8,128)S(1)} all-gather(f32[8,64]{1,0:T(8,128)S(1)} %get-tuple-element.255), channel_id=1, replica_groups=mesh['dom'=8,'seg'=4] {'seg'}, dimensions={0}, use_global_device_ids=true | all-gather | bytes 10240 | tf_op jit(solution)/shard_map/all_gather | solution.py:147
  82.9 45.3 %while.33 = (s32[]{:T(128)}, f32[8,6,64]{2,0,1:T(8,128)S(1)}, s32[8]{0:T(128)S(1)}, f32[8,9,64]{2,1,0:T(8,128)S(1)}, s32[8,27]{1,0:T(8,128)S(1)}, /*index=5*/f32...) while((s32[]{:T(128)}, f32[8,6,64]{2,0,1:T(8,128)S(1)}, ...), condition=%wide.region_13.15_spmd, body=%wide.region_5.14_spmd.sunk | while | flops 4221689 | bytes 4039032 | solution.py:121
  82.9 0.7 dynamic_slice.68
  87.7 0.8 multiply_reduce_fusion.17
  93.3 0.8 multiply_reduce_fusion.17
  99.0 0.8 multiply_reduce_fusion.17
  104.7 0.8 multiply_reduce_fusion.17
  110.3 0.8 multiply_reduce_fusion.17
  116.0 0.8 multiply_reduce_fusion.17
  121.7 0.8 multiply_reduce_fusion.17
  127.3 0.8 multiply_reduce_fusion.17
  128.4 6.8 %all_gather.21 = f32[32,7,64]{2,0,1:T(8,128)S(1)} all-gather(f32[8,7,64]{2,0,1:T(8,128)S(1)} %pad_maximum_fusion.6), channel_id=1, replica_groups=mesh['dom'=8,'seg'=4] {'seg'}, dimensions={0}, use_global_device_ids=true | all-gather | bytes 71680 | tf_op jit(solution)/shard_map/all_gather | solution.py:94
  135.1 5.3 %collective-permute-start.5 = (f32[32,7,64]{2,0,1:T(8,128)S(1)}, f32[32,7,64]{2,0,1:T(8,128)S(1)}, u32[]{:S(2)}, u32[]{:S(2)}) collective-permute-start(f32[32,7,64]{2,0,1:T(8,128)S(1)} %all_gather.21), channel_id=1, source_target_pairs={{4,0},{8,4},{12,8},{16,12},{20,16},{24,20},{28,24},{5,1},{9,5},{13... | collective-permute-start | bytes 172040 | tf_op jit(solution)/shard_map/ppermute | solution.py:21
  140.4 3.1 %collective-permute-start.4 = (f32[32,7,64]{2,0,1:T(8,128)S(1)}, f32[32,7,64]{2,0,1:T(8,128)S(1)}, u32[]{:S(2)}, u32[]{:S(2)}) collective-permute-start(f32[32,7,64]{2,0,1:T(8,128)S(1)} %all_gather.21), channel_id=1, source_target_pairs={{0,4},{4,8},{8,12},{12,16},{16,20},{20,24},{24,28},{1,5},{5,9},{9,... | collective-permute-start | bytes 172040 | tf_op jit(solution)/shard_map/ppermute | solution.py:18
  144.2 1.1 collective-permute-done.4
  145.6 61.7 %while.34 = (s32[]{:T(128)}, f32[8,3,64]{2,0,1:T(8,128)S(1)}, f32[8,64]{1,0:T(8,128)S(1)}, s32[8]{0:T(128)S(1)}, s32[8,27]{1,0:T(8,128)S(1)}, /*index=5*/f32[96,...) while((s32[]{:T(128)}, f32[8,3,64]{2,0,1:T(8,128)S(1)}, ...), condition=%wide.region_19.21_spmd, body=%wide.region_14.20_spmd.sunk | while | flops 10425598 | bytes 13043228 | solution.py:137
  207.3 6.9 %all_gather.22 = f32[32,9,64]{2,0,1:T(8,128)S(1)} all-gather(f32[8,9,64]{2,0,1:T(8,128)S(1)} %pad_maximum_fusion.5), channel_id=1, replica_groups=mesh['dom'=8,'seg'=4] {'seg'}, dimensions={0}, use_global_device_ids=true | all-gather | bytes 92160 | tf_op jit(solution)/shard_map/all_gather | solution.py:146
  (668 shorter events, 85.8 us)
Async XLA Ops:
  10.8 19.3 %collective-permute-start.1 = (f32[32,9,64]{2,0,1:T(8,128)S(1)}, f32[32,9,64]{2,0,1:T(8,128)S(1)}, u32[]{:S(2)}, u32[]{:S(2)}) collective-permute-start(f32[32,9,64]{2,0,1:T(8,128)S(1)} %all_gather.19), channel_id=1, source_target_pairs={{4,0},{8,4},{12,8},{16,12},{20,16},{24,20},{28,24},{5,1},{9,5},{13... | collective-permute-start | bytes 221192 | tf_op jit(solution)/shard_map/ppermute | solution.py:21
  15.4 14.8 %collective-permute-start = (f32[32,9,64]{2,0,1:T(8,128)S(1)}, f32[32,9,64]{2,0,1:T(8,128)S(1)}, u32[]{:S(2)}, u32[]{:S(2)}) collective-permute-start(f32[32,9,64]{2,0,1:T(8,128)S(1)} %all_gather.19), channel_id=1, source_target_pairs={{0,4},{4,8},{8,12},{12,16},{16,20},{20,24},{24,28},{1,5},{5,9},{9,... | collective-permute-start | bytes 221192 | tf_op jit(solution)/shard_map/ppermute | solution.py:18
  31.1 31.5 %copy-start = (f32[8,9,64]{2,0,1:T(8,128)S(1)}, f32[8,9,64]{2,0,1:T(8,128)}, u32[]{:S(2)}) copy-start(f32[8,9,64]{2,0,1:T(8,128)} %param.12) | copy-start | bytes 55300
  31.1 31.5 %copy-start.1 = (s32[8]{0:T(128)S(1)}, s32[8]{0:T(128)}, u32[]{:S(2)}) copy-start(s32[8]{0:T(128)} %param.13) | copy-start | bytes 100
  68.8 14.1 %collective-permute-start.3 = (f32[32,64]{1,0:T(8,128)S(1)}, f32[32,64]{1,0:T(8,128)S(1)}, u32[]{:S(2)}, u32[]{:S(2)}) collective-permute-start(f32[32,64]{1,0:T(8,128)S(1)} %all_gather.20), channel_id=1, source_target_pairs={{4,0},{8,4},{12,8},{16,12},{20,16},{24,20},{28,24},{5,1},{9,5},{13... | collective-permute-start | bytes 24584 | tf_op jit(solution)/shard_map/ppermute | solution.py:21
  74.0 8.9 %collective-permute-start.2 = (f32[32,64]{1,0:T(8,128)S(1)}, f32[32,64]{1,0:T(8,128)S(1)}, u32[]{:S(2)}, u32[]{:S(2)}) collective-permute-start(f32[32,64]{1,0:T(8,128)S(1)} %all_gather.20), channel_id=1, source_target_pairs={{0,4},{4,8},{8,12},{12,16},{16,20},{20,24},{24,28},{1,5},{5,9},{9,... | collective-permute-start | bytes 24584 | tf_op jit(solution)/shard_map/ppermute | solution.py:18
  135.1 9.0 %collective-permute-start.5 = (f32[32,7,64]{2,0,1:T(8,128)S(1)}, f32[32,7,64]{2,0,1:T(8,128)S(1)}, u32[]{:S(2)}, u32[]{:S(2)}) collective-permute-start(f32[32,7,64]{2,0,1:T(8,128)S(1)} %all_gather.21), channel_id=1, source_target_pairs={{4,0},{8,4},{12,8},{16,12},{20,16},{24,20},{28,24},{5,1},{9,5},{13... | collective-permute-start | bytes 172040 | tf_op jit(solution)/shard_map/ppermute | solution.py:21
  140.4 4.9 %collective-permute-start.4 = (f32[32,7,64]{2,0,1:T(8,128)S(1)}, f32[32,7,64]{2,0,1:T(8,128)S(1)}, u32[]{:S(2)}, u32[]{:S(2)}) collective-permute-start(f32[32,7,64]{2,0,1:T(8,128)S(1)} %all_gather.21), channel_id=1, source_target_pairs={{0,4},{4,8},{8,12},{12,16},{16,20},{20,24},{24,28},{1,5},{5,9},{9,... | collective-permute-start | bytes 172040 | tf_op jit(solution)/shard_map/ppermute | solution.py:18
where the time goes:
time: 218 us; the launch traced here: 216 us
  local copies, waits for them, and re-layouts  60.2 us (28%)
  loops' own time  49.9 us (23%)
  blocking collectives  39.9 us (18%)
  other arithmetic  38.6 us (18%)
  starting transfers between devices  24.3 us (11%)
    gather x40, local copies, waits for them, and re-layouts, tile_of(): tile = jnp.take(region, index, axis=0)  23.2 us
    all_gather x3, blocking collectives, spread(): whole = lax.all_gather(values, 'seg', axis=0, tiled=True)  20.8 us
    another operation x1, loops' own time, local(): accel, heat = lax.map(third, block_ids)  18.2 us
    another operation x1, loops' own time, local(): lax.map(second, block_ids)  17.5 us
    dynamic_slice x24, local copies, waits for them, and re-layouts, local(): rho = lax.map(first, block_ids) + (1.0 - live)  15.3 us
    ppermute x3, starting transfers between devices, with_halo(): lax.ppermute(lax.slice_in_dim(block, 0, width, axis=dim), axis, backward)  15 us
    another operation x1, loops' own time, local(): rho = lax.map(first, block_ids) + (1.0 - live)  14.1 us
    ppermute x3, starting transfers between devices, with_halo(): lax.ppermute(lax.slice_in_dim(block, block.shape[dim] - width, None, axis...  9.3 us
  transfers between devices with their start and end apart: 6, of which 1 were waited for; matrix products, arithmetic and copies ran while one was open for 2% of the time, Pallas kernels for 0%

commit v1 on v0

v1 whole, which is shorter than its diff:
```python
import functools
import math

import jax
import jax.numpy as jnp
from jax import lax
from jax.experimental import pallas as pl
from jax.experimental.pallas import tpu as pltpu
from jax.sharding import PartitionSpec as P

SIGMA = 21.0 / (16.0 * math.pi)
GAMMA_LESS = 2.0 / 3.0
STEP_DT = 0.1
SLOPE = -5.0 * SIGMA * 32.0
TINY = 1e-37
SUB = 8
LANES = 128
X, VEL, MASS, SMOOTH = 0, 3, 6, 7
VMEM = pltpu.VMEM
SMEM = pltpu.SMEM


def lane_iota(rows=SUB):
    return lax.broadcasted_iota(jnp.int32, (rows, LANES), 1)


def row_iota(rows=SUB):
    return lax.broadcasted_iota(jnp.int32, (rows, LANES), 0)


def call(body, outs, scratch=(), in_specs=None, out_specs=None, name=None):
    return pl.pallas_call(
        body,
        out_shape=outs,
        in_specs=in_specs,
        out_specs=out_specs,
        scratch_shapes=list(scratch),
        compiler_params=pltpu.CompilerParams(vmem_limit_bytes=56 << 20),
        name=name,
    )


def shape(*dims, dtype=jnp.float32):
    return jax.ShapeDtypeStruct(dims, dtype)


def pack_body(blocks, width, nbr, counts, place, state, lists, out):
    pairs = blocks // 2
    lane = lane_iota()
    row = row_iota()
    low = lane < width
    meta = jnp.concatenate(
        [lists[...].astype(jnp.float32), jnp.zeros((blocks, LANES - nbr), jnp.float32)], axis=1
    )
    for b in range(blocks):
        meta = jnp.where((row == b) & (lane == nbr), place[b].astype(jnp.float32), meta)
    base = pairs * SUB
    out[base : base + SUB, :] = meta
    for p in range(pairs):
        full = jnp.concatenate([state[2 * p], state[2 * p + 1]], axis=1)
        live = lane < jnp.where(low, counts[2 * p], counts[2 * p + 1] + width)
        tile = full[0:SUB]
        out[p * SUB : (p + 1) * SUB, :] = jnp.where((row == MASS) & jnp.logical_not(live), 0.0, tile)
        out[base + SUB + p : base + SUB + p + 1, :] = full[8:9]
        out[base + SUB + pairs + p : base + SUB + pairs + p + 1, :] = full[MASS : MASS + 1]
        out[base + 2 * SUB + p : base + 2 * SUB + p + 1, :] = jnp.where(live, 1.0, 0.0)[0:1]
    out[base + 2 * SUB + pairs : base + 3 * SUB, :] = jnp.zeros((SUB - pairs, LANES), jnp.float32)


def range_bases(slab):
    odd = lax.rem(lax.axis_index("dom"), 2)
    first = jnp.where(odd == 0, 2 * slab, 0)
    second = jnp.where(odd == 0, 0, 2 * slab)
    return first, second


def spread_tile(tile, width):
    low = lane_iota(tile.shape[0]) < width
    turned = pltpu.roll(tile, width, axis=1)
    return jnp.where(low, tile, turned), jnp.where(low, turned, tile)


def far_pair(left, right):
    return jnp.where(lane_iota(left.shape[0]) < LANES // 2, left, right)


def column(value, index):
    return jnp.broadcast_to(value[:, index : index + 1], (SUB, LANES))


def own_columns(cols, turned, d):
    turned[...] = pltpu.roll(cols[...], lax.rem(LANES - d * SUB, LANES), axis=1)


def put(result, g, slot, value):
    rows = pl.ds(pl.multiple_of(g * SUB, SUB), SUB)
    total = jnp.sum(value, axis=1, keepdims=True)
    result[rows, :] = jnp.where(lane_iota() == slot, total, result[rows, :])


def far_row(ref, d, t, field):
    return jnp.broadcast_to(ref[d, t, field : field + 1, :], (SUB, LANES))


def distance(own, far):
    dx, dy, dz = own[0] - far[0], own[1] - far[1], own[2] - far[2]
    square = dx * dx + dy * dy + dz * dz
    return (dx, dy, dz), square * lax.rsqrt(jnp.maximum(square, TINY))


def density_body(groups, blocks, width, nbr, tiles, *refs):
    seg = refs[:groups]
    first, second = refs[groups : groups + 2]
    (vol_out, rho_out, far, cols, own_rows, index_out) = refs[groups + 2 : groups + 8]
    (region, aux, meta, table, inverse, own_tiles, turned, result, sem) = refs[groups + 8 :]
    slab = groups * blocks
    pairs = blocks // 2
    main = pairs * SUB
    me = lax.axis_index("seg")
    base_first, base_second = range_bases(slab)
    for k in range(groups):
        s = jnp.bitwise_xor(me, k)
        for base, tile in (
            (slab, seg[k][main : main + SUB, :]),
            (base_first, first[k * (main + SUB) + main : (k + 1) * (main + SUB), :]),
            (base_second, second[k * (main + SUB) + main : (k + 1) * (main + SUB), :]),
        ):
            rows = pl.ds(pl.multiple_of(base + s * blocks, SUB), SUB)
            meta[rows, :] = tile.astype(jnp.int32)
    copy = pltpu.make_async_copy(meta, table, sem)
    copy.start()
    for k in range(groups):
        s = jnp.bitwise_xor(me, k)
        for base, ref, start in (
            (slab, seg[k], 0),
            (base_first, first, k * (main + SUB)),
            (base_second, second, k * (main + SUB)),
        ):
            for p in range(pairs):
                even, odd = spread_tile(ref[start + p * SUB : start + (p + 1) * SUB, :], width)
                at = base + s * blocks + 2 * p
                region[at] = even
                region[at + 1] = odd
        aux[2 * s] = seg[k][main + SUB : main + 2 * SUB, :]
        aux[2 * s + 1] = seg[k][main + 2 * SUB : main + 3 * SUB, :]
    region[3 * slab] = jnp.zeros((SUB, LANES), jnp.float32)
    own_tiles[...] = jnp.zeros_like(own_tiles)
    result[...] = jnp.zeros_like(result)
    copy.wait()

    def invert(k, carry):
        inverse[table[slab + k, nbr]] = k
        return carry

    lax.fori_loop(0, slab, invert, 0)
    lane = lane_iota(1)

    def gather(d, carry):
        k = inverse[me * blocks + d]
        tile = region[slab + k]
        own_tiles[pl.ds(pl.multiple_of(d * SUB, SUB), SUB), :] = tile
        own_rows[pl.ds(d, SUB, stride=SUB), :] = tile
        s, b = k // blocks, lax.rem(k, blocks)
        p, half = b // 2, lax.rem(b, 2)
        for n, (at, r) in enumerate(((2 * s, p), (2 * s, pairs + p), (2 * s + 1, p))):
            value = aux[at, pl.ds(r, 1), :]
            other = pltpu.roll(value, width, axis=1)
            value = jnp.where(lane // width == half, value, other)
            own_rows[pl.ds((SUB + n) * SUB + d, 1), :] = value
        for t in range(tiles):
            pick = []
            for n in (2 * t, 2 * t + 1):
                if n == 0:
                    pick.append(slab + k)
                elif n <= nbr:
                    pick.append(table[slab + k, n - 1])
                else:
                    pick.append(3 * slab)
            far[d, t] = far_pair(region[pick[0]], region[pick[1]])
        return carry

    lax.fori_loop(0, blocks, gather, 0)
    cols[...] = jnp.transpose(own_tiles[...])[0:width, :]

    def slot(d, carry):
        own_columns(cols, turned, d)

        def group(g, carry):
            own = turned[pl.ds(pl.multiple_of(g * SUB, SUB), SUB), :]
            pos = [column(own, X + a) for a in range(3)]
            scale = 0.5 / column(own, SMOOTH)
            total = jnp.zeros((SUB, LANES), jnp.float32)
            for t in range(tiles):
                _, dist = distance(pos, [far_row(far, d, t, X + a) for a in range(3)])
                ratio = dist * scale
                shell = jnp.maximum(1.0 - ratio, 0.0)
                shell = shell * shell
                shell = shell * shell
                total += shell * (far_row(far, d, t, MASS) * (1.0 + 4.0 * ratio))
            put(result, g, d, total)
            return carry

        return lax.fori_loop(0, width // SUB, group, carry)

    lax.fori_loop(0, blocks, slot, 0)
    sums = jnp.transpose(result[...])[0:SUB, 0:width]
    smooth = own_rows[SMOOTH * SUB : (SMOOTH + 1) * SUB, 0:width]
    live = own_rows[10 * SUB : 11 * SUB, 0:width]
    rho = SIGMA / (smooth * smooth * smooth) * sums + (1.0 - live)
    rho_out[...] = rho
    vol = own_rows[MASS * SUB : (MASS + 1) * SUB, 0:width] / rho
    vol_out[...] = jnp.concatenate([vol, vol], axis=1)

    def remap(d, carry):
        k = inverse[me * blocks + d]
        for n in range(2 * tiles):
            if n == 0:
                j = slab + k
            elif n <= nbr:
                j = table[slab + k, n - 1]
            else:
                index_out[d, n] = 3 * slab
                continue
            start = jnp.where(j < slab, 0, jnp.where(j < 2 * slab, slab, 2 * slab))
            index_out[d, n] = start + table[j, nbr]
        return carry

    lax.fori_loop(0, blocks, remap, 0)


def factor_body(blocks, width, tiles, far, cols, out, turned):
    def slot(d, carry):
        own_columns(cols, turned, d)

        def group(g, carry):
            own = turned[pl.ds(pl.multiple_of(g * SUB, SUB), SUB), :]
            pos = [column(own, X + a) for a in range(3)]
            smooth = column(own, SMOOTH)
            for t in range(tiles):
                _, dist = distance(pos, [far_row(far, d, t, X + a) for a in range(3)])
                inv = 1.0 / (smooth + far_row(far, d, t, SMOOTH))
                inv2 = inv * inv
                part = jnp.maximum(inv - dist * inv2, 0.0)
                out[d, g, t] = part * part * part * inv2
            return carry

        return lax.fori_loop(0, width // SUB, group, carry)

    lax.fori_loop(0, blocks, slot, 0)


def place_region(groups, blocks, refs, store):
    slab = groups * blocks
    me = lax.axis_index("seg")
    base_first, base_second = range_bases(slab)
    size = refs[0].shape[0]
    for k in range(groups):
        s = jnp.bitwise_xor(me, k)
        for base, ref, start in (
            (slab, refs[k], 0),
            (base_first, refs[groups], k * size),
            (base_second, refs[groups + 1], k * size),
        ):
            store(pl.multiple_of(base + s * blocks, SUB), ref, start)


def tensor_body(groups, blocks, width, tiles, *refs):
    index = refs[0]
    far, cols, own_rows, factor, rho = refs[1:6]
    vols = refs[6 : 6 + groups + 2]
    coef_out, corr_out = refs[8 + groups : 10 + groups]
    turned, region, far_vol, result = refs[10 + groups :]
    slab = groups * blocks

    def store(at, ref, start):
        region[pl.ds(at, SUB), :] = ref[start : start + SUB, :]

    place_region(groups, blocks, vols, store)
    region[3 * slab : 3 * slab + SUB, :] = jnp.zeros((SUB, LANES), jnp.float32)
    result[...] = jnp.zeros_like(result)

    def slot(d, carry):
        own_columns(cols, turned, d)
        for t in range(tiles):
            left = region[pl.ds(index[d, 2 * t], 1), :]
            right = region[pl.ds(index[d, 2 * t + 1], 1), :]
            far_vol[t] = jnp.broadcast_to(far_pair(left, right), (SUB, LANES))

        def group(g, carry):
            own = turned[pl.ds(pl.multiple_of(g * SUB, SUB), SUB), :]
            pos = [column(own, X + a) for a in range(3)]
            total = [jnp.zeros((SUB, LANES), jnp.float32) for _ in range(6)]
            for t in range(tiles):
                dx, dy, dz = [pos[a] - far_row(far, d, t, X + a) for a in range(3)]
                weight = factor[d, g, t] * far_vol[t]
                wx, wy, wz = weight * dx, weight * dy, weight * dz
                for n, term in enumerate((wx * dx, wy * dy, wz * dz, wx * dy, wx * dz, wy * dz)):
                    total[n] += term
            for n in range(6):
                put(result, g, n * blocks + d, total[n])
            return carry

        return lax.fori_loop(0, width // SUB, group, carry)

    lax.fori_loop(0, blocks, slot, 0)
    sums = jnp.transpose(result[...])
    press = GAMMA_LESS * own_rows[SUB * SUB : 9 * SUB, 0:width] / rho[...]
    scale = own_rows[MASS * SUB : (MASS + 1) * SUB, 0:width] * press
    coefs = []
    for n in range(6):
        tensor = SLOPE * sums[n * blocks : (n + 1) * blocks, 0:width]
        corr = (2.0 + tensor) if n < 3 else tensor
        corr_out[n] = corr
        coefs.append(scale * corr)
    corr_out[6] = press
    for n in range(3):
        coef_out[n * SUB : (n + 1) * SUB, :] = jnp.concatenate([coefs[n], coefs[n + 3]], axis=1)


def moment_body(blocks, width, tiles, far, cols, factor, out, turned, result):
    result[...] = jnp.zeros_like(result)

    def slot(d, carry):
        own_columns(cols, turned, d)

        def group(g, carry):
            own = turned[pl.ds(pl.multiple_of(g * SUB, SUB), SUB), :]
            pos = [column(own, X + a) for a in range(3)]
            vel = [column(own, VEL + a) for a in range(3)]
            total = [jnp.zeros((SUB, LANES), jnp.float32) for _ in range(9)]
            for t in range(tiles):
                weight = factor[d, g, t] * far_row(far, d, t, MASS)
                px, py, pz = [weight * (pos[a] - far_row(far, d, t, X + a)) for a in range(3)]
                vx, vy, vz = [vel[a] - far_row(far, d, t, VEL + a) for a in range(3)]
                terms = (
                    px,
                    py,
                    pz,
                    vx * px,
                    vy * py,
                    vz * pz,
                    vx * py + vy * px,
                    vx * pz + vz * px,
                    vy * pz + vz * py,
                )
                for n, term in enumerate(terms):
                    total[n] += term
            for n in range(9):
                put(result, g, n * blocks + d, total[n])
            return carry

        return lax.fori_loop(0, width // SUB, group, carry)

    lax.fori_loop(0, blocks, slot, 0)
    sums = jnp.transpose(result[...])
    for n in range(9):
        out[n] = sums[n * blocks : (n + 1) * blocks, 0:width]


def update_body(groups, blocks, width, tiles, *refs):
    index = refs[0]
    far, cols, own_rows, factor, corr, moments = refs[1:7]
    coefs = refs[7 : 9 + groups]
    state_out = refs[9 + groups]
    turned, region, far_coef, result = refs[10 + groups :]
    slab = groups * blocks

    def store(at, ref, start):
        for n in range(3):
            low, high = spread_tile(ref[start + n * SUB : start + (n + 1) * SUB, :], width)
            region[n, pl.ds(at, SUB), :] = low
            region[n + 3, pl.ds(at, SUB), :] = high

    place_region(groups, blocks, coefs, store)
    for n in range(6):
        region[n, 3 * slab : 3 * slab + SUB, :] = jnp.zeros((SUB, LANES), jnp.float32)
    result[...] = jnp.zeros_like(result)

    def slot(d, carry):
        own_columns(cols, turned, d)
        for t in range(tiles):
            one, two = index[d, 2 * t], index[d, 2 * t + 1]
            for n in range(6):
                value = far_pair(region[n, pl.ds(one, 1), :], region[n, pl.ds(two, 1), :])
                far_coef[t, n] = jnp.broadcast_to(value, (SUB, LANES))

        def group(g, carry):
            own = turned[pl.ds(pl.multiple_of(g * SUB, SUB), SUB), :]
            pos = [column(own, X + a) for a in range(3)]
            total = [jnp.zeros((SUB, LANES), jnp.float32) for _ in range(3)]
            for t in range(tiles):
                weight = factor[d, g, t]
                ex, ey, ez = [weight * (pos[a] - far_row(far, d, t, X + a)) for a in range(3)]
                xx, yy, zz, xy, xz, yz = [far_coef[t, n] for n in range(6)]
                total[0] += xx * ex + xy * ey + xz * ez
                total[1] += xy * ex + yy * ey + yz * ez
                total[2] += xz * ex + yz * ey + zz * ez
            for n in range(3):
                put(result, g, n * blocks + d, total[n])
            return carry

        return lax.fori_loop(0, width // SUB, group, carry)

    lax.fori_loop(0, blocks, slot, 0)
    sums = jnp.transpose(result[...])
    field = lambda n: own_rows[n * SUB : (n + 1) * SUB, 0:width]
    live, press = field(10), corr[6]
    xx, yy, zz, xy, xz, yz = [corr[n] for n in range(6)]
    sx, sy, sz = [moments[n] for n in range(3)]
    near = (xx * sx + xy * sy + xz * sz, xy * sx + yy * sy + yz * sz, xz * sx + yz * sy + zz * sz)
    outs = {}
    for a in range(3):
        far_sum = sums[a * blocks : (a + 1) * blocks, 0:width]
        accel = -SLOPE * live * (press * near[a] + far_sum)
        velocity = field(VEL + a) + STEP_DT * accel
        outs[VEL + a] = velocity
        outs[X + a] = field(X + a) + STEP_DT * velocity
    heat = moments[3] * xx + moments[4] * yy + moments[5] * zz
    heat += moments[6] * xy + moments[7] * xz + moments[8] * yz
    outs[MASS] = field(9)
    outs[SMOOTH] = field(SMOOTH)
    outs[8] = field(8) + STEP_DT * (SLOPE * live * press * heat)
    for n in range(9):
        state_out[:, n, :] = outs[n]


def exchange(own, send_rows):
    groups = lax.axis_size("seg")
    ranges = lax.axis_size("dom")
    seg = [own]
    for k in range(1, groups):
        seg.append(lax.ppermute(own, "seg", [(i, i ^ k) for i in range(groups)]))
    whole = jnp.concatenate([part[:send_rows] for part in seg], axis=0)
    first = [(i, i ^ 1) for i in range(ranges)]
    second = [(i, ((i + 1) ^ 1) - 1) for i in range(1, ranges - 1)]
    return seg + [lax.ppermute(whole, "dom", first), lax.ppermute(whole, "dom", second)]


def local(state, counts, neighbours, new_place):
    blocks, fields, width = state.shape
    nbr = neighbours.shape[1]
    groups = lax.axis_size("seg")
    slab = blocks * groups
    pairs = blocks // 2
    tiles = (nbr + 2) // 2
    main = pairs * SUB
    f32, i32 = jnp.float32, jnp.int32
    vm = pl.BlockSpec(memory_space=VMEM)
    sm = pl.BlockSpec(memory_space=SMEM)
    packed = call(
        functools.partial(pack_body, blocks, width, nbr),
        shape(main + 3 * SUB, LANES),
        in_specs=[sm, sm, vm, vm],
        out_specs=vm,
        name="pack",
    )(counts, new_place, state, neighbours)
    parts = exchange(packed, main + SUB)
    vol, rho, far, cols, own_rows, index = call(
        functools.partial(density_body, groups, blocks, width, nbr, tiles),
        (
            shape(SUB, LANES),
            shape(blocks, width),
            shape(blocks, tiles, SUB, LANES),
            shape(width, LANES),
            shape(11 * SUB, LANES),
            shape(blocks, 2 * tiles, dtype=i32),
        ),
        in_specs=[vm] * (groups + 2),
        out_specs=(vm, vm, vm, vm, vm, sm),
        scratch=(
            VMEM((3 * slab + 1, SUB, LANES), f32),
            VMEM((2 * groups, SUB, LANES), f32),
            VMEM((3 * slab, LANES), i32),
            SMEM((3 * slab, LANES), i32),
            SMEM((slab,), i32),
            VMEM((LANES, LANES), f32),
            VMEM((width, LANES), f32),
            VMEM((width, LANES), f32),
            pltpu.SemaphoreType.DMA,
        ),
        name="density",
    )(*parts)
    vols = exchange(vol, SUB)
    factor = call(
        functools.partial(factor_body, blocks, width, tiles),
        shape(blocks, width // SUB, tiles, SUB, LANES),
        in_specs=[vm, vm],
        out_specs=vm,
        scratch=(VMEM((width, LANES), f32),),
        name="factor",
    )(far, cols)
    coef, corr = call(
        functools.partial(tensor_body, groups, blocks, width, tiles),
        (shape(3 * SUB, LANES), shape(7, blocks, width)),
        in_specs=[sm] + [vm] * (5 + groups + 2),
        out_specs=(vm, vm),
        scratch=(
            VMEM((width, LANES), f32),
            VMEM((3 * slab + SUB, LANES), f32),
            VMEM((tiles, SUB, LANES), f32),
            VMEM((width, LANES), f32),
        ),
        name="tensor",
    )(index, far, cols, own_rows, factor, rho, *vols)
    coefs = exchange(coef, 3 * SUB)
    moments = call(
        functools.partial(moment_body, blocks, width, tiles),
        shape(9, blocks, width),
        in_specs=[vm] * 3,
        out_specs=vm,
        scratch=(VMEM((width, LANES), f32), VMEM((width, LANES), f32)),
        name="moments",
    )(far, cols, factor)
    moved = call(
        functools.partial(update_body, groups, blocks, width, tiles),
        shape(blocks, fields, width),
        in_specs=[sm] + [vm] * (6 + groups + 2),
        out_specs=vm,
        scratch=(
            VMEM((width, LANES), f32),
            VMEM((6, 3 * slab + SUB, LANES), f32),
            VMEM((tiles, 6, SUB, LANES), f32),
            VMEM((width, LANES), f32),
        ),
        name="update",
    )(index, far, cols, own_rows, factor, corr, moments, *coefs)
    return (moved, rho)


def solution(mesh):
    return jax.shard_map(
        local,
        mesh=mesh,
        in_specs=(
            P(("dom", "seg"), None, None),
            P(("dom", "seg")),
            P(("dom", "seg"), None),
            P(("dom", "seg")),
        ),
        out_specs=(P(("dom", "seg"), None, None), P(("dom", "seg"), None)),
        check_vma=False,
    )
```

time: 218 us -> 121 us (0.56)
  Pallas kernels: 0 us -> 79.5 us
  local copies, waits for them, and re-layouts: 60.2 us -> 7.56 us
  loops' own time: 49.9 us -> 0 us
  blocking collectives: 39.9 us -> 0 us
  other arithmetic: 38.6 us -> 0.01 us
  waiting for transfers between devices: 1.12 us -> 6.74 us
    pallas_call x0 -> x6, Pallas kernels: none -> 79.5 us  [the longest x1 18 us: local(): call(functools.partial(density_body, groups, blocks, width, nbr, tiles),...]
    another operation x3 -> x0, loops' own time: 49.9 us -> none  [the longest x1 18.2 us: local(): accel, heat = lax.map(third, block_ids)]
    all_gather x5 -> x0, blocking collectives: 32.9 us -> none  [the longest x3 20.8 us: spread(): whole = lax.all_gather(values, 'seg', axis=0, tiled=True)]
    gather x42 -> x0, local copies, waits for them, and re-layouts: 24.3 us -> none  [the longest x40 23.2 us: tile_of(): tile = jnp.take(region, index, axis=0)]
    reduce_sum x49 -> x0, other arithmetic: 18.6 us -> none  [the longest x8 6.64 us: tensor_tile(): jnp.sum(weight * diff[a] * diff[b], axis=1)]
    dynamic_slice x24 -> x0, local copies, waits for them, and re-layouts: 15.3 us -> none  [local(): rho = lax.map(first, block_ids) + (1.0 - live)]
    unnamed x1 -> x0, blocking collectives: 6.98 us -> none
    ppermute x6 -> x15, waiting for transfers between devices: 1.12 us -> 6.74 us  [the longest x9 4.69 us: exchange(): seg.append(lax.ppermute(own, 'seg', [(i, i ^ k) for i in range(groups)]))]
  transfers between devices with their start and end apart: 6 -> 15, of which waited for: 1 -> 6; matrix products, arithmetic and copies ran while one was open for 2% -> 2% of each run, Pallas kernels for 0% -> 23%
where the time goes in v1:
time: 121 us; the launch traced here: 120 us
  Pallas kernels  79.5 us (66%)
  starting transfers between devices  24.9 us (21%)
  local copies, waits for them, and re-layouts  7.56 us (6%)
  waiting for transfers between devices  6.74 us (6%)
    pallas_call x1, Pallas kernels, local(): call(functools.partial(density_body, groups, blocks, width, nbr, tiles),...  18 us
    pallas_call x1, Pallas kernels, local(): call(functools.partial(moment_body, blocks, width, tiles), shape(9, block...  17 us
    pallas_call x1, Pallas kernels, local(): call(functools.partial(update_body, groups, blocks, width, tiles), shape(...  16.4 us
    ppermute x3, starting transfers between devices, exchange(): lax.ppermute(whole, 'dom', second)  16 us
    pallas_call x1, Pallas kernels, local(): call(functools.partial(tensor_body, groups, blocks, width, tiles), (shape...  15.8 us
    pallas_call x1, Pallas kernels, local(): call(functools.partial(factor_body, blocks, width, tiles), shape(blocks,...  10.8 us
    ppermute x9, starting transfers between devices, exchange(): seg.append(lax.ppermute(own, 'seg', [(i, i ^ k) for i in range(groups)]))  8.63 us
    unnamed x38, local copies, waits for them, and re-layouts  6.77 us
  transfers between devices with their start and end apart: 15, of which 6 were waited for; matrix products, arithmetic and copies ran while one was open for 2% of the time, Pallas kernels for 23%

profile of v1, /device:TPU:1, one launch (start us, length us, event | category | flops | bytes accessed | tf_op | source)
XLA Modules:
  0.0 119.6 jit_solution(16941509251424421381)
XLA Ops:
  0.6 1.4 %copy.6.state = f32[8,9,64]{2,1,0:T(8,128)} copy(f32[8,9,64]{2,0,1:T(8,128)} %param.4) | data formatting | bytes 36864 | tf_op args[0]
  2.0 1.5 %pack.1.refs_0_ = f32[56,128]{1,0:T(8,128)} custom-call(s32[8]{0:T(128)} %counts.1, s32[8]{0:T(128)} %place.1, f32[8,9,64]{2,1,0:T(8,128)} %copy.6.state, s32[8,26]{1,0:T(8,128)} %lists.1), custom_call_target="tpu_custom_call" | custom-call | tf_op jit(solution)/shard_map/pack/pallas_call | solution.py:450
  3.6 3.0 %collective-permute-start.2 = (f32[56,128]{1,0:T(8,128)}, f32[56,128]{1,0:T(8,128)S(1)}, u32[]{:S(2)}, u32[]{:S(2)}) collective-permute-start(f32[56,128]{1,0:T(8,128)} %pack.1.refs_0_), channel_id=1, source_target_pairs={{0,3},{1,2},{2,1},{3,0},{4,7},{5,6},{6,5},{7,4},{8,11},{9,10},{10,... | collective-permute-start | bytes 86024 | tf_op jit(solution)/shard_map/ppermute | solution.py:432
  6.5 0.2 collective-permute-start.1
  6.8 0.8 slice.16
  7.6 0.4 collective-permute-done.2.refs_3_
  8.0 1.5 %collective-permute-done.1.refs_2_ = f32[56,128]{1,0:T(8,128)S(1)} collective-permute-done((f32[56,128]{1,0:T(8,128)}, f32[56,128]{1,0:T(8,128)S(1)}, u32[]{:S(2)}, u32[]{:S(2)}) %collective-permute-start.1) | collective-permute-done | bytes 28704 | tf_op jit(solution)/shard_map/ppermute | solution.py:432
  9.5 0.2 collective-permute-done.refs_1_
  9.7 5.5 %collective-permute-start.4 = (f32[160,128]{1,0:T(8,128)S(1)}, f32[160,128]{1,0:T(8,128)S(1)}, u32[]{:S(2)}, u32[]{:S(2)}) collective-permute-start(f32[160,128]{1,0:T(8,128)S(1)} %pad_maximum_fusion), channel_id=1, source_target_pairs={{4,8},{8,4},{12,16},{16,12},{20,24},{24,20},{5,9},{9,5},{13,17},{1... | collective-permute-start | bytes 245768 | tf_op jit(solution)/shard_map/ppermute | solution.py:436
  15.3 2.0 %collective-permute-done.4.refs_5_ = f32[160,128]{1,0:T(8,128)S(1)} collective-permute-done((f32[160,128]{1,0:T(8,128)S(1)}, f32[160,128]{1,0:T(8,128)S(1)}, u32[]{:S(2)}, u32[]{:S(2)}) %collective-permute-start.4) | collective-permute-done | bytes 81952 | tf_op jit(solution)/shard_map/ppermute | solution.py:436
  17.3 0.6 copy-done.3
  18.0 0.6 copy-done.4
  18.6 18.0 %density.1 = (f32[8,128]{1,0:T(8,128)}, f32[8,64]{1,0:T(8,128)}, f32[8,14,8,128]{3,2,1,0:T(8,128)}, f32[64,128]{1,0:T(8,128)}, f32[88,128]{1,0:T(8,128)}, /*index=5*/s32[8,28]{1,0:T(8,128)}) custom-call(f32[56,128]{1,0:T(8,128)} %pack.1.refs_0_, f32[56,128]{1,0:T(8,128)} %copy-done.2, f32[56,128]{1,0:T(8,128)} %copy-done.1, f32[56,128]{1,0:T(8,128)} %copy-done, ...), custom_call_target="tpu_custom_call" | custom-call | tf_op jit(solution)/shard_map/density/pallas_call | solution.py:458
  36.6 1.3 %collective-permute-start.7 = (f32[8,128]{1,0:T(8,128)}, f32[8,128]{1,0:T(8,128)S(1)}, u32[]{:S(2)}, u32[]{:S(2)}) collective-permute-start(f32[8,128]{1,0:T(8,128)} %get-tuple-element.15.refs_6_), channel_id=1, source_target_pairs={{0,3},{1,2},{2,1},{3,0},{4,7},{5,6},{6,5},{7,4},{8,11},{9,10},{10,... | collective-permute-start | bytes 12296 | tf_op jit(solution)/shard_map/ppermute | solution.py:432
  37.9 0.2 collective-permute-start.6
  38.1 1.2 %collective-permute-start.5 = (f32[8,128]{1,0:T(8,128)}, f32[8,128]{1,0:T(8,128)S(1)}, u32[]{:S(2)}, u32[]{:S(2)}) collective-permute-start(f32[8,128]{1,0:T(8,128)} %get-tuple-element.15.refs_6_), channel_id=1, source_target_pairs={{0,1},{1,0},{2,3},{3,2},{4,5},{5,4},{6,7},{7,6},{8,9},{9,8},{10,11... | collective-permute-start | bytes 12296 | tf_op jit(solution)/shard_map/ppermute | solution.py:432
  39.3 0.7 constant_dynamic-update-slice_fusion.3
  40.0 0.8 collective-permute-done.5.refs_7_
  40.9 5.3 %collective-permute-start.9 = (f32[32,128]{1,0:T(8,128)S(1)}, f32[32,128]{1,0:T(8,128)S(1)}, u32[]{:S(2)}, u32[]{:S(2)}) collective-permute-start(f32[32,128]{1,0:T(8,128)S(1)} %constant_dynamic-update-slice_fusion), channel_id=1, source_target_pairs={{4,8},{8,4},{12,16},{16,12},{20,24},{24,20},{5,9},{9,5},{13,17},{1... | collective-permute-start | bytes 49160 | tf_op jit(solution)/shard_map/ppermute | solution.py:436
  46.3 10.8 %factor.1.refs_4_ = f32[8,8,14,8,128]{4,3,2,1,0:T(8,128)} custom-call(f32[8,14,8,128]{3,2,1,0:T(8,128)} %get-tuple-element.11.far.refs_1_, f32[64,128]{1,0:T(8,128)} %get-tuple-element.12.cols.refs_2_), custom_call_target="tpu_custom_call" | custom-call | tf_op jit(solution)/shard_map/factor/pallas_call | solution.py:484
  57.1 0.5 copy-done.10
  57.7 15.8 %tensor.1 = (f32[24,128]{1,0:T(8,128)}, f32[7,8,64]{2,1,0:T(8,128)}) custom-call(s32[8,28]{1,0:T(8,128)} %get-tuple-element.10.refs_0_, f32[8,14,8,128]{3,2,1,0:T(8,128)} %get-tuple-element.11.far.refs_1_, f32[64,128]{1,0:T(8,128)} %get-tuple-element.12.cols.refs_2_, f32[88,128]{1,0:T(8,128)} %get-tuple-element.13.refs_3_, ...), custom_call_target="tpu_custom_call" | custom-call | tf_op jit(solution)/shard_map/tensor/pallas_call | solution.py:492
  73.5 2.2 %collective-permute-start.12 = (f32[24,128]{1,0:T(8,128)}, f32[24,128]{1,0:T(8,128)S(1)}, u32[]{:S(2)}, u32[]{:S(2)}) collective-permute-start(f32[24,128]{1,0:T(8,128)} %get-tuple-element.17.refs_7_), channel_id=1, source_target_pairs={{0,3},{1,2},{2,1},{3,0},{4,7},{5,6},{6,5},{7,4},{8,11},{9,10},{10,... | collective-permute-start | bytes 36872 | tf_op jit(solution)/shard_map/ppermute | solution.py:432
  75.6 0.2 collective-permute-start.11
  75.9 0.3 collective-permute-start.10
  76.1 0.7 constant_dynamic-update-slice_fusion.7
  76.8 1.8 %collective-permute-done.10.refs_8_ = f32[24,128]{1,0:T(8,128)S(1)} collective-permute-done((f32[24,128]{1,0:T(8,128)}, f32[24,128]{1,0:T(8,128)S(1)}, u32[]{:S(2)}, u32[]{:S(2)}) %collective-permute-start.10) | collective-permute-done | bytes 12320 | tf_op jit(solution)/shard_map/ppermute | solution.py:432
  78.7 5.3 %collective-permute-start.14 = (f32[96,128]{1,0:T(8,128)S(1)}, f32[96,128]{1,0:T(8,128)S(1)}, u32[]{:S(2)}, u32[]{:S(2)}) collective-permute-start(f32[96,128]{1,0:T(8,128)S(1)} %constant_dynamic-update-slice_fusion.4), channel_id=1, source_target_pairs={{4,8},{8,4},{12,16},{16,12},{20,24},{24,20},{5,9},{9,5},{13,17},{1... | collective-permute-start | bytes 147464 | tf_op jit(solution)/shard_map/ppermute | solution.py:436
  84.1 17.0 %moments.1.refs_6_ = f32[9,8,64]{2,1,0:T(8,128)} custom-call(f32[8,14,8,128]{3,2,1,0:T(8,128)} %get-tuple-element.11.far.refs_1_, f32[64,128]{1,0:T(8,128)} %get-tuple-element.12.cols.refs_2_, f32[8,8,14,8,128]{4,3,2,1,0:T(8,128)} %factor.1.refs_4_), custom_call_target="tpu_custom_call" | custom-call | tf_op jit(solution)/shard_map/moments/pallas_call | solution.py:506
  101.1 0.6 copy-done.5
  101.7 16.4 %update.1 = f32[8,9,64]{2,1,0:T(8,128)} custom-call(s32[8,28]{1,0:T(8,128)} %get-tuple-element.10.refs_0_, f32[8,14,8,128]{3,2,1,0:T(8,128)} %get-tuple-element.11.far.refs_1_, f32[64,128]{1,0:T(8,128)} %get-tuple-element.12.cols.refs_2_, f32[88,128]{1,0:T(8,128)} %get-tuple-element.13.refs_3_, f32[8,8,14,8,128]{4,3,2,1,0:T(8,128)} %factor.1.refs_4_, ...), custom_call_target="tpu_custom_call" | custom-call | tf_op jit(solution)/shard_map/update/pallas_call | solution.py:514
  118.1 1.5 %copy.7 = f32[8,9,64]{2,0,1:T(8,128)} copy(f32[8,9,64]{2,1,0:T(8,128)} %update.1) | data formatting | bytes 36864
  (49 shorter events, 0.4 us)
Async XLA Ops:
  3.6 4.5 %collective-permute-start.2 = (f32[56,128]{1,0:T(8,128)}, f32[56,128]{1,0:T(8,128)S(1)}, u32[]{:S(2)}, u32[]{:S(2)}) collective-permute-start(f32[56,128]{1,0:T(8,128)} %pack.1.refs_0_), channel_id=1, source_target_pairs={{0,3},{1,2},{2,1},{3,0},{4,7},{5,6},{6,5},{7,4},{8,11},{9,10},{10,... | collective-permute-start | bytes 86024 | tf_op jit(solution)/shard_map/ppermute | solution.py:432
  6.5 2.9 %collective-permute-start.1 = (f32[56,128]{1,0:T(8,128)}, f32[56,128]{1,0:T(8,128)S(1)}, u32[]{:S(2)}, u32[]{:S(2)}) collective-permute-start(f32[56,128]{1,0:T(8,128)} %pack.1.refs_0_), channel_id=1, source_target_pairs={{0,2},{1,3},{2,0},{3,1},{4,6},{5,7},{6,4},{7,5},{8,10},{9,11},{10,... | collective-permute-start | bytes 86024 | tf_op jit(solution)/shard_map/ppermute | solution.py:432
  6.8 2.9 %collective-permute-start = (f32[56,128]{1,0:T(8,128)}, f32[56,128]{1,0:T(8,128)S(1)}, u32[]{:S(2)}, u32[]{:S(2)}) collective-permute-start(f32[56,128]{1,0:T(8,128)} %pack.1.refs_0_), channel_id=1, source_target_pairs={{0,1},{1,0},{2,3},{3,2},{4,5},{5,4},{6,7},{7,6},{8,9},{9,8},{10,11... | collective-permute-start | bytes 86024 | tf_op jit(solution)/shard_map/ppermute | solution.py:432
  8.0 9.3 %copy-start = (f32[56,128]{1,0:T(8,128)}, f32[56,128]{1,0:T(8,128)S(1)}, u32[]{:S(2)}) copy-start(f32[56,128]{1,0:T(8,128)S(1)} %collective-permute-done.2.refs_3_) | copy-start | bytes 86020
  9.5 7.8 %copy-start.1 = (f32[56,128]{1,0:T(8,128)}, f32[56,128]{1,0:T(8,128)S(1)}, u32[]{:S(2)}) copy-start(f32[56,128]{1,0:T(8,128)S(1)} %collective-permute-done.1.refs_2_) | copy-start | bytes 86020
  9.7 7.6 %copy-start.2 = (f32[56,128]{1,0:T(8,128)}, f32[56,128]{1,0:T(8,128)S(1)}, u32[]{:S(2)}) copy-start(f32[56,128]{1,0:T(8,128)S(1)} %collective-permute-done.refs_1_) | copy-start | bytes 86020
  9.7 7.6 %collective-permute-start.4 = (f32[160,128]{1,0:T(8,128)S(1)}, f32[160,128]{1,0:T(8,128)S(1)}, u32[]{:S(2)}, u32[]{:S(2)}) collective-permute-start(f32[160,128]{1,0:T(8,128)S(1)} %pad_maximum_fusion), channel_id=1, source_target_pairs={{4,8},{8,4},{12,16},{16,12},{20,24},{24,20},{5,9},{9,5},{13,17},{1... | collective-permute-start | bytes 245768 | tf_op jit(solution)/shard_map/ppermute | solution.py:436
  15.2 2.1 %collective-permute-start.3 = (f32[160,128]{1,0:T(8,128)S(1)}, f32[160,128]{1,0:T(8,128)S(1)}, u32[]{:S(2)}, u32[]{:S(2)}) collective-permute-start(f32[160,128]{1,0:T(8,128)S(1)} %pad_maximum_fusion), channel_id=1, source_target_pairs={{0,4},{4,0},{8,12},{12,8},{16,20},{20,16},{24,28},{28,24},{1,5},{5... | collective-permute-start | bytes 245768 | tf_op jit(solution)/shard_map/ppermute | solution.py:436
  17.3 0.6 copy-start.3
  18.0 0.6 copy-start.4
  36.6 4.3 %collective-permute-start.7 = (f32[8,128]{1,0:T(8,128)}, f32[8,128]{1,0:T(8,128)S(1)}, u32[]{:S(2)}, u32[]{:S(2)}) collective-permute-start(f32[8,128]{1,0:T(8,128)} %get-tuple-element.15.refs_6_), channel_id=1, source_target_pairs={{0,3},{1,2},{2,1},{3,0},{4,7},{5,6},{6,5},{7,4},{8,11},{9,10},{10,... | collective-permute-start | bytes 12296 | tf_op jit(solution)/shard_map/ppermute | solution.py:432
  37.9 3.0 %collective-permute-start.6 = (f32[8,128]{1,0:T(8,128)}, f32[8,128]{1,0:T(8,128)S(1)}, u32[]{:S(2)}, u32[]{:S(2)}) collective-permute-start(f32[8,128]{1,0:T(8,128)} %get-tuple-element.15.refs_6_), channel_id=1, source_target_pairs={{0,2},{1,3},{2,0},{3,1},{4,6},{5,7},{6,4},{7,5},{8,10},{9,11},{10,... | collective-permute-start | bytes 12296 | tf_op jit(solution)/shard_map/ppermute | solution.py:432
  38.1 2.8 %collective-permute-start.5 = (f32[8,128]{1,0:T(8,128)}, f32[8,128]{1,0:T(8,128)S(1)}, u32[]{:S(2)}, u32[]{:S(2)}) collective-permute-start(f32[8,128]{1,0:T(8,128)} %get-tuple-element.15.refs_6_), channel_id=1, source_target_pairs={{0,1},{1,0},{2,3},{3,2},{4,5},{5,4},{6,7},{7,6},{8,9},{9,8},{10,11... | collective-permute-start | bytes 12296 | tf_op jit(solution)/shard_map/ppermute | solution.py:432
  40.9 16.2 %copy-start.14 = (f32[8,128]{1,0:T(8,128)}, f32[8,128]{1,0:T(8,128)S(1)}, u32[]{:S(2)}) copy-start(f32[8,128]{1,0:T(8,128)S(1)} %collective-permute-done.5.refs_7_) | copy-start | bytes 12292
  40.9 16.2 %copy-start.13 = (f32[8,128]{1,0:T(8,128)}, f32[8,128]{1,0:T(8,128)S(1)}, u32[]{:S(2)}) copy-start(f32[8,128]{1,0:T(8,128)S(1)} %collective-permute-done.6.refs_8_) | copy-start | bytes 12292
  40.9 16.2 %copy-start.12 = (f32[8,128]{1,0:T(8,128)}, f32[8,128]{1,0:T(8,128)S(1)}, u32[]{:S(2)}) copy-start(f32[8,128]{1,0:T(8,128)S(1)} %collective-permute-done.7.refs_9_) | copy-start | bytes 12292
  40.9 16.1 %collective-permute-start.9 = (f32[32,128]{1,0:T(8,128)S(1)}, f32[32,128]{1,0:T(8,128)S(1)}, u32[]{:S(2)}, u32[]{:S(2)}) collective-permute-start(f32[32,128]{1,0:T(8,128)S(1)} %constant_dynamic-update-slice_fusion), channel_id=1, source_target_pairs={{4,8},{8,4},{12,16},{16,12},{20,24},{24,20},{5,9},{9,5},{13,17},{1... | collective-permute-start | bytes 49160 | tf_op jit(solution)/shard_map/ppermute | solution.py:436
  46.2 10.9 %collective-permute-start.8 = (f32[32,128]{1,0:T(8,128)S(1)}, f32[32,128]{1,0:T(8,128)S(1)}, u32[]{:S(2)}, u32[]{:S(2)}) collective-permute-start(f32[32,128]{1,0:T(8,128)S(1)} %constant_dynamic-update-slice_fusion), channel_id=1, source_target_pairs={{0,4},{4,0},{8,12},{12,8},{16,20},{20,16},{24,28},{28,24},{1,5},{5... | collective-permute-start | bytes 49160 | tf_op jit(solution)/shard_map/ppermute | solution.py:436
  57.1 0.6 copy-start.10
  57.1 0.6 copy-start.11
  73.5 5.2 %collective-permute-start.12 = (f32[24,128]{1,0:T(8,128)}, f32[24,128]{1,0:T(8,128)S(1)}, u32[]{:S(2)}, u32[]{:S(2)}) collective-permute-start(f32[24,128]{1,0:T(8,128)} %get-tuple-element.17.refs_7_), channel_id=1, source_target_pairs={{0,3},{1,2},{2,1},{3,0},{4,7},{5,6},{6,5},{7,4},{8,11},{9,10},{10,... | collective-permute-start | bytes 36872 | tf_op jit(solution)/shard_map/ppermute | solution.py:432
  75.6 3.0 %collective-permute-start.11 = (f32[24,128]{1,0:T(8,128)}, f32[24,128]{1,0:T(8,128)S(1)}, u32[]{:S(2)}, u32[]{:S(2)}) collective-permute-start(f32[24,128]{1,0:T(8,128)} %get-tuple-element.17.refs_7_), channel_id=1, source_target_pairs={{0,2},{1,3},{2,0},{3,1},{4,6},{5,7},{6,4},{7,5},{8,10},{9,11},{10,... | collective-permute-start | bytes 36872 | tf_op jit(solution)/shard_map/ppermute | solution.py:432
  75.9 2.8 %collective-permute-start.10 = (f32[24,128]{1,0:T(8,128)}, f32[24,128]{1,0:T(8,128)S(1)}, u32[]{:S(2)}, u32[]{:S(2)}) collective-permute-start(f32[24,128]{1,0:T(8,128)} %get-tuple-element.17.refs_7_), channel_id=1, source_target_pairs={{0,1},{1,0},{2,3},{3,2},{4,5},{5,4},{6,7},{7,6},{8,9},{9,8},{10,11... | collective-permute-start | bytes 36872 | tf_op jit(solution)/shard_map/ppermute | solution.py:432
  78.6 22.5 %copy-start.9 = (f32[24,128]{1,0:T(8,128)}, f32[24,128]{1,0:T(8,128)S(1)}, u32[]{:S(2)}) copy-start(f32[24,128]{1,0:T(8,128)S(1)} %collective-permute-done.10.refs_8_) | copy-start | bytes 36868
  78.6 22.5 %copy-start.8 = (f32[24,128]{1,0:T(8,128)}, f32[24,128]{1,0:T(8,128)S(1)}, u32[]{:S(2)}) copy-start(f32[24,128]{1,0:T(8,128)S(1)} %collective-permute-done.11.refs_9_) | copy-start | bytes 36868
  78.7 22.4 %copy-start.7 = (f32[24,128]{1,0:T(8,128)}, f32[24,128]{1,0:T(8,128)S(1)}, u32[]{:S(2)}) copy-start(f32[24,128]{1,0:T(8,128)S(1)} %collective-permute-done.12.refs_10_) | copy-start | bytes 36868
  78.7 22.4 %collective-permute-start.14 = (f32[96,128]{1,0:T(8,128)S(1)}, f32[96,128]{1,0:T(8,128)S(1)}, u32[]{:S(2)}, u32[]{:S(2)}) collective-permute-start(f32[96,128]{1,0:T(8,128)S(1)} %constant_dynamic-update-slice_fusion.4), channel_id=1, source_target_pairs={{4,8},{8,4},{12,16},{16,12},{20,24},{24,20},{5,9},{9,5},{13,17},{1... | collective-permute-start | bytes 147464 | tf_op jit(solution)/shard_map/ppermute | solution.py:436
  84.0 17.1 %collective-permute-start.13 = (f32[96,128]{1,0:T(8,128)S(1)}, f32[96,128]{1,0:T(8,128)S(1)}, u32[]{:S(2)}, u32[]{:S(2)}) collective-permute-start(f32[96,128]{1,0:T(8,128)S(1)} %constant_dynamic-update-slice_fusion.4), channel_id=1, source_target_pairs={{0,4},{4,0},{8,12},{12,8},{16,20},{20,16},{24,28},{28,24},{1,5},{5... | collective-permute-start | bytes 147464 | tf_op jit(solution)/shard_map/ppermute | solution.py:436
  101.1 0.6 copy-start.5
  101.1 0.6 copy-start.6

commit v2 on v1

--- a/solution.py
+++ b/solution.py
@@ -13,6 +13,8 @@
 STEP_DT = 0.1
 SLOPE = -5.0 * SIGMA * 32.0
 TINY = 1e-37
+UNROLL = (8, 8, 8, 8, 8)
+GRANT = (4, 4, 4, 4, 4, 4)
 SUB = 8
 LANES = 128
 X, VEL, MASS, SMOOTH = 0, 3, 6, 7
@@ -28,14 +30,14 @@
     return lax.broadcasted_iota(jnp.int32, (rows, LANES), 0)
 
 
-def call(body, outs, scratch=(), in_specs=None, out_specs=None, name=None):
+def call(body, outs, scratch=(), in_specs=None, out_specs=None, name=None, grant=8):
     return pl.pallas_call(
         body,
         out_shape=outs,
         in_specs=in_specs,
         out_specs=out_specs,
         scratch_shapes=list(scratch),
-        compiler_params=pltpu.CompilerParams(vmem_limit_bytes=56 << 20),
+        compiler_params=pltpu.CompilerParams(vmem_limit_bytes=grant << 20),
         name=name,
     )
 
@@ -44,7 +46,7 @@
     return jax.ShapeDtypeStruct(dims, dtype)
 
 
-def pack_body(blocks, width, nbr, counts, place, state, lists, out):
+def pack_body(blocks, width, nbr, fields, counts, place, state, lists, out):
     pairs = blocks // 2
     lane = lane_iota()
     row = row_iota()
@@ -57,12 +59,14 @@
     base = pairs * SUB
     out[base : base + SUB, :] = meta
     for p in range(pairs):
-        full = jnp.concatenate([state[2 * p], state[2 * p + 1]], axis=1)
+        even, odd = [state[pl.ds(2 * p + n, SUB, stride=SUB), :] for n in (0, 1)]
+        tile = jnp.concatenate([even, odd], axis=1)
+        at = 8 * SUB + 2 * p
+        energy = jnp.concatenate([state[at : at + 1, :], state[at + 1 : at + 2, :]], axis=1)
         live = lane < jnp.where(low, counts[2 * p], counts[2 * p + 1] + width)
-        tile = full[0:SUB]
         out[p * SUB : (p + 1) * SUB, :] = jnp.where((row == MASS) & jnp.logical_not(live), 0.0, tile)
-        out[base + SUB + p : base + SUB + p + 1, :] = full[8:9]
-        out[base + SUB + pairs + p : base + SUB + pairs + p + 1, :] = full[MASS : MASS + 1]
+        out[base + SUB + p : base + SUB + p + 1, :] = energy
+        out[base + SUB + pairs + p : base + SUB + pairs + p + 1, :] = tile[MASS : MASS + 1]
         out[base + 2 * SUB + p : base + 2 * SUB + p + 1, :] = jnp.where(live, 1.0, 0.0)[0:1]
     out[base + 2 * SUB + pairs : base + 3 * SUB, :] = jnp.zeros((SUB - pairs, LANES), jnp.float32)
 
@@ -92,8 +96,26 @@
     turned[...] = pltpu.roll(cols[...], lax.rem(LANES - d * SUB, LANES), axis=1)
 
 
+def each_group(width, unroll, group):
+    count = width // SUB
+
+    def step(i, carry):
+        for n in range(unroll):
+            group(i * unroll + n)
+        return carry
+
+    if unroll == count:
+        step(0, 0)
+    else:
+        lax.fori_loop(0, count // unroll, step, 0)
+
+
+def group_rows(g):
+    return pl.ds(g * SUB if isinstance(g, int) else pl.multiple_of(g * SUB, SUB), SUB)
+
+
 def put(result, g, slot, value):
-    rows = pl.ds(pl.multiple_of(g * SUB, SUB), SUB)
+    rows = group_rows(g)
     total = jnp.sum(value, axis=1, keepdims=True)
     result[rows, :] = jnp.where(lane_iota() == slot, total, result[rows, :])
 
@@ -108,11 +130,16 @@
     return (dx, dy, dz), square * lax.rsqrt(jnp.maximum(square, TINY))
 
 
+def invert(inverse, table, slab, nbr):
+    for k in range(slab):
+        inverse[table[slab + k, nbr]] = k
+
+
 def density_body(groups, blocks, width, nbr, tiles, *refs):
     seg = refs[:groups]
     first, second = refs[groups : groups + 2]
-    (vol_out, rho_out, far, cols, own_rows, index_out) = refs[groups + 2 : groups + 8]
-    (region, aux, meta, table, inverse, own_tiles, turned, result, sem) = refs[groups + 8 :]
+    (vol_out, rho_out, far, cols, own_rows, meta) = refs[groups + 2 : groups + 8]
+    (region, aux, table, inverse, own_tiles, turned, result, sem) = refs[groups + 8 :]
     slab = groups * blocks
     pairs = blocks // 2
     main = pairs * SUB
@@ -148,11 +175,7 @@
     result[...] = jnp.zeros_like(result)
     copy.wait()
 
-    def invert(k, carry):
-        inverse[table[slab + k, nbr]] = k
-        return carry
-
-    lax.fori_loop(0, slab, invert, 0)
+    invert(inverse, table, slab, nbr)
     lane = lane_iota(1)
 
     def gather(d, carry):
@@ -185,8 +208,8 @@
     def slot(d, carry):
         own_columns(cols, turned, d)
 
-        def group(g, carry):
-            own = turned[pl.ds(pl.multiple_of(g * SUB, SUB), SUB), :]
+        def group(g):
+            own = turned[group_rows(g), :]
             pos = [column(own, X + a) for a in range(3)]
             scale = 0.5 / column(own, SMOOTH)
             total = jnp.zeros((SUB, LANES), jnp.float32)
@@ -196,44 +219,34 @@
                 shell = jnp.maximum(1.0 - ratio, 0.0)
                 shell = shell * shell
                 shell = shell * shell
-                total += shell * (far_row(far, d, t, MASS) * (1.0 + 4.0 * ratio))
+                total += shell * (far_row(far, d, t, MASS) * (0.25 + ratio))
             put(result, g, d, total)
-            return carry
-
-        return lax.fori_loop(0, width // SUB, group, carry)
+
+        each_group(width, UNROLL[0], group)
+        return carry
 
     lax.fori_loop(0, blocks, slot, 0)
     sums = jnp.transpose(result[...])[0:SUB, 0:width]
     smooth = own_rows[SMOOTH * SUB : (SMOOTH + 1) * SUB, 0:width]
     live = own_rows[10 * SUB : 11 * SUB, 0:width]
-    rho = SIGMA / (smooth * smooth * smooth) * sums + (1.0 - live)
+    rho = 4.0 * SIGMA / (smooth * smooth * smooth) * sums + (1.0 - live)
     rho_out[...] = rho
     vol = own_rows[MASS * SUB : (MASS + 1) * SUB, 0:width] / rho
     vol_out[...] = jnp.concatenate([vol, vol], axis=1)
 
-    def remap(d, carry):
-        k = inverse[me * blocks + d]
-        for n in range(2 * tiles):
-            if n == 0:
-                j = slab + k
-            elif n <= nbr:
-                j = table[slab + k, n - 1]
-            else:
-                index_out[d, n] = 3 * slab
-                continue
-            start = jnp.where(j < slab, 0, jnp.where(j < 2 * slab, slab, 2 * slab))
-            index_out[d, n] = start + table[j, nbr]
-        return carry
-
-    lax.fori_loop(0, blocks, remap, 0)
-
-
-def factor_body(blocks, width, tiles, far, cols, out, turned):
+
+def factor_body(groups, blocks, width, nbr, tiles, *refs):
+    far, cols, meta, out, index_out, turned, table, inverse, sem = refs
+    slab = groups * blocks
+    me = lax.axis_index("seg")
+    copy = pltpu.make_async_copy(meta, table, sem)
+    copy.start()
+
     def slot(d, carry):
         own_columns(cols, turned, d)
 
-        def group(g, carry):
-            own = turned[pl.ds(pl.multiple_of(g * SUB, SUB), SUB), :]
+        def group(g):
+            own = turned[group_rows(g), :]
             pos = [column(own, X + a) for a in range(3)]
             smooth = column(own, SMOOTH)
             for t in range(tiles):
@@ -242,11 +255,26 @@
                 inv2 = inv * inv
                 part = jnp.maximum(inv - dist * inv2, 0.0)
                 out[d, g, t] = part * part * part * inv2
-            return carry
-
-        return lax.fori_loop(0, width // SUB, group, carry)
+
+        each_group(width, UNROLL[1], group)
+        return carry
 
     lax.fori_loop(0, blocks, slot, 0)
+    copy.wait()
+    invert(inverse, table, slab, nbr)
+
+    def remap(d, carry):
+        k = inverse[me * blocks + d]
+        for n in range(2 * tiles):
+            if n > nbr:
+                index_out[d, n] = 3 * slab
+                continue
+            j = slab + k if n == 0 else table[slab + k, n - 1]
+            start = jnp.where(j < slab, 0, jnp.where(j < 2 * slab, slab, 2 * slab))
+            index_out[d, n] = start + table[j, nbr]
+        return carry
+
+    lax.fori_loop(0, blocks, remap, 0)
 
 
 def place_region(groups, blocks, refs, store):
@@ -286,8 +314,8 @@
             right = region[pl.ds(index[d, 2 * t + 1], 1), :]
             far_vol[t] = jnp.broadcast_to(far_pair(left, right), (SUB, LANES))
 
-        def group(g, carry):
-            own = turned[pl.ds(pl.multiple_of(g * SUB, SUB), SUB), :]
+        def group(g):
+            own = turned[group_rows(g), :]
             pos = [column(own, X + a) for a in range(3)]
             total = [jnp.zeros((SUB, LANES), jnp.float32) for _ in range(6)]
             for t in range(tiles):
@@ -298,9 +326,9 @@
                     total[n] += term
             for n in range(6):
                 put(result, g, n * blocks + d, total[n])
-            return carry
-
-        return lax.fori_loop(0, width // SUB, group, carry)
+
+        each_group(width, UNROLL[2], group)
+        return carry
 
     lax.fori_loop(0, blocks, slot, 0)
     sums = jnp.transpose(result[...])
@@ -323,8 +351,8 @@
     def slot(d, carry):
         own_columns(cols, turned, d)
 
-        def group(g, carry):
-            own = turned[pl.ds(pl.multiple_of(g * SUB, SUB), SUB), :]
+        def group(g):
+            own = turned[group_rows(g), :]
             pos = [column(own, X + a) for a in range(3)]
             vel = [column(own, VEL + a) for a in range(3)]
             total = [jnp.zeros((SUB, LANES), jnp.float32) for _ in range(9)]
@@ -347,9 +375,9 @@
                     total[n] += term
             for n in range(9):
                 put(result, g, n * blocks + d, total[n])
-            return carry
-
-        return lax.fori_loop(0, width // SUB, group, carry)
+
+        each_group(width, UNROLL[3], group)
+        return carry
 
     lax.fori_loop(0, blocks, slot, 0)
     sums = jnp.transpose(result[...])
@@ -384,8 +412,8 @@
                 value = far_pair(region[n, pl.ds(one, 1), :], region[n, pl.ds(two, 1), :])
                 far_coef[t, n] = jnp.broadcast_to(value, (SUB, LANES))
 
-        def group(g, carry):
-            own = turned[pl.ds(pl.multiple_of(g * SUB, SUB), SUB), :]
+        def group(g):
+            own = turned[group_rows(g), :]
             pos = [column(own, X + a) for a in range(3)]
             total = [jnp.zeros((SUB, LANES), jnp.float32) for _ in range(3)]
             for t in range(tiles):
@@ -397,9 +425,9 @@
                 total[2] += xz * ex + yz * ey + zz * ez
             for n in range(3):
                 put(result, g, n * blocks + d, total[n])
-            return carry
-
-        return lax.fori_loop(0, width // SUB, group, carry)
+
+        each_group(width, UNROLL[4], group)
+        return carry
 
     lax.fori_loop(0, blocks, slot, 0)
     sums = jnp.transpose(result[...])
@@ -421,7 +449,7 @@
     outs[SMOOTH] = field(SMOOTH)
     outs[8] = field(8) + STEP_DT * (SLOPE * live * press * heat)
     for n in range(9):
-        state_out[:, n, :] = outs[n]
+        state_out[n] = outs[n]
 
 
 def exchange(own, send_rows):
@@ -448,14 +476,14 @@
     vm = pl.BlockSpec(memory_space=VMEM)
     sm = pl.BlockSpec(memory_space=SMEM)
     packed = call(
-        functools.partial(pack_body, blocks, width, nbr),
+        functools.partial(pack_body, blocks, width, nbr, fields),
         shape(main + 3 * SUB, LANES),
         in_specs=[sm, sm, vm, vm],
         out_specs=vm,
         name="pack",
-    )(counts, new_place, state, neighbours)
+    )(counts, new_place, jnp.swapaxes(state, 0, 1).reshape(fields * blocks, width), neighbours)
     parts = exchange(packed, main + SUB)
-    vol, rho, far, cols, own_rows, index = call(
+    vol, rho, far, cols, own_rows, meta = call(
         functools.partial(density_body, groups, blocks, width, nbr, tiles),
         (
             shape(SUB, LANES),
@@ -463,14 +491,13 @@
             shape(blocks, tiles, SUB, LANES),
             shape(width, LANES),
             shape(11 * SUB, LANES),
-            shape(blocks, 2 * tiles, dtype=i32),
+            shape(3 * slab, LANES, dtype=i32),
         ),
         in_specs=[vm] * (groups + 2),
-        out_specs=(vm, vm, vm, vm, vm, sm),
+        out_specs=(vm,) * 6,
         scratch=(
             VMEM((3 * slab + 1, SUB, LANES), f32),
             VMEM((2 * groups, SUB, LANES), f32),
-            VMEM((3 * slab, LANES), i32),
             SMEM((3 * slab, LANES), i32),
             SMEM((slab,), i32),
             VMEM((LANES, LANES), f32),
@@ -481,14 +508,19 @@
         name="density",
     )(*parts)
     vols = exchange(vol, SUB)
-    factor = call(
-        functools.partial(factor_body, blocks, width, tiles),
-        shape(blocks, width // SUB, tiles, SUB, LANES),
-        in_specs=[vm, vm],
-        out_specs=vm,
-        scratch=(VMEM((width, LANES), f32),),
+    factor, index = call(
+        functools.partial(factor_body, groups, blocks, width, nbr, tiles),
+        (shape(blocks, width // SUB, tiles, SUB, LANES), shape(blocks, 2 * tiles, dtype=i32)),
+        in_specs=[vm, vm, vm],
+        out_specs=(vm, sm),
+        scratch=(
+            VMEM((width, LANES), f32),
+            SMEM((3 * slab, LANES), i32),
+            SMEM((slab,), i32),
+            pltpu.SemaphoreType.DMA,
+        ),
         name="factor",
-    )(far, cols)
+    )(far, cols, meta)
     coef, corr = call(
         functools.partial(tensor_body, groups, blocks, width, tiles),
         (shape(3 * SUB, LANES), shape(7, blocks, width)),
@@ -513,7 +545,7 @@
     )(far, cols, factor)
     moved = call(
         functools.partial(update_body, groups, blocks, width, tiles),
-        shape(blocks, fields, width),
+        shape(fields, blocks, width),
         in_specs=[sm] + [vm] * (6 + groups + 2),
         out_specs=vm,
         scratch=(
@@ -524,7 +556,7 @@
         ),
         name="update",
     )(index, far, cols, own_rows, factor, corr, moments, *coefs)
-    return (moved, rho)
+    return (jnp.swapaxes(moved, 0, 1), rho)
 
 
 def solution(mesh):

time: 121 us -> 69.2 us (0.57)
  Pallas kernels: 79.5 us -> 31.2 us
  local copies, waits for them, and re-layouts: 7.56 us -> 3.46 us
  waiting for transfers between devices: 6.74 us -> 10.5 us
  starting transfers between devices: 24.9 us -> 23 us
    pallas_call x1, Pallas kernels: 18 us -> 7.03 us  [local(): call(functools.partial(density_body, groups, blocks, width, nbr, tiles),...]
    pallas_call x1, Pallas kernels: 15.8 us -> 5.4 us  [local(): call(functools.partial(tensor_body, groups, blocks, width, tiles), (shape...]
    pallas_call x1, Pallas kernels: 17 us -> 6.72 us  [local(): call(functools.partial(moment_body, blocks, width, tiles), shape(9, block...]
    pallas_call x1, Pallas kernels: 16.4 us -> 6.27 us  [local(): call(functools.partial(update_body, groups, blocks, width, tiles), shape(...]
    pallas_call x2, Pallas kernels: 12.3 us -> 5.76 us  [the longest x1 5.14 us: local(): call(functools.partial(factor_body, groups, blocks, width, nbr, tiles), (...]
    ppermute x3, starting transfers between devices: 16 us -> 11.8 us  [exchange(): lax.ppermute(whole, 'dom', second)]
    unnamed x38 -> x16, local copies, waits for them, and re-layouts: 6.77 us -> 3.45 us
    ppermute x9, waiting for transfers between devices: 4.69 us -> 7.84 us  [exchange(): seg.append(lax.ppermute(own, 'seg', [(i, i ^ k) for i in range(groups)]))]
  transfers between devices with their start and end apart: 15 -> 15, of which waited for: 6 -> 7; matrix products, arithmetic and copies ran while one was open for 2% -> 0% of each run, Pallas kernels for 23% -> 17%
where the time goes in v2:
time: 69.2 us; the launch traced here: 68.9 us
  Pallas kernels  31.2 us (45%)
  starting transfers between devices  23 us (33%)
  waiting for transfers between devices  10.5 us (15%)
  local copies, waits for them, and re-layouts  3.46 us (5%)
  between operations  0.76 us (1%)
    ppermute x3, starting transfers between devices, exchange(): lax.ppermute(whole, 'dom', second)  11.8 us
    ppermute x9, starting transfers between devices, exchange(): seg.append(lax.ppermute(own, 'seg', [(i, i ^ k) for i in range(groups)]))  8.7 us
    ppermute x9, waiting for transfers between devices, exchange(): seg.append(lax.ppermute(own, 'seg', [(i, i ^ k) for i in range(groups)]))  7.84 us
    pallas_call x1, Pallas kernels, local(): call(functools.partial(density_body, groups, blocks, width, nbr, tiles),...  7.03 us
    pallas_call x1, Pallas kernels, local(): call(functools.partial(moment_body, blocks, width, tiles), shape(9, block...  6.72 us
    pallas_call x1, Pallas kernels, local(): call(functools.partial(update_body, groups, blocks, width, tiles), shape(...  6.27 us
    pallas_call x1, Pallas kernels, local(): call(functools.partial(tensor_body, groups, blocks, width, tiles), (shape...  5.4 us
    pallas_call x1, Pallas kernels, local(): call(functools.partial(factor_body, groups, blocks, width, nbr, tiles), (...  5.14 us
  transfers between devices with their start and end apart: 15, of which 7 were waited for; matrix products, arithmetic and copies ran while one was open for 0% of the time, Pallas kernels for 17%

profile of v2, /device:TPU:1, one launch (start us, length us, event | category | flops | bytes accessed | tf_op | source)
XLA Modules:
  0.0 68.9 jit_solution(6406471369422735348)
XLA Ops:
  0.6 0.8 %copy-done = f32[8,9,64]{2,0,1:T(8,128)S(1)} copy-done((f32[8,9,64]{2,0,1:T(8,128)S(1)}, f32[8,9,64]{2,0,1:T(8,128)}, u32[]{:S(2)}) %copy-start) | copy-done | bytes 18456
  1.4 0.7 copy-done.2
  2.1 0.7 copy-done.3
  2.7 0.7 copy-done.4
  3.4 0.6 pack.1.refs_0_
  4.0 2.1 %collective-permute-start = (f32[56,128]{1,0:T(8,128)S(1)}, f32[56,128]{1,0:T(8,128)S(1)}, u32[]{:S(2)}, u32[]{:S(2)}) collective-permute-start(f32[56,128]{1,0:T(8,128)S(1)} %pack.1.refs_0_), channel_id=1, source_target_pairs={{0,1},{1,0},{2,3},{3,2},{4,5},{5,4},{6,7},{7,6},{8,9},{9,8},{10,11... | collective-permute-start | bytes 86024 | tf_op jit(solution)/shard_map/ppermute | solution.py:460
  6.1 1.2 %collective-permute-start.1 = (f32[56,128]{1,0:T(8,128)S(1)}, f32[56,128]{1,0:T(8,128)S(1)}, u32[]{:S(2)}, u32[]{:S(2)}) collective-permute-start(f32[56,128]{1,0:T(8,128)S(1)} %pack.1.refs_0_), channel_id=1, source_target_pairs={{0,2},{1,3},{2,0},{3,1},{4,6},{5,7},{6,4},{7,5},{8,10},{9,11},{10,... | collective-permute-start | bytes 86024 | tf_op jit(solution)/shard_map/ppermute | solution.py:460
  7.3 0.0 collective-permute-start.2
  7.4 1.4 %collective-permute-done.1.refs_2_ = f32[56,128]{1,0:T(8,128)S(1)} collective-permute-done((f32[56,128]{1,0:T(8,128)S(1)}, f32[56,128]{1,0:T(8,128)S(1)}, u32[]{:S(2)}, u32[]{:S(2)}) %collective-permute-start.1) | collective-permute-done | bytes 28704 | tf_op jit(solution)/shard_map/ppermute | solution.py:460
  8.8 2.1 %collective-permute-done.2.refs_3_ = f32[56,128]{1,0:T(8,128)S(1)} collective-permute-done((f32[56,128]{1,0:T(8,128)S(1)}, f32[56,128]{1,0:T(8,128)S(1)}, u32[]{:S(2)}, u32[]{:S(2)}) %collective-permute-start.2) | collective-permute-done | bytes 28704 | tf_op jit(solution)/shard_map/ppermute | solution.py:460
  11.0 2.5 %collective-permute-start.3 = (f32[160,128]{1,0:T(8,128)S(1)}, f32[160,128]{1,0:T(8,128)S(1)}, u32[]{:S(2)}, u32[]{:S(2)}) collective-permute-start(f32[160,128]{1,0:T(8,128)S(1)} %pad_maximum_fusion), channel_id=1, source_target_pairs={{0,4},{4,0},{8,12},{12,8},{16,20},{20,16},{24,28},{28,24},{1,5},{5... | collective-permute-start | bytes 245768 | tf_op jit(solution)/shard_map/ppermute | solution.py:464
  13.4 3.1 %collective-permute-start.4 = (f32[160,128]{1,0:T(8,128)S(1)}, f32[160,128]{1,0:T(8,128)S(1)}, u32[]{:S(2)}, u32[]{:S(2)}) collective-permute-start(f32[160,128]{1,0:T(8,128)S(1)} %pad_maximum_fusion), channel_id=1, source_target_pairs={{4,8},{8,4},{12,16},{16,12},{20,24},{24,20},{5,9},{9,5},{13,17},{1... | collective-permute-start | bytes 245768 | tf_op jit(solution)/shard_map/ppermute | solution.py:464
  16.5 2.6 %collective-permute-done.4.refs_5_ = f32[160,128]{1,0:T(8,128)S(1)} collective-permute-done((f32[160,128]{1,0:T(8,128)S(1)}, f32[160,128]{1,0:T(8,128)S(1)}, u32[]{:S(2)}, u32[]{:S(2)}) %collective-permute-start.4) | collective-permute-done | bytes 81952 | tf_op jit(solution)/shard_map/ppermute | solution.py:464
  19.2 7.0 %density.1 = (f32[8,128]{1,0:T(8,128)S(1)}, f32[8,64]{1,0:T(8,128)}, f32[8,14,8,128]{3,2,1,0:T(8,128)S(1)}, f32[64,128]{1,0:T(8,128)S(1)}, f32[88,128]{1,0:T(8,128)S(1)}, /*index=5*/s32[96,128]{1,0:T(8,128)S(1)}) custom-call(f32[56,128]{1,0:T(8,128)S(1)} %pack.1.refs_0_, f32[56,128]{1,0:T(8,128)S(1)} %collective-permute-done.refs_1_, ...), custom_call_target="tpu_custom_call" | custom-call | tf_op jit(solution)/shard_map/density/pallas_call | solution.py:486
  26.2 0.3 collective-permute-start.5
  26.5 0.1 collective-permute-start.6
  26.6 2.3 %collective-permute-start.7 = (f32[8,128]{1,0:T(8,128)S(1)}, f32[8,128]{1,0:T(8,128)S(1)}, u32[]{:S(2)}, u32[]{:S(2)}) collective-permute-start(f32[8,128]{1,0:T(8,128)S(1)} %get-tuple-element.19.refs_6_), channel_id=1, source_target_pairs={{0,3},{1,2},{2,1},{3,0},{4,7},{5,6},{6,5},{7,4},{8,11},{9,10},{10,... | collective-permute-start | bytes 12296 | tf_op jit(solution)/shard_map/ppermute | solution.py:460
  28.9 0.1 collective-permute-done.6.refs_8_
  29.0 1.0 %collective-permute-done.7.refs_9_ = f32[8,128]{1,0:T(8,128)S(1)} collective-permute-done((f32[8,128]{1,0:T(8,128)S(1)}, f32[8,128]{1,0:T(8,128)S(1)}, u32[]{:S(2)}, u32[]{:S(2)}) %collective-permute-start.7) | collective-permute-done | bytes 4128 | tf_op jit(solution)/shard_map/ppermute | solution.py:460
  29.9 5.0 %collective-permute-start.9 = (f32[32,128]{1,0:T(8,128)S(1)}, f32[32,128]{1,0:T(8,128)S(1)}, u32[]{:S(2)}, u32[]{:S(2)}) collective-permute-start(f32[32,128]{1,0:T(8,128)S(1)} %constant_dynamic-update-slice_fusion), channel_id=1, source_target_pairs={{4,8},{8,4},{12,16},{16,12},{20,24},{24,20},{5,9},{9,5},{13,17},{1... | collective-permute-start | bytes 49160 | tf_op jit(solution)/shard_map/ppermute | solution.py:464
  34.9 5.1 %factor.1 = (f32[8,8,14,8,128]{4,3,2,1,0:T(8,128)S(1)}, s32[8,28]{1,0:T(8,128)S(1)}) custom-call(f32[8,14,8,128]{3,2,1,0:T(8,128)S(1)} %get-tuple-element.12.refs_0_.refs_1_.far, f32[64,128]{1,0:T(8,128)S(1)} %get-tuple-element.13.refs_1_.refs_2_.cols, s32[96,128]{1,0:T(8,128)S(1)} %get-tuple-element.14.refs_2_), custom_call_target="tpu_custom_call" | custom-call | tf_op jit(solution)/shard_map/factor/pallas_call | solution.py:511
  40.1 0.0 copy-start.1
  40.1 0.7 copy-done.1
  40.8 5.4 %tensor.1 = (f32[24,128]{1,0:T(8,128)S(1)}, f32[7,8,64]{2,1,0:T(8,128)S(1)}) custom-call(s32[8,28]{1,0:T(8,128)S(1)} %get-tuple-element.15.refs_0_, f32[8,14,8,128]{3,2,1,0:T(8,128)S(1)} %get-tuple-element.12.refs_0_.refs_1_.far, f32[64,128]{1,0:T(8,128)S(1)} %get-tuple-element.13.refs_1_.refs_2_.cols, f32[88,128]{1,0:T(8,128)S(1)} %get-tuple-element.16.refs_3_, ...), custom_call_target="tpu_custom_call" | custom-call | tf_op jit(solution)/shard_map/tensor/pallas_call | solution.py:524
  46.2 1.2 %collective-permute-start.10 = (f32[24,128]{1,0:T(8,128)S(1)}, f32[24,128]{1,0:T(8,128)S(1)}, u32[]{:S(2)}, u32[]{:S(2)}) collective-permute-start(f32[24,128]{1,0:T(8,128)S(1)} %get-tuple-element.21.refs_7_), channel_id=1, source_target_pairs={{0,1},{1,0},{2,3},{3,2},{4,5},{5,4},{6,7},{7,6},{8,9},{9,8},{10,11... | collective-permute-start | bytes 36872 | tf_op jit(solution)/shard_map/ppermute | solution.py:460
  47.4 1.2 %collective-permute-start.11 = (f32[24,128]{1,0:T(8,128)S(1)}, f32[24,128]{1,0:T(8,128)S(1)}, u32[]{:S(2)}, u32[]{:S(2)}) collective-permute-start(f32[24,128]{1,0:T(8,128)S(1)} %get-tuple-element.21.refs_7_), channel_id=1, source_target_pairs={{0,2},{1,3},{2,0},{3,1},{4,6},{5,7},{6,4},{7,5},{8,10},{9,11},{10,... | collective-permute-start | bytes 36872 | tf_op jit(solution)/shard_map/ppermute | solution.py:460
  48.7 0.2 collective-permute-start.12
  48.9 1.1 %collective-permute-done.11.refs_9_ = f32[24,128]{1,0:T(8,128)S(1)} collective-permute-done((f32[24,128]{1,0:T(8,128)S(1)}, f32[24,128]{1,0:T(8,128)S(1)}, u32[]{:S(2)}, u32[]{:S(2)}) %collective-permute-start.11) | collective-permute-done | bytes 12320 | tf_op jit(solution)/shard_map/ppermute | solution.py:460
  50.0 2.1 %collective-permute-done.12.refs_10_ = f32[24,128]{1,0:T(8,128)S(1)} collective-permute-done((f32[24,128]{1,0:T(8,128)S(1)}, f32[24,128]{1,0:T(8,128)S(1)}, u32[]{:S(2)}, u32[]{:S(2)}) %collective-permute-start.12) | collective-permute-done | bytes 12320 | tf_op jit(solution)/shard_map/ppermute | solution.py:460
  52.1 3.7 %collective-permute-start.14 = (f32[96,128]{1,0:T(8,128)S(1)}, f32[96,128]{1,0:T(8,128)S(1)}, u32[]{:S(2)}, u32[]{:S(2)}) collective-permute-start(f32[96,128]{1,0:T(8,128)S(1)} %constant_dynamic-update-slice_fusion.4), channel_id=1, source_target_pairs={{4,8},{8,4},{12,16},{16,12},{20,24},{24,20},{5,9},{9,5},{13,17},{1... | collective-permute-start | bytes 147464 | tf_op jit(solution)/shard_map/ppermute | solution.py:464
  55.9 6.7 %moments.1.refs_6_ = f32[9,8,64]{2,1,0:T(8,128)S(1)} custom-call(f32[8,14,8,128]{3,2,1,0:T(8,128)S(1)} %get-tuple-element.12.refs_0_.refs_1_.far, f32[64,128]{1,0:T(8,128)S(1)} %get-tuple-element.13.refs_1_.refs_2_.cols, f32[8,8,14,8,128]{4,3,2,1,0:T(8,128)S(1)} %get-tuple-element.17.refs_4_.factor), custom_call_target="tpu_custom_call" | custom-call | tf_op jit(solution)/shard_map/moments/pallas_call | solution.py:538
  62.6 6.3 %update.1 = f32[9,8,64]{2,1,0:T(8,128)} custom-call(s32[8,28]{1,0:T(8,128)S(1)} %get-tuple-element.15.refs_0_, f32[8,14,8,128]{3,2,1,0:T(8,128)S(1)} %get-tuple-element.12.refs_0_.refs_1_.far, f32[64,128]{1,0:T(8,128)S(1)} %get-tuple-element.13.refs_1_.refs_2_.cols, f32[88,128]{1,0:T(8,128)S(1)} %get-tuple-element.16.refs_3_, ...), custom_call_target="tpu_custom_call" | custom-call | tf_op jit(solution)/shard_map/update/pallas_call | solution.py:546
  (27 shorter events, 0.1 us)
Async XLA Ops:
  0.6 0.8 %copy-start = (f32[8,9,64]{2,0,1:T(8,128)S(1)}, f32[8,9,64]{2,0,1:T(8,128)}, u32[]{:S(2)}) copy-start(f32[8,9,64]{2,0,1:T(8,128)} %param.4) | copy-start | bytes 55300
  1.4 0.7 copy-start.2
  2.1 0.7 copy-start.3
  2.7 0.7 copy-start.4
  4.0 3.3 %collective-permute-start = (f32[56,128]{1,0:T(8,128)S(1)}, f32[56,128]{1,0:T(8,128)S(1)}, u32[]{:S(2)}, u32[]{:S(2)}) collective-permute-start(f32[56,128]{1,0:T(8,128)S(1)} %pack.1.refs_0_), channel_id=1, source_target_pairs={{0,1},{1,0},{2,3},{3,2},{4,5},{5,4},{6,7},{7,6},{8,9},{9,8},{10,11... | collective-permute-start | bytes 86024 | tf_op jit(solution)/shard_map/ppermute | solution.py:460
  6.1 2.7 %collective-permute-start.1 = (f32[56,128]{1,0:T(8,128)S(1)}, f32[56,128]{1,0:T(8,128)S(1)}, u32[]{:S(2)}, u32[]{:S(2)}) collective-permute-start(f32[56,128]{1,0:T(8,128)S(1)} %pack.1.refs_0_), channel_id=1, source_target_pairs={{0,2},{1,3},{2,0},{3,1},{4,6},{5,7},{6,4},{7,5},{8,10},{9,11},{10,... | collective-permute-start | bytes 86024 | tf_op jit(solution)/shard_map/ppermute | solution.py:460
  7.3 3.6 %collective-permute-start.2 = (f32[56,128]{1,0:T(8,128)S(1)}, f32[56,128]{1,0:T(8,128)S(1)}, u32[]{:S(2)}, u32[]{:S(2)}) collective-permute-start(f32[56,128]{1,0:T(8,128)S(1)} %pack.1.refs_0_), channel_id=1, source_target_pairs={{0,3},{1,2},{2,1},{3,0},{4,7},{5,6},{6,5},{7,4},{8,11},{9,10},{10,... | collective-permute-start | bytes 86024 | tf_op jit(solution)/shard_map/ppermute | solution.py:460
  11.0 5.6 %collective-permute-start.3 = (f32[160,128]{1,0:T(8,128)S(1)}, f32[160,128]{1,0:T(8,128)S(1)}, u32[]{:S(2)}, u32[]{:S(2)}) collective-permute-start(f32[160,128]{1,0:T(8,128)S(1)} %pad_maximum_fusion), channel_id=1, source_target_pairs={{0,4},{4,0},{8,12},{12,8},{16,20},{20,16},{24,28},{28,24},{1,5},{5... | collective-permute-start | bytes 245768 | tf_op jit(solution)/shard_map/ppermute | solution.py:464
  13.4 5.7 %collective-permute-start.4 = (f32[160,128]{1,0:T(8,128)S(1)}, f32[160,128]{1,0:T(8,128)S(1)}, u32[]{:S(2)}, u32[]{:S(2)}) collective-permute-start(f32[160,128]{1,0:T(8,128)S(1)} %pad_maximum_fusion), channel_id=1, source_target_pairs={{4,8},{8,4},{12,16},{16,12},{20,24},{24,20},{5,9},{9,5},{13,17},{1... | collective-permute-start | bytes 245768 | tf_op jit(solution)/shard_map/ppermute | solution.py:464
  26.2 2.7 %collective-permute-start.5 = (f32[8,128]{1,0:T(8,128)S(1)}, f32[8,128]{1,0:T(8,128)S(1)}, u32[]{:S(2)}, u32[]{:S(2)}) collective-permute-start(f32[8,128]{1,0:T(8,128)S(1)} %get-tuple-element.19.refs_6_), channel_id=1, source_target_pairs={{0,1},{1,0},{2,3},{3,2},{4,5},{5,4},{6,7},{7,6},{8,9},{9,8},{10,11... | collective-permute-start | bytes 12296 | tf_op jit(solution)/shard_map/ppermute | solution.py:460
  26.5 2.5 %collective-permute-start.6 = (f32[8,128]{1,0:T(8,128)S(1)}, f32[8,128]{1,0:T(8,128)S(1)}, u32[]{:S(2)}, u32[]{:S(2)}) collective-permute-start(f32[8,128]{1,0:T(8,128)S(1)} %get-tuple-element.19.refs_6_), channel_id=1, source_target_pairs={{0,2},{1,3},{2,0},{3,1},{4,6},{5,7},{6,4},{7,5},{8,10},{9,11},{10,... | collective-permute-start | bytes 12296 | tf_op jit(solution)/shard_map/ppermute | solution.py:460
  26.6 3.4 %collective-permute-start.7 = (f32[8,128]{1,0:T(8,128)S(1)}, f32[8,128]{1,0:T(8,128)S(1)}, u32[]{:S(2)}, u32[]{:S(2)}) collective-permute-start(f32[8,128]{1,0:T(8,128)S(1)} %get-tuple-element.19.refs_6_), channel_id=1, source_target_pairs={{0,3},{1,2},{2,1},{3,0},{4,7},{5,6},{6,5},{7,4},{8,11},{9,10},{10,... | collective-permute-start | bytes 12296 | tf_op jit(solution)/shard_map/ppermute | solution.py:460
  29.9 10.1 %collective-permute-start.8 = (f32[32,128]{1,0:T(8,128)S(1)}, f32[32,128]{1,0:T(8,128)S(1)}, u32[]{:S(2)}, u32[]{:S(2)}) collective-permute-start(f32[32,128]{1,0:T(8,128)S(1)} %constant_dynamic-update-slice_fusion), channel_id=1, source_target_pairs={{0,4},{4,0},{8,12},{12,8},{16,20},{20,16},{24,28},{28,24},{1,5},{5... | collective-permute-start | bytes 49160 | tf_op jit(solution)/shard_map/ppermute | solution.py:464
  29.9 10.2 %collective-permute-start.9 = (f32[32,128]{1,0:T(8,128)S(1)}, f32[32,128]{1,0:T(8,128)S(1)}, u32[]{:S(2)}, u32[]{:S(2)}) collective-permute-start(f32[32,128]{1,0:T(8,128)S(1)} %constant_dynamic-update-slice_fusion), channel_id=1, source_target_pairs={{4,8},{8,4},{12,16},{16,12},{20,24},{24,20},{5,9},{9,5},{13,17},{1... | collective-permute-start | bytes 49160 | tf_op jit(solution)/shard_map/ppermute | solution.py:464
  40.1 0.7 %copy-start.1 = (f32[8,64]{1,0:T(8,128)S(1)}, f32[8,64]{1,0:T(8,128)}, u32[]{:S(2)}) copy-start(f32[8,64]{1,0:T(8,128)} %get-tuple-element.11.refs_5_) | copy-start | bytes 6148
  46.2 2.7 %collective-permute-start.10 = (f32[24,128]{1,0:T(8,128)S(1)}, f32[24,128]{1,0:T(8,128)S(1)}, u32[]{:S(2)}, u32[]{:S(2)}) collective-permute-start(f32[24,128]{1,0:T(8,128)S(1)} %get-tuple-element.21.refs_7_), channel_id=1, source_target_pairs={{0,1},{1,0},{2,3},{3,2},{4,5},{5,4},{6,7},{7,6},{8,9},{9,8},{10,11... | collective-permute-start | bytes 36872 | tf_op jit(solution)/shard_map/ppermute | solution.py:460
  47.4 2.5 %collective-permute-start.11 = (f32[24,128]{1,0:T(8,128)S(1)}, f32[24,128]{1,0:T(8,128)S(1)}, u32[]{:S(2)}, u32[]{:S(2)}) collective-permute-start(f32[24,128]{1,0:T(8,128)S(1)} %get-tuple-element.21.refs_7_), channel_id=1, source_target_pairs={{0,2},{1,3},{2,0},{3,1},{4,6},{5,7},{6,4},{7,5},{8,10},{9,11},{10,... | collective-permute-start | bytes 36872 | tf_op jit(solution)/shard_map/ppermute | solution.py:460
  48.7 3.4 %collective-permute-start.12 = (f32[24,128]{1,0:T(8,128)S(1)}, f32[24,128]{1,0:T(8,128)S(1)}, u32[]{:S(2)}, u32[]{:S(2)}) collective-permute-start(f32[24,128]{1,0:T(8,128)S(1)} %get-tuple-element.21.refs_7_), channel_id=1, source_target_pairs={{0,3},{1,2},{2,1},{3,0},{4,7},{5,6},{6,5},{7,4},{8,11},{9,10},{10,... | collective-permute-start | bytes 36872 | tf_op jit(solution)/shard_map/ppermute | solution.py:460
  52.1 10.5 %collective-permute-start.13 = (f32[96,128]{1,0:T(8,128)S(1)}, f32[96,128]{1,0:T(8,128)S(1)}, u32[]{:S(2)}, u32[]{:S(2)}) collective-permute-start(f32[96,128]{1,0:T(8,128)S(1)} %constant_dynamic-update-slice_fusion.4), channel_id=1, source_target_pairs={{0,4},{4,0},{8,12},{12,8},{16,20},{20,16},{24,28},{28,24},{1,5},{5... | collective-permute-start | bytes 147464 | tf_op jit(solution)/shard_map/ppermute | solution.py:464
  52.1 10.5 %collective-permute-start.14 = (f32[96,128]{1,0:T(8,128)S(1)}, f32[96,128]{1,0:T(8,128)S(1)}, u32[]{:S(2)}, u32[]{:S(2)}) collective-permute-start(f32[96,128]{1,0:T(8,128)S(1)} %constant_dynamic-update-slice_fusion.4), channel_id=1, source_target_pairs={{4,8},{8,4},{12,16},{16,12},{20,24},{24,20},{5,9},{9,5},{13,17},{1... | collective-permute-start | bytes 147464 | tf_op jit(solution)/shard_map/ppermute | solution.py:464

commit v3 on v0

v3 whole, which is shorter than its diff:
```python
import functools
import math

import jax
import jax.numpy as jnp
from jax import lax
from jax.experimental import pallas as pl
from jax.experimental.pallas import tpu as pltpu
from jax.sharding import PartitionSpec as P

SIGMA = 21.0 / (16.0 * math.pi)
GAMMA_LESS = 2.0 / 3.0
STEP_DT = 0.1
SLOPE = -5.0 * SIGMA * 32.0
TINY = 1e-37
SUB = 8
LANES = 128
X, SMOOTH, MASS, VEL = 0, 3, 4, 5
HALF = LANES // 2
VMEM = pltpu.VMEM
SMEM = pltpu.SMEM


def lane_iota(rows=SUB):
    return lax.broadcasted_iota(jnp.int32, (rows, LANES), 1)


def row_iota(rows=SUB):
    return lax.broadcasted_iota(jnp.int32, (rows, LANES), 0)


def call(body, outs, scratch=(), in_specs=None, out_specs=None, name=None, grant=8):
    return pl.pallas_call(
        body,
        out_shape=outs,
        in_specs=in_specs,
        out_specs=out_specs,
        scratch_shapes=list(scratch),
        compiler_params=pltpu.CompilerParams(vmem_limit_bytes=grant << 20),
        name=name,
    )


def shape(*dims, dtype=jnp.float32):
    return jax.ShapeDtypeStruct(dims, dtype)


def pack_body(blocks, width, nbr, tiles, *refs):
    counts, place, state, lists, out, held, entries, few, ids, sem = refs
    copies = [
        pltpu.make_async_copy(source, target, sem.at[n])
        for n, (source, target) in enumerate(
            ((state, held), (lists, entries), (counts, few), (place, ids))
        )
    ]
    for copy in copies:
        copy.start()
    for copy in copies:
        copy.wait()
    groups = lax.axis_size("seg")
    me = lax.axis_index("seg")
    lane, row = lane_iota(), row_iota()
    count = jnp.zeros((SUB, LANES), jnp.int32)
    spot = jnp.zeros((SUB, LANES), jnp.int32)
    for b in range(blocks):
        count = jnp.where(row == b, few[b], count)
        spot = jnp.where(row == b, ids[b], spot)
    listed = jnp.concatenate(
        [entries[...], jnp.zeros((blocks, LANES - nbr), jnp.int32)], axis=1
    ).astype(jnp.float32)
    listed = pltpu.roll(listed, 1, axis=1)
    own = (groups * blocks + me * blocks + row).astype(jnp.float32)
    meta = jnp.where(lane == 0, own, jnp.where(lane <= nbr, listed, -1.0))
    meta = jnp.where(lane == 2 * tiles, spot.astype(jnp.float32), meta)
    meta = jnp.where(lane == 2 * tiles + 1, count.astype(jnp.float32), meta)
    rows = [held[n] for n in range(9)]
    mass = jnp.where(lane[:, 0:width] < count[:, 0:width], rows[6], 0.0)
    order = (rows[0], rows[1], rows[2], rows[7], mass, rows[3], rows[4], rows[5])
    for n in range(4):
        out[n * SUB : (n + 1) * SUB, :] = jnp.concatenate(order[2 * n : 2 * n + 2], axis=1)
    out[4 * SUB : 5 * SUB, :] = meta
    out[5 * SUB : 6 * SUB, :] = jnp.concatenate([rows[8], rows[6]], axis=1)


def place_region(groups, blocks, refs, rows, store):
    slab = groups * blocks
    me = lax.axis_index("seg")
    odd = lax.rem(lax.axis_index("dom"), 2)
    base_first = jnp.where(odd == 0, 2 * slab, 0)
    base_second = jnp.where(odd == 0, 0, 2 * slab)
    for k in range(groups):
        s = jnp.bitwise_xor(me, k)
        for base, ref, start in (
            (slab, refs[k], 0),
            (base_first, refs[groups], k * rows),
            (base_second, refs[groups + 1], k * rows),
        ):
            store(pl.multiple_of(base + s * blocks, SUB), ref, start)


def clear_tail(ref, first):
    if ref.shape[0] > first:
        ref[first:, :] = jnp.zeros((ref.shape[0] - first, ref.shape[1]), jnp.float32)


def parts_of(value):
    high = value.astype(jnp.bfloat16)
    rest = value - high.astype(jnp.float32)
    mid = rest.astype(jnp.bfloat16)
    return high, mid, (rest - mid.astype(jnp.float32)).astype(jnp.bfloat16)


def select(onehot, parts):
    total = None
    for part in reversed(parts):
        term = jnp.dot(onehot, part, preferred_element_type=jnp.float32)
        total = term if total is None else total + term
    return total


def far_fields(left, right, store):
    low = lane_iota(left.shape[0]) < HALF
    for n in range(left.shape[1] // LANES):
        one, two = left[:, n * LANES : (n + 1) * LANES], right[:, n * LANES : (n + 1) * LANES]
        store(2 * n, jnp.where(low, one, pltpu.roll(two, HALF, axis=1)))
        store(2 * n + 1, jnp.where(low, pltpu.roll(one, HALF, axis=1), two))


def column(value, index):
    at = index * SUB
    return jnp.broadcast_to(value[:, at : at + 1], (SUB, LANES))


def own_columns(cols, turned, d):
    turned[...] = pltpu.roll(cols[...], lax.rem(LANES - d, LANES), axis=1)


def group_rows(g):
    return slice(g * SUB, (g + 1) * SUB)


def put(result, g, slot, value):
    rows = group_rows(g)
    total = jnp.sum(value, axis=1, keepdims=True)
    result[rows, :] = jnp.where(lane_iota() == slot, total, result[rows, :])


def far_row(ref, field, tiles, d, t):
    return jnp.broadcast_to(ref[pl.ds((field * tiles + t) * SUB + d, 1), :], (SUB, LANES))


def each_slot(blocks, width, cols, turned, group):
    def slot(d, carry):
        own_columns(cols, turned, d)
        for g in range(width // SUB):
            group(d, g, turned[group_rows(g), :])
        return carry

    lax.fori_loop(0, blocks, slot, 0)


def sums_of(result, n, blocks, width):
    return jnp.transpose(result[...])[n * blocks : (n + 1) * blocks, 0:width]


def density_body(groups, blocks, width, tiles, *refs):
    parts = refs[: groups + 2]
    vol_out, rho_out, far, cols, own_rows, meta, hot, dist_out = refs[groups + 2 : groups + 10]
    region, own_range, own_tiles, turned, result = refs[groups + 10 :]
    slab = groups * blocks
    me = lax.axis_index("seg")
    kept = parts[groups].shape[0] // groups

    def store(at, ref, start):
        rows = pl.ds(at, SUB)
        for n in range(4):
            region[rows, n * LANES : (n + 1) * LANES] = ref[start + n * SUB : start + (n + 1) * SUB, :]
        meta[rows, :] = ref[start + 4 * SUB : start + 5 * SUB, :]

    place_region(groups, blocks, parts, kept, store)
    clear_tail(region, 3 * slab)
    clear_tail(meta, 3 * slab)
    for k in range(groups):
        rows = pl.ds(pl.multiple_of(jnp.bitwise_xor(me, k) * blocks, SUB), SUB)
        for n in range(6):
            own_range[rows, n * LANES : (n + 1) * LANES] = parts[k][n * SUB : (n + 1) * SUB, :]
    own_tiles[...] = jnp.zeros_like(own_tiles)
    result[...] = jnp.zeros_like(result)
    places = own_range[:, 4 * LANES + 2 * tiles : 4 * LANES + 2 * tiles + 1].astype(jnp.int32)
    wanted = me * blocks + lane_iota(slab)
    picks = jnp.where(jnp.broadcast_to(places, (slab, LANES)) == wanted, 1.0, 0.0)
    if slab < LANES:
        picks = jnp.concatenate([picks, jnp.zeros((LANES - slab, LANES), jnp.float32)], axis=0)
    picks = jnp.transpose(picks)[0:blocks, 0:slab].astype(jnp.bfloat16)
    mine = select(picks, parts_of(own_range[...]))
    entries = mine[:, 4 * LANES : 5 * LANES]
    for n in range(6):
        tile = mine[:, n * LANES : (n + 1) * LANES]
        if n == 4:
            continue
        at = 2 * n if n < 4 else 8
        own_rows[at] = tile
        own_rows[at + 1] = pltpu.roll(tile, HALF, axis=1)
    own_rows[10] = jnp.broadcast_to(entries[:, 2 * tiles + 1 : 2 * tiles + 2], (SUB, LANES))
    for n in range(8):
        own_tiles[n * SUB : (n + 1) * SUB, :] = own_rows[n]
    cols[...] = jnp.transpose(own_tiles[...])[0:width, :]
    size = region.shape[0]
    column_ids = lax.broadcasted_iota(jnp.int32, (SUB, size), 1)
    index = entries.astype(jnp.int32)
    for n in range(2 * tiles):
        chosen = jnp.broadcast_to(index[:, n : n + 1], (SUB, size)) == column_ids
        hot[n * SUB : (n + 1) * SUB, :] = jnp.where(chosen, 1.0, 0.0)
    values = parts_of(region[...])
    half = tiles * SUB
    left = select(hot[0:half, :].astype(jnp.bfloat16), values)
    right = select(hot[half:, :].astype(jnp.bfloat16), values)

    def keep(n, value):
        far[n * half : (n + 1) * half, :] = value

    far_fields(left, right, keep)

    def group(d, g, own):
        pos = [column(own, X + a) for a in range(3)]
        scale = 0.5 / column(own, SMOOTH)
        total = jnp.zeros((SUB, LANES), jnp.float32)
        for t in range(tiles):
            dx, dy, dz = [pos[a] - far_row(far, X + a, tiles, d, t) for a in range(3)]
            square = dx * dx + dy * dy + dz * dz
            dist = square * lax.rsqrt(jnp.maximum(square, TINY))
            dist_out[d, g, t] = dist
            ratio = dist * scale
            shell = jnp.maximum(1.0 - ratio, 0.0)
            shell = shell * shell
            shell = shell * shell
            total += shell * (far_row(far, MASS, tiles, d, t) * (0.25 + ratio))
        put(result, g, d, total)

    each_slot(blocks, width, cols, turned, group)
    sums = sums_of(result, 0, blocks, width)
    smooth, mass, count = [own_rows[n, :, 0:width] for n in (SMOOTH, MASS, 10)]
    live = jnp.where(lane_iota()[:, 0:width].astype(jnp.float32) < count, 1.0, 0.0)
    rho = 4.0 * SIGMA / (smooth * smooth * smooth) * sums + (1.0 - live)
    rho_out[...] = rho
    vol = mass / rho
    vol_out[...] = jnp.concatenate([vol, vol], axis=1)


def factor_body(groups, blocks, width, tiles, far, cols, meta, hot, dist, out, hot_out, turned):
    slab = groups * blocks
    size = hot.shape[1]
    spot = meta[:, 2 * tiles : 2 * tiles + 1].astype(jnp.int32)
    rows = lax.broadcasted_iota(jnp.int32, (size, size), 0)
    start = jnp.where(rows < slab, 0, jnp.where(rows < 2 * slab, slab, 2 * slab))
    chosen = start + spot == lax.broadcasted_iota(jnp.int32, (size, size), 1)
    moves = jnp.where(chosen, 1.0, 0.0).astype(jnp.bfloat16)
    hot_out[...] = jnp.dot(
        hot[...].astype(jnp.bfloat16), moves, preferred_element_type=jnp.float32
    )

    def group(d, g, own):
        smooth = column(own, SMOOTH)
        for t in range(tiles):
            inv = 1.0 / (smooth + far_row(far, SMOOTH, tiles, d, t))
            inv2 = inv * inv
            part = jnp.maximum(inv - dist[d, g, t] * inv2, 0.0)
            out[d, g, t] = part * part * part * inv2

    each_slot(blocks, width, cols, turned, group)


def tensor_body(groups, blocks, width, tiles, *refs):
    far, cols, own_rows, factor, hot, rho = refs[:6]
    vols = refs[6 : 8 + groups]
    coef_out, corr_out = refs[8 + groups : 10 + groups]
    turned, region, far_vol, result = refs[10 + groups :]
    slab = groups * blocks

    def store(at, ref, start):
        region[pl.ds(at, SUB), :] = ref[start : start + SUB, :]

    place_region(groups, blocks, vols, SUB, store)
    clear_tail(region, 3 * slab)
    result[...] = jnp.zeros_like(result)
    values = parts_of(region[...])
    half = tiles * SUB
    left = select(hot[0:half, :].astype(jnp.bfloat16), values)
    right = select(hot[half:, :].astype(jnp.bfloat16), values)
    far_vol[...] = jnp.where(lane_iota(half) < HALF, left, right)

    def group(d, g, own):
        pos = [column(own, X + a) for a in range(3)]
        total = [jnp.zeros((SUB, LANES), jnp.float32) for _ in range(6)]
        for t in range(tiles):
            dx, dy, dz = [pos[a] - far_row(far, X + a, tiles, d, t) for a in range(3)]
            weight = factor[d, g, t] * far_row(far_vol, 0, tiles, d, t)
            wx, wy, wz = weight * dx, weight * dy, weight * dz
            for n, term in enumerate((wx * dx, wy * dy, wz * dz, wx * dy, wx * dz, wy * dz)):
                total[n] += term
        for n in range(6):
            put(result, g, n * blocks + d, total[n])

    each_slot(blocks, width, cols, turned, group)
    sums = jnp.transpose(result[...])
    press = GAMMA_LESS * own_rows[8, :, 0:width] / rho[...]
    scale = own_rows[MASS, :, 0:width] * press
    coefs = []
    for n in range(6):
        tensor = SLOPE * sums[n * blocks : (n + 1) * blocks, 0:width]
        corr = (2.0 + tensor) if n < 3 else tensor
        corr_out[n] = corr
        coefs.append(scale * corr)
    corr_out[6] = press
    for n in range(3):
        coef_out[n * SUB : (n + 1) * SUB, :] = jnp.concatenate(coefs[2 * n : 2 * n + 2], axis=1)


def moment_body(blocks, width, tiles, far, cols, factor, out, slopes, turned, result):
    result[...] = jnp.zeros_like(result)

    def group(d, g, own):
        pos = [column(own, X + a) for a in range(3)]
        vel = [column(own, VEL + a) for a in range(3)]
        total = [jnp.zeros((SUB, LANES), jnp.float32) for _ in range(9)]
        for t in range(tiles):
            weight = factor[d, g, t]
            mass = far_row(far, MASS, tiles, d, t)
            slope = [weight * (pos[a] - far_row(far, X + a, tiles, d, t)) for a in range(3)]
            for a in range(3):
                slopes[a, d, g, t] = slope[a]
            px, py, pz = [mass * slope[a] for a in range(3)]
            vx, vy, vz = [vel[a] - far_row(far, VEL + a, tiles, d, t) for a in range(3)]
            terms = (
                px,
                py,
                pz,
                vx * px,
                vy * py,
                vz * pz,
                vx * py + vy * px,
                vx * pz + vz * px,
                vy * pz + vz * py,
            )
            for n, term in enumerate(terms):
                total[n] += term
        for n in range(9):
            put(result, g, n * blocks + d, total[n])

    each_slot(blocks, width, cols, turned, group)
    sums = jnp.transpose(result[...])
    for n in range(9):
        out[n] = sums[n * blocks : (n + 1) * blocks, 0:width]


def update_body(groups, blocks, width, tiles, *refs):
    own_rows, slopes, hot, corr, moments = refs[:5]
    coefs = refs[5 : 7 + groups]
    state_out = refs[7 + groups]
    region, far_coef, result = refs[8 + groups :]
    slab = groups * blocks

    def store(at, ref, start):
        for n in range(3):
            tile = ref[start + n * SUB : start + (n + 1) * SUB, :]
            region[pl.ds(at, SUB), n * LANES : (n + 1) * LANES] = tile

    place_region(groups, blocks, coefs, 3 * SUB, store)
    clear_tail(region, 3 * slab)
    result[...] = jnp.zeros_like(result)
    values = parts_of(region[...])
    half = tiles * SUB
    left = select(hot[0:half, :].astype(jnp.bfloat16), values)
    right = select(hot[half:, :].astype(jnp.bfloat16), values)

    def keep(n, value):
        far_coef[n * half : (n + 1) * half, :] = value

    far_fields(left, right, keep)

    def slot(d, carry):
        for g in range(width // SUB):
            total = [jnp.zeros((SUB, LANES), jnp.float32) for _ in range(3)]
            for t in range(tiles):
                ex, ey, ez = [slopes[a, d, g, t] for a in range(3)]
                xx, yy, zz, xy, xz, yz = [far_row(far_coef, n, tiles, d, t) for n in range(6)]
                total[0] += xx * ex + xy * ey + xz * ez
                total[1] += xy * ex + yy * ey + yz * ez
                total[2] += xz * ex + yz * ey + zz * ez
            for n in range(3):
                put(result, g, n * blocks + d, total[n])
        return carry

    lax.fori_loop(0, blocks, slot, 0)
    sums = jnp.transpose(result[...])
    field = lambda n: own_rows[n, :, 0:width]
    live = jnp.where(lane_iota()[:, 0:width].astype(jnp.float32) < field(10), 1.0, 0.0)
    press = corr[6]
    xx, yy, zz, xy, xz, yz = [corr[n] for n in range(6)]
    sx, sy, sz = [moments[n] for n in range(3)]
    near = (xx * sx + xy * sy + xz * sz, xy * sx + yy * sy + yz * sz, xz * sx + yz * sy + zz * sz)
    for a in range(3):
        far_sum = sums[a * blocks : (a + 1) * blocks, 0:width]
        accel = -SLOPE * live * (press * near[a] + far_sum)
        velocity = field(VEL + a) + STEP_DT * accel
        state_out[3 + a] = velocity
        state_out[a] = field(X + a) + STEP_DT * velocity
    heat = moments[3] * xx + moments[4] * yy + moments[5] * zz
    heat += moments[6] * xy + moments[7] * xz + moments[8] * yz
    state_out[6] = field(9)
    state_out[7] = field(SMOOTH)
    state_out[8] = field(8) + STEP_DT * (SLOPE * live * press * heat)


def exchange(own, send_rows):
    groups = lax.axis_size("seg")
    ranges = lax.axis_size("dom")
    seg = [own]
    for k in range(1, groups):
        seg.append(lax.ppermute(own, "seg", [(i, i ^ k) for i in range(groups)]))
    whole = jnp.concatenate([part[:send_rows] for part in seg], axis=0)
    first = [(i, i ^ 1) for i in range(ranges)]
    second = [(i, ((i + 1) ^ 1) - 1) for i in range(1, ranges - 1)]
    return seg + [lax.ppermute(whole, "dom", first), lax.ppermute(whole, "dom", second)]


def local(state, counts, neighbours, new_place):
    blocks, fields, width = state.shape
    nbr = neighbours.shape[1]
    groups = lax.axis_size("seg")
    slab = blocks * groups
    tiles = (nbr + 2) // 2
    size = -(-3 * slab // LANES) * LANES
    many = (blocks, width // SUB, tiles, SUB, LANES)
    f32, i32 = jnp.float32, jnp.int32
    vm = pl.BlockSpec(memory_space=VMEM)
    any_space = pl.BlockSpec(memory_space=pltpu.HBM)
    columns = VMEM((width, LANES), f32)
    packed = call(
        functools.partial(pack_body, blocks, width, nbr, tiles),
        shape(6 * SUB, LANES),
        in_specs=[any_space] * 4,
        out_specs=vm,
        scratch=(
            VMEM((fields, blocks, width), f32),
            VMEM((blocks, nbr), i32),
            SMEM((blocks,), i32),
            SMEM((blocks,), i32),
            pltpu.SemaphoreType.DMA((4,)),
        ),
        name="pack",
    )(counts, new_place, jnp.swapaxes(state, 0, 1), neighbours)
    parts = exchange(packed, 5 * SUB)
    vol, rho, far, cols, own_rows, meta, hot, dist = call(
        functools.partial(density_body, groups, blocks, width, tiles),
        (
            shape(SUB, LANES),
            shape(blocks, width),
            shape(8 * tiles * SUB, LANES),
            shape(width, LANES),
            shape(11, SUB, LANES),
            shape(size, LANES),
            shape(2 * tiles * SUB, size),
            shape(*many),
        ),
        in_specs=[vm] * (groups + 2),
        out_specs=(vm,) * 8,
        scratch=(
            VMEM((size, 4 * LANES), f32),
            VMEM((slab, 6 * LANES), f32),
            VMEM((LANES, LANES), f32),
            columns,
            columns,
        ),
        name="density",
    )(*parts)
    vols = exchange(vol, SUB)
    factor, placed = call(
        functools.partial(factor_body, groups, blocks, width, tiles),
        (shape(*many), shape(2 * tiles * SUB, size)),
        in_specs=[vm] * 5,
        out_specs=(vm, vm),
        scratch=(columns,),
        name="factor",
    )(far, cols, meta, hot, dist)
    coef, corr = call(
        functools.partial(tensor_body, groups, blocks, width, tiles),
        (shape(3 * SUB, LANES), shape(7, blocks, width)),
        in_specs=[vm] * (6 + groups + 2),
        out_specs=(vm, vm),
        scratch=(columns, VMEM((size, LANES), f32), VMEM((tiles * SUB, LANES), f32), columns),
        name="tensor",
    )(far, cols, own_rows, factor, placed, rho, *vols)
    coefs = exchange(coef, 3 * SUB)
    moments, slopes = call(
        functools.partial(moment_body, blocks, width, tiles),
        (shape(9, blocks, width), shape(3, *many)),
        in_specs=[vm] * 3,
        out_specs=(vm, vm),
        scratch=(columns, columns),
        name="moments",
    )(far, cols, factor)
    moved = call(
        functools.partial(update_body, groups, blocks, width, tiles),
        shape(fields, blocks, width),
        in_specs=[vm] * (5 + groups + 2),
        out_specs=vm,
        scratch=(
            VMEM((size, 3 * LANES), f32),
            VMEM((6 * tiles * SUB, LANES), f32),
            columns,
        ),
        name="update",
    )(own_rows, slopes, placed, corr, moments, *coefs)
    return (jnp.swapaxes(moved, 0, 1), rho)


def solution(mesh):
    return jax.shard_map(
        local,
        mesh=mesh,
        in_specs=(
            P(("dom", "seg"), None, None),
            P(("dom", "seg")),
            P(("dom", "seg"), None),
            P(("dom", "seg")),
        ),
        out_specs=(P(("dom", "seg"), None, None), P(("dom", "seg"), None)),
        check_vma=False,
    )
```

time: 218 us -> 62.4 us (0.29)
  local copies, waits for them, and re-layouts: 60.2 us -> 2.79 us
  loops' own time: 49.9 us -> 0 us
  blocking collectives: 39.9 us -> 0 us
  other arithmetic: 38.6 us -> 0.01 us
  Pallas kernels: 0 us -> 25.7 us
  waiting for transfers between devices: 1.12 us -> 9.58 us
    another operation x3 -> x0, loops' own time: 49.9 us -> none  [the longest x1 18.2 us: local(): accel, heat = lax.map(third, block_ids)]
    all_gather x5 -> x0, blocking collectives: 32.9 us -> none  [the longest x3 20.8 us: spread(): whole = lax.all_gather(values, 'seg', axis=0, tiled=True)]
    pallas_call x0 -> x6, Pallas kernels: none -> 25.7 us  [the longest x1 7.09 us: local(): call(functools.partial(moment_body, blocks, width, tiles), (shape(9, bloc...]
    gather x42 -> x0, local copies, waits for them, and re-layouts: 24.3 us -> none  [the longest x40 23.2 us: tile_of(): tile = jnp.take(region, index, axis=0)]
    reduce_sum x49 -> x0, other arithmetic: 18.6 us -> none  [the longest x8 6.64 us: tensor_tile(): jnp.sum(weight * diff[a] * diff[b], axis=1)]
    dynamic_slice x24 -> x0, local copies, waits for them, and re-layouts: 15.3 us -> none  [local(): rho = lax.map(first, block_ids) + (1.0 - live)]
    ppermute x6 -> x15, waiting for transfers between devices: 1.12 us -> 9.58 us  [the longest x9 6.94 us: exchange(): seg.append(lax.ppermute(own, 'seg', [(i, i ^ k) for i in range(groups)]))]
    unnamed x1 -> x0, blocking collectives: 6.98 us -> none
  transfers between devices with their start and end apart: 6 -> 15, of which waited for: 1 -> 7; matrix products, arithmetic and copies ran while one was open for 2% -> 0% of each run, Pallas kernels for 0% -> 15%
where the time goes in v3:
time: 62.4 us; the launch traced here: 62.1 us
  Pallas kernels  25.7 us (41%)
  starting transfers between devices  23.3 us (37%)
  waiting for transfers between devices  9.58 us (15%)
  local copies, waits for them, and re-layouts  2.79 us (4%)
  between operations  0.77 us (1%)
    ppermute x3, starting transfers between devices, exchange(): lax.ppermute(whole, 'dom', second)  12.1 us
    ppermute x9, starting transfers between devices, exchange(): seg.append(lax.ppermute(own, 'seg', [(i, i ^ k) for i in range(groups)]))  8.72 us
    pallas_call x1, Pallas kernels, local(): call(functools.partial(moment_body, blocks, width, tiles), (shape(9, bloc...  7.09 us
    ppermute x9, waiting for transfers between devices, exchange(): seg.append(lax.ppermute(own, 'seg', [(i, i ^ k) for i in range(groups)]))  6.94 us
    pallas_call x1, Pallas kernels, local(): call(functools.partial(density_body, groups, blocks, width, tiles), (shap...  5.71 us
    pallas_call x1, Pallas kernels, local(): call(functools.partial(tensor_body, groups, blocks, width, tiles), (shape...  5.04 us
    pallas_call x1, Pallas kernels, local(): call(functools.partial(update_body, groups, blocks, width, tiles), shape(...  4.64 us
    unnamed x16, local copies, waits for them, and re-layouts  2.77 us
  transfers between devices with their start and end apart: 15, of which 7 were waited for; matrix products, arithmetic and copies ran while one was open for 0% of the time, Pallas kernels for 15%

profile of v3, /device:TPU:1, one launch (start us, length us, event | category | flops | bytes accessed | tf_op | source)
XLA Modules:
  0.0 62.1 jit_solution(10227831988498107429)
XLA Ops:
  0.6 0.8 %copy-done = f32[8,9,64]{2,0,1:T(8,128)S(1)} copy-done((f32[8,9,64]{2,0,1:T(8,128)S(1)}, f32[8,9,64]{2,0,1:T(8,128)}, u32[]{:S(2)}) %copy-start) | copy-done | bytes 18456
  1.4 0.7 %copy-done.1 = s32[8,26]{1,0:T(8,128)S(1)} copy-done((s32[8,26]{1,0:T(8,128)S(1)}, s32[8,26]{1,0:T(8,128)}, u32[]{:S(2)}) %copy-start.1) | copy-done | bytes 856
  2.1 0.7 %copy-done.3 = s32[8]{0:T(128)S(1)} copy-done((s32[8]{0:T(128)S(1)}, s32[8]{0:T(128)}, u32[]{:S(2)}) %copy-start.3) | copy-done | bytes 56
  2.7 0.7 %copy-done.4 = s32[8]{0:T(128)S(1)} copy-done((s32[8]{0:T(128)S(1)}, s32[8]{0:T(128)}, u32[]{:S(2)}) %copy-start.4) | copy-done | bytes 56
  3.4 0.7 %pack.1.refs_0_ = f32[48,128]{1,0:T(8,128)S(1)} custom-call(s32[8]{0:T(128)S(1)} %copy-done.3, s32[8]{0:T(128)S(1)} %copy-done.4, f32[9,8,64]{2,1,0:T(8,128)S(1)} %bitcast.2, s32[8,26]{1,0:T(8,128)S(1)} %copy-done.1), custom_call_target="tpu_custom_call" | custom-call | tf_op jit(solution)/shard_map/pack/pallas_call | solution.py:439
  4.1 3.0 %collective-permute-start.2 = (f32[48,128]{1,0:T(8,128)S(1)}, f32[48,128]{1,0:T(8,128)S(1)}, u32[]{:S(2)}, u32[]{:S(2)}) collective-permute-start(f32[48,128]{1,0:T(8,128)S(1)} %pack.1.refs_0_), channel_id=1, source_target_pairs={{0,3},{1,2},{2,1},{3,0},{4,7},{5,6},{6,5},{7,4},{8,11},{9,10},{10,... | collective-permute-start | bytes 73736 | tf_op jit(solution)/shard_map/ppermute | solution.py:420
  7.1 0.2 collective-permute-start.1
  7.4 0.1 collective-permute-start
  7.5 0.9 %collective-permute-done.2.refs_3_ = f32[48,128]{1,0:T(8,128)S(1)} collective-permute-done((f32[48,128]{1,0:T(8,128)S(1)}, f32[48,128]{1,0:T(8,128)S(1)}, u32[]{:S(2)}, u32[]{:S(2)}) %collective-permute-start.2) | collective-permute-done | bytes 24608 | tf_op jit(solution)/shard_map/ppermute | solution.py:420
  8.4 1.5 %collective-permute-done.1.refs_2_ = f32[48,128]{1,0:T(8,128)S(1)} collective-permute-done((f32[48,128]{1,0:T(8,128)S(1)}, f32[48,128]{1,0:T(8,128)S(1)}, u32[]{:S(2)}, u32[]{:S(2)}) %collective-permute-start.1) | collective-permute-done | bytes 24608 | tf_op jit(solution)/shard_map/ppermute | solution.py:420
  9.8 0.2 collective-permute-done.refs_1_
  10.0 2.5 %collective-permute-start.3 = (f32[160,128]{1,0:T(8,128)S(1)}, f32[160,128]{1,0:T(8,128)S(1)}, u32[]{:S(2)}, u32[]{:S(2)}) collective-permute-start(f32[160,128]{1,0:T(8,128)S(1)} %pad_maximum_fusion), channel_id=1, source_target_pairs={{0,4},{4,0},{8,12},{12,8},{16,20},{20,16},{24,28},{28,24},{1,5},{5... | collective-permute-start | bytes 245768 | tf_op jit(solution)/shard_map/ppermute | solution.py:424
  12.5 3.1 %collective-permute-start.4 = (f32[160,128]{1,0:T(8,128)S(1)}, f32[160,128]{1,0:T(8,128)S(1)}, u32[]{:S(2)}, u32[]{:S(2)}) collective-permute-start(f32[160,128]{1,0:T(8,128)S(1)} %pad_maximum_fusion), channel_id=1, source_target_pairs={{4,8},{8,4},{12,16},{16,12},{20,24},{24,20},{5,9},{9,5},{13,17},{1... | collective-permute-start | bytes 245768 | tf_op jit(solution)/shard_map/ppermute | solution.py:424
  15.6 0.0 collective-permute-done.3.refs_4_
  15.6 2.6 %collective-permute-done.4.refs_5_ = f32[160,128]{1,0:T(8,128)S(1)} collective-permute-done((f32[160,128]{1,0:T(8,128)S(1)}, f32[160,128]{1,0:T(8,128)S(1)}, u32[]{:S(2)}, u32[]{:S(2)}) %collective-permute-start.4) | collective-permute-done | bytes 81952 | tf_op jit(solution)/shard_map/ppermute | solution.py:424
  18.2 5.7 %density.1 = (f32[8,128]{1,0:T(8,128)S(1)}, f32[8,64]{1,0:T(8,128)}, f32[896,128]{1,0:T(8,128)S(1)}, f32[64,128]{1,0:T(8,128)S(1)}, f32[11,8,128]{2,1,0:T(8,128)...) custom-call(f32[48,128]{1,0:T(8,128)S(1)} %pack.1.refs_0_, ...), custom_call_target="tpu_custom_call" | custom-call | tf_op jit(solution)/shard_map/density/pallas_call | solution.py:454
  24.0 1.5 %collective-permute-start.6 = (f32[8,128]{1,0:T(8,128)S(1)}, f32[8,128]{1,0:T(8,128)S(1)}, u32[]{:S(2)}, u32[]{:S(2)}) collective-permute-start(f32[8,128]{1,0:T(8,128)S(1)} %get-tuple-element.26.refs_6_), channel_id=1, source_target_pairs={{0,2},{1,3},{2,0},{3,1},{4,6},{5,7},{6,4},{7,5},{8,10},{9,11},{10,... | collective-permute-start | bytes 12296 | tf_op jit(solution)/shard_map/ppermute | solution.py:420
  25.5 1.2 %collective-permute-start.7 = (f32[8,128]{1,0:T(8,128)S(1)}, f32[8,128]{1,0:T(8,128)S(1)}, u32[]{:S(2)}, u32[]{:S(2)}) collective-permute-start(f32[8,128]{1,0:T(8,128)S(1)} %get-tuple-element.26.refs_6_), channel_id=1, source_target_pairs={{0,3},{1,2},{2,1},{3,0},{4,7},{5,6},{6,5},{7,4},{8,11},{9,10},{10,... | collective-permute-start | bytes 12296 | tf_op jit(solution)/shard_map/ppermute | solution.py:420
  26.6 2.2 %collective-permute-done.7.refs_9_ = f32[8,128]{1,0:T(8,128)S(1)} collective-permute-done((f32[8,128]{1,0:T(8,128)S(1)}, f32[8,128]{1,0:T(8,128)S(1)}, u32[]{:S(2)}, u32[]{:S(2)}) %collective-permute-start.7) | collective-permute-done | bytes 4128 | tf_op jit(solution)/shard_map/ppermute | solution.py:420
  28.8 0.0 collective-permute-start.8
  28.8 4.8 %collective-permute-start.9 = (f32[32,128]{1,0:T(8,128)S(1)}, f32[32,128]{1,0:T(8,128)S(1)}, u32[]{:S(2)}, u32[]{:S(2)}) collective-permute-start(f32[32,128]{1,0:T(8,128)S(1)} %constant_dynamic-update-slice_fusion), channel_id=1, source_target_pairs={{4,8},{8,4},{12,16},{16,12},{20,24},{24,20},{5,9},{9,5},{13,17},{1... | collective-permute-start | bytes 49160 | tf_op jit(solution)/shard_map/ppermute | solution.py:424
  33.6 2.5 %factor.1 = (f32[8,8,14,8,128]{4,3,2,1,0:T(8,128)S(1)}, f32[224,128]{1,0:T(8,128)S(1)}) custom-call(f32[896,128]{1,0:T(8,128)S(1)} %get-tuple-element.17.far.refs_0_, f32[64,128]{1,0:T(8,128)S(1)} %get-tuple-element.18.cols.refs_1_, f32[128,128]{1,0:T(8,128)S(1)} %get-tuple-element.19.meta, f32[224,128]{1,0:T(8,128)S(1)} %get-tuple-element.20.hot, ...), custom_call_target="tpu_custom_call" | custom-call | tf_op jit(solution)/shard_map/factor/pallas_call | solution.py:478
  36.2 5.0 %tensor.1 = (f32[24,128]{1,0:T(8,128)S(1)}, f32[7,8,64]{2,1,0:T(8,128)S(1)}) custom-call(f32[896,128]{1,0:T(8,128)S(1)} %get-tuple-element.17.far.refs_0_, f32[64,128]{1,0:T(8,128)S(1)} %get-tuple-element.18.cols.refs_1_, f32[11,8,128]{2,1,0:T(8,128)S(1)} %get-tuple-element.16.refs_2_.refs_0_, f32[8,8,14,8,128]{4,3,2,1,0:T(8,128)S(1)} %get-tuple-element.22.factor.refs_3_, ...), custom_call_target="tpu_custom_call" | custom-call | tf_op jit(solution)/shard_map/tensor/pallas_call | solution.py:486
  41.2 1.2 %collective-permute-start.10 = (f32[24,128]{1,0:T(8,128)S(1)}, f32[24,128]{1,0:T(8,128)S(1)}, u32[]{:S(2)}, u32[]{:S(2)}) collective-permute-start(f32[24,128]{1,0:T(8,128)S(1)} %get-tuple-element.29.refs_5_), channel_id=1, source_target_pairs={{0,1},{1,0},{2,3},{3,2},{4,5},{5,4},{6,7},{7,6},{8,9},{9,8},{10,11... | collective-permute-start | bytes 36872 | tf_op jit(solution)/shard_map/ppermute | solution.py:420
  42.5 0.2 collective-permute-start.11
  42.7 1.2 %collective-permute-start.12 = (f32[24,128]{1,0:T(8,128)S(1)}, f32[24,128]{1,0:T(8,128)S(1)}, u32[]{:S(2)}, u32[]{:S(2)}) collective-permute-start(f32[24,128]{1,0:T(8,128)S(1)} %get-tuple-element.29.refs_5_), channel_id=1, source_target_pairs={{0,3},{1,2},{2,1},{3,0},{4,7},{5,6},{6,5},{7,4},{8,11},{9,10},{10,... | collective-permute-start | bytes 36872 | tf_op jit(solution)/shard_map/ppermute | solution.py:420
  43.9 1.1 %collective-permute-done.11.refs_7_ = f32[24,128]{1,0:T(8,128)S(1)} collective-permute-done((f32[24,128]{1,0:T(8,128)S(1)}, f32[24,128]{1,0:T(8,128)S(1)}, u32[]{:S(2)}, u32[]{:S(2)}) %collective-permute-start.11) | collective-permute-done | bytes 12320 | tf_op jit(solution)/shard_map/ppermute | solution.py:420
  45.0 1.1 %collective-permute-done.12.refs_8_ = f32[24,128]{1,0:T(8,128)S(1)} collective-permute-done((f32[24,128]{1,0:T(8,128)S(1)}, f32[24,128]{1,0:T(8,128)S(1)}, u32[]{:S(2)}, u32[]{:S(2)}) %collective-permute-start.12) | collective-permute-done | bytes 12320 | tf_op jit(solution)/shard_map/ppermute | solution.py:420
  46.2 4.2 %collective-permute-start.14 = (f32[96,128]{1,0:T(8,128)S(1)}, f32[96,128]{1,0:T(8,128)S(1)}, u32[]{:S(2)}, u32[]{:S(2)}) collective-permute-start(f32[96,128]{1,0:T(8,128)S(1)} %constant_dynamic-update-slice_fusion.4), channel_id=1, source_target_pairs={{4,8},{8,4},{12,16},{16,12},{20,24},{24,20},{5,9},{9,5},{13,17},{1... | collective-permute-start | bytes 147464 | tf_op jit(solution)/shard_map/ppermute | solution.py:424
  50.3 7.1 %moments.1 = (f32[9,8,64]{2,1,0:T(8,128)S(1)}, f32[3,8,8,14,8,128]{5,4,3,2,1,0:T(8,128)S(1)}) custom-call(f32[896,128]{1,0:T(8,128)S(1)} %get-tuple-element.17.far.refs_0_, f32[64,128]{1,0:T(8,128)S(1)} %get-tuple-element.18.cols.refs_1_, f32[8,8,14,8,128]{4,3,2,1,0:T(8,128)S(1)} %get-tuple-element.22.factor.refs_3_), custom_call_target="tpu_custom_call" | custom-call | tf_op jit(solution)/shard_map/moments/pallas_call | solution.py:495
  57.4 0.0 collective-permute-done.13.refs_9_
  57.4 4.6 %update.1 = f32[9,8,64]{2,1,0:T(8,128)} custom-call(f32[11,8,128]{2,1,0:T(8,128)S(1)} %get-tuple-element.16.refs_2_.refs_0_, f32[3,8,8,14,8,128]{5,4,3,2,1,0:T(8,128)S(1)} %get-tuple-element.23.refs_1_, f32[224,128]{1,0:T(8,128)S(1)} %get-tuple-element.24.refs_4_.refs_2_, f32[7,8,64]{2,1,0:T(8,128)S(1)} %get-tuple-element.27.refs_3_, ...), custom_call_target="tpu_custom_call" | custom-call | tf_op jit(solution)/shard_map/update/pallas_call | solution.py:503
  (27 shorter events, 0.1 us)
Async XLA Ops:
  0.6 0.8 %copy-start = (f32[8,9,64]{2,0,1:T(8,128)S(1)}, f32[8,9,64]{2,0,1:T(8,128)}, u32[]{:S(2)}) copy-start(f32[8,9,64]{2,0,1:T(8,128)} %param.4) | copy-start | bytes 55300
  1.4 0.7 %copy-start.1 = (s32[8,26]{1,0:T(8,128)S(1)}, s32[8,26]{1,0:T(8,128)}, u32[]{:S(2)}) copy-start(s32[8,26]{1,0:T(8,128)} %refs_3_.1) | copy-start | bytes 2500
  2.1 0.7 %copy-start.3 = (s32[8]{0:T(128)S(1)}, s32[8]{0:T(128)}, u32[]{:S(2)}) copy-start(s32[8]{0:T(128)} %refs_0_.1) | copy-start | bytes 100
  2.7 0.7 %copy-start.4 = (s32[8]{0:T(128)S(1)}, s32[8]{0:T(128)}, u32[]{:S(2)}) copy-start(s32[8]{0:T(128)} %refs_1_.1) | copy-start | bytes 100
  4.1 4.3 %collective-permute-start.2 = (f32[48,128]{1,0:T(8,128)S(1)}, f32[48,128]{1,0:T(8,128)S(1)}, u32[]{:S(2)}, u32[]{:S(2)}) collective-permute-start(f32[48,128]{1,0:T(8,128)S(1)} %pack.1.refs_0_), channel_id=1, source_target_pairs={{0,3},{1,2},{2,1},{3,0},{4,7},{5,6},{6,5},{7,4},{8,11},{9,10},{10,... | collective-permute-start | bytes 73736 | tf_op jit(solution)/shard_map/ppermute | solution.py:420
  7.1 2.7 %collective-permute-start.1 = (f32[48,128]{1,0:T(8,128)S(1)}, f32[48,128]{1,0:T(8,128)S(1)}, u32[]{:S(2)}, u32[]{:S(2)}) collective-permute-start(f32[48,128]{1,0:T(8,128)S(1)} %pack.1.refs_0_), channel_id=1, source_target_pairs={{0,2},{1,3},{2,0},{3,1},{4,6},{5,7},{6,4},{7,5},{8,10},{9,11},{10,... | collective-permute-start | bytes 73736 | tf_op jit(solution)/shard_map/ppermute | solution.py:420
  7.4 2.7 %collective-permute-start = (f32[48,128]{1,0:T(8,128)S(1)}, f32[48,128]{1,0:T(8,128)S(1)}, u32[]{:S(2)}, u32[]{:S(2)}) collective-permute-start(f32[48,128]{1,0:T(8,128)S(1)} %pack.1.refs_0_), channel_id=1, source_target_pairs={{0,1},{1,0},{2,3},{3,2},{4,5},{5,4},{6,7},{7,6},{8,9},{9,8},{10,11... | collective-permute-start | bytes 73736 | tf_op jit(solution)/shard_map/ppermute | solution.py:420
  10.0 5.6 %collective-permute-start.3 = (f32[160,128]{1,0:T(8,128)S(1)}, f32[160,128]{1,0:T(8,128)S(1)}, u32[]{:S(2)}, u32[]{:S(2)}) collective-permute-start(f32[160,128]{1,0:T(8,128)S(1)} %pad_maximum_fusion), channel_id=1, source_target_pairs={{0,4},{4,0},{8,12},{12,8},{16,20},{20,16},{24,28},{28,24},{1,5},{5... | collective-permute-start | bytes 245768 | tf_op jit(solution)/shard_map/ppermute | solution.py:424
  12.5 5.7 %collective-permute-start.4 = (f32[160,128]{1,0:T(8,128)S(1)}, f32[160,128]{1,0:T(8,128)S(1)}, u32[]{:S(2)}, u32[]{:S(2)}) collective-permute-start(f32[160,128]{1,0:T(8,128)S(1)} %pad_maximum_fusion), channel_id=1, source_target_pairs={{4,8},{8,4},{12,16},{16,12},{20,24},{24,20},{5,9},{9,5},{13,17},{1... | collective-permute-start | bytes 245768 | tf_op jit(solution)/shard_map/ppermute | solution.py:424
  24.0 12.2 %copy-start.2 = (f32[8,64]{1,0:T(8,128)S(1)}, f32[8,64]{1,0:T(8,128)}, u32[]{:S(2)}) copy-start(f32[8,64]{1,0:T(8,128)} %get-tuple-element.15.refs_5_) | copy-start | bytes 6148
  24.0 2.7 %collective-permute-start.5 = (f32[8,128]{1,0:T(8,128)S(1)}, f32[8,128]{1,0:T(8,128)S(1)}, u32[]{:S(2)}, u32[]{:S(2)}) collective-permute-start(f32[8,128]{1,0:T(8,128)S(1)} %get-tuple-element.26.refs_6_), channel_id=1, source_target_pairs={{0,1},{1,0},{2,3},{3,2},{4,5},{5,4},{6,7},{7,6},{8,9},{9,8},{10,11... | collective-permute-start | bytes 12296 | tf_op jit(solution)/shard_map/ppermute | solution.py:420
  24.0 2.7 %collective-permute-start.6 = (f32[8,128]{1,0:T(8,128)S(1)}, f32[8,128]{1,0:T(8,128)S(1)}, u32[]{:S(2)}, u32[]{:S(2)}) collective-permute-start(f32[8,128]{1,0:T(8,128)S(1)} %get-tuple-element.26.refs_6_), channel_id=1, source_target_pairs={{0,2},{1,3},{2,0},{3,1},{4,6},{5,7},{6,4},{7,5},{8,10},{9,11},{10,... | collective-permute-start | bytes 12296 | tf_op jit(solution)/shard_map/ppermute | solution.py:420
  25.5 3.4 %collective-permute-start.7 = (f32[8,128]{1,0:T(8,128)S(1)}, f32[8,128]{1,0:T(8,128)S(1)}, u32[]{:S(2)}, u32[]{:S(2)}) collective-permute-start(f32[8,128]{1,0:T(8,128)S(1)} %get-tuple-element.26.refs_6_), channel_id=1, source_target_pairs={{0,3},{1,2},{2,1},{3,0},{4,7},{5,6},{6,5},{7,4},{8,11},{9,10},{10,... | collective-permute-start | bytes 12296 | tf_op jit(solution)/shard_map/ppermute | solution.py:420
  28.8 7.4 %collective-permute-start.8 = (f32[32,128]{1,0:T(8,128)S(1)}, f32[32,128]{1,0:T(8,128)S(1)}, u32[]{:S(2)}, u32[]{:S(2)}) collective-permute-start(f32[32,128]{1,0:T(8,128)S(1)} %constant_dynamic-update-slice_fusion), channel_id=1, source_target_pairs={{0,4},{4,0},{8,12},{12,8},{16,20},{20,16},{24,28},{28,24},{1,5},{5... | collective-permute-start | bytes 49160 | tf_op jit(solution)/shard_map/ppermute | solution.py:424
  28.8 7.4 %collective-permute-start.9 = (f32[32,128]{1,0:T(8,128)S(1)}, f32[32,128]{1,0:T(8,128)S(1)}, u32[]{:S(2)}, u32[]{:S(2)}) collective-permute-start(f32[32,128]{1,0:T(8,128)S(1)} %constant_dynamic-update-slice_fusion), channel_id=1, source_target_pairs={{4,8},{8,4},{12,16},{16,12},{20,24},{24,20},{5,9},{9,5},{13,17},{1... | collective-permute-start | bytes 49160 | tf_op jit(solution)/shard_map/ppermute | solution.py:424
  41.2 2.7 %collective-permute-start.10 = (f32[24,128]{1,0:T(8,128)S(1)}, f32[24,128]{1,0:T(8,128)S(1)}, u32[]{:S(2)}, u32[]{:S(2)}) collective-permute-start(f32[24,128]{1,0:T(8,128)S(1)} %get-tuple-element.29.refs_5_), channel_id=1, source_target_pairs={{0,1},{1,0},{2,3},{3,2},{4,5},{5,4},{6,7},{7,6},{8,9},{9,8},{10,11... | collective-permute-start | bytes 36872 | tf_op jit(solution)/shard_map/ppermute | solution.py:420
  42.5 2.5 %collective-permute-start.11 = (f32[24,128]{1,0:T(8,128)S(1)}, f32[24,128]{1,0:T(8,128)S(1)}, u32[]{:S(2)}, u32[]{:S(2)}) collective-permute-start(f32[24,128]{1,0:T(8,128)S(1)} %get-tuple-element.29.refs_5_), channel_id=1, source_target_pairs={{0,2},{1,3},{2,0},{3,1},{4,6},{5,7},{6,4},{7,5},{8,10},{9,11},{10,... | collective-permute-start | bytes 36872 | tf_op jit(solution)/shard_map/ppermute | solution.py:420
  42.7 3.4 %collective-permute-start.12 = (f32[24,128]{1,0:T(8,128)S(1)}, f32[24,128]{1,0:T(8,128)S(1)}, u32[]{:S(2)}, u32[]{:S(2)}) collective-permute-start(f32[24,128]{1,0:T(8,128)S(1)} %get-tuple-element.29.refs_5_), channel_id=1, source_target_pairs={{0,3},{1,2},{2,1},{3,0},{4,7},{5,6},{6,5},{7,4},{8,11},{9,10},{10,... | collective-permute-start | bytes 36872 | tf_op jit(solution)/shard_map/ppermute | solution.py:420
  46.1 11.3 %collective-permute-start.13 = (f32[96,128]{1,0:T(8,128)S(1)}, f32[96,128]{1,0:T(8,128)S(1)}, u32[]{:S(2)}, u32[]{:S(2)}) collective-permute-start(f32[96,128]{1,0:T(8,128)S(1)} %constant_dynamic-update-slice_fusion.4), channel_id=1, source_target_pairs={{0,4},{4,0},{8,12},{12,8},{16,20},{20,16},{24,28},{28,24},{1,5},{5... | collective-permute-start | bytes 147464 | tf_op jit(solution)/shard_map/ppermute | solution.py:424
  46.2 11.3 %collective-permute-start.14 = (f32[96,128]{1,0:T(8,128)S(1)}, f32[96,128]{1,0:T(8,128)S(1)}, u32[]{:S(2)}, u32[]{:S(2)}) collective-permute-start(f32[96,128]{1,0:T(8,128)S(1)} %constant_dynamic-update-slice_fusion.4), channel_id=1, source_target_pairs={{4,8},{8,4},{12,16},{16,12},{20,24},{24,20},{5,9},{9,5},{13,17},{1... | collective-permute-start | bytes 147464 | tf_op jit(solution)/shard_map/ppermute | solution.py:424

commit v4 on v3

--- a/solution.py
+++ b/solution.py
@@ -8,11 +8,13 @@
 from jax.experimental.pallas import tpu as pltpu
 from jax.sharding import PartitionSpec as P
 
+
 SIGMA = 21.0 / (16.0 * math.pi)
 GAMMA_LESS = 2.0 / 3.0
 STEP_DT = 0.1
 SLOPE = -5.0 * SIGMA * 32.0
 TINY = 1e-37
+SPLIT = (2, 6, 8)
 SUB = 8
 LANES = 128
 X, SMOOTH, MASS, VEL = 0, 3, 4, 5
@@ -29,7 +31,7 @@
     return lax.broadcasted_iota(jnp.int32, (rows, LANES), 0)
 
 
-def call(body, outs, scratch=(), in_specs=None, out_specs=None, name=None, grant=8):
+def call(body, outs, scratch=(), in_specs=None, out_specs=None, grant=8):
     return pl.pallas_call(
         body,
         out_shape=outs,
@@ -37,7 +39,6 @@
         out_specs=out_specs,
         scratch_shapes=list(scratch),
         compiler_params=pltpu.CompilerParams(vmem_limit_bytes=grant << 20),
-        name=name,
     )
 
 
@@ -82,7 +83,7 @@
     out[5 * SUB : 6 * SUB, :] = jnp.concatenate([rows[8], rows[6]], axis=1)
 
 
-def place_region(groups, blocks, refs, rows, store):
+def place_region(groups, blocks, refs, rows, region, store):
     slab = groups * blocks
     me = lax.axis_index("seg")
     odd = lax.rem(lax.axis_index("dom"), 2)
@@ -96,6 +97,14 @@
             (base_second, refs[groups + 1], k * rows),
         ):
             store(pl.multiple_of(base + s * blocks, SUB), ref, start)
+    at_end = (lax.axis_index("dom") == 0) | (lax.axis_index("dom") == lax.axis_size("dom") - 1)
+
+    @pl.when(at_end)
+    def _():
+        rows = pl.ds(pl.multiple_of(base_second, SUB), slab)
+        region[rows, :] = jnp.zeros((slab, region.shape[1]), jnp.float32)
+
+    clear_tail(region, 3 * slab)
 
 
 def clear_tail(ref, first):
@@ -149,14 +158,14 @@
     return jnp.broadcast_to(ref[pl.ds((field * tiles + t) * SUB + d, 1), :], (SUB, LANES))
 
 
-def each_slot(blocks, width, cols, turned, group):
+def each_slot(first, count, width, cols, turned, group):
     def slot(d, carry):
-        own_columns(cols, turned, d)
+        own_columns(cols, turned, first + d)
         for g in range(width // SUB):
             group(d, g, turned[group_rows(g), :])
         return carry
 
-    lax.fori_loop(0, blocks, slot, 0)
+    lax.fori_loop(0, count, slot, 0)
 
 
 def sums_of(result, n, blocks, width):
@@ -177,8 +186,7 @@
             region[rows, n * LANES : (n + 1) * LANES] = ref[start + n * SUB : start + (n + 1) * SUB, :]
         meta[rows, :] = ref[start + 4 * SUB : start + 5 * SUB, :]
 
-    place_region(groups, blocks, parts, kept, store)
-    clear_tail(region, 3 * slab)
+    place_region(groups, blocks, parts, kept, region, store)
     clear_tail(meta, 3 * slab)
     for k in range(groups):
         rows = pl.ds(pl.multiple_of(jnp.bitwise_xor(me, k) * blocks, SUB), SUB)
@@ -237,7 +245,7 @@
             total += shell * (far_row(far, MASS, tiles, d, t) * (0.25 + ratio))
         put(result, g, d, total)
 
-    each_slot(blocks, width, cols, turned, group)
+    each_slot(0, blocks, width, cols, turned, group)
     sums = sums_of(result, 0, blocks, width)
     smooth, mass, count = [own_rows[n, :, 0:width] for n in (SMOOTH, MASS, 10)]
     live = jnp.where(lane_iota()[:, 0:width].astype(jnp.float32) < count, 1.0, 0.0)
@@ -267,7 +275,7 @@
             part = jnp.maximum(inv - dist[d, g, t] * inv2, 0.0)
             out[d, g, t] = part * part * part * inv2
 
-    each_slot(blocks, width, cols, turned, group)
+    each_slot(0, blocks, width, cols, turned, group)
 
 
 def tensor_body(groups, blocks, width, tiles, *refs):
@@ -275,13 +283,11 @@
     vols = refs[6 : 8 + groups]
     coef_out, corr_out = refs[8 + groups : 10 + groups]
     turned, region, far_vol, result = refs[10 + groups :]
-    slab = groups * blocks
 
     def store(at, ref, start):
         region[pl.ds(at, SUB), :] = ref[start : start + SUB, :]
 
-    place_region(groups, blocks, vols, SUB, store)
-    clear_tail(region, 3 * slab)
+    place_region(groups, blocks, vols, SUB, region, store)
     result[...] = jnp.zeros_like(result)
     values = parts_of(region[...])
     half = tiles * SUB
@@ -301,7 +307,7 @@
         for n in range(6):
             put(result, g, n * blocks + d, total[n])
 
-    each_slot(blocks, width, cols, turned, group)
+    each_slot(0, blocks, width, cols, turned, group)
     sums = jnp.transpose(result[...])
     press = GAMMA_LESS * own_rows[8, :, 0:width] / rho[...]
     scale = own_rows[MASS, :, 0:width] * press
@@ -316,21 +322,22 @@
         coef_out[n * SUB : (n + 1) * SUB, :] = jnp.concatenate(coefs[2 * n : 2 * n + 2], axis=1)
 
 
-def moment_body(blocks, width, tiles, far, cols, factor, out, slopes, turned, result):
+def moment_body(first, count, blocks, width, tiles, far, cols, factor, out, slopes, turned, result):
     result[...] = jnp.zeros_like(result)
 
     def group(d, g, own):
+        at = first + d
         pos = [column(own, X + a) for a in range(3)]
         vel = [column(own, VEL + a) for a in range(3)]
         total = [jnp.zeros((SUB, LANES), jnp.float32) for _ in range(9)]
         for t in range(tiles):
-            weight = factor[d, g, t]
-            mass = far_row(far, MASS, tiles, d, t)
-            slope = [weight * (pos[a] - far_row(far, X + a, tiles, d, t)) for a in range(3)]
+            weight = factor[at, g, t]
+            mass = far_row(far, MASS, tiles, at, t)
+            slope = [weight * (pos[a] - far_row(far, X + a, tiles, at, t)) for a in range(3)]
             for a in range(3):
                 slopes[a, d, g, t] = slope[a]
             px, py, pz = [mass * slope[a] for a in range(3)]
-            vx, vy, vz = [vel[a] - far_row(far, VEL + a, tiles, d, t) for a in range(3)]
+            vx, vy, vz = [vel[a] - far_row(far, VEL + a, tiles, at, t) for a in range(3)]
             terms = (
                 px,
                 py,
@@ -345,28 +352,27 @@
             for n, term in enumerate(terms):
                 total[n] += term
         for n in range(9):
-            put(result, g, n * blocks + d, total[n])
-
-    each_slot(blocks, width, cols, turned, group)
+            put(result, g, n * blocks + at, total[n])
+
+    each_slot(first, count, width, cols, turned, group)
     sums = jnp.transpose(result[...])
     for n in range(9):
         out[n] = sums[n * blocks : (n + 1) * blocks, 0:width]
 
 
-def update_body(groups, blocks, width, tiles, *refs):
-    own_rows, slopes, hot, corr, moments = refs[:5]
-    coefs = refs[5 : 7 + groups]
-    state_out = refs[7 + groups]
-    region, far_coef, result = refs[8 + groups :]
-    slab = groups * blocks
+def update_body(spans, groups, blocks, width, tiles, *refs):
+    own_rows, hot, corr = refs[:3]
+    pieces, refs = refs[3 : 3 + 2 * len(spans)], refs[3 + 2 * len(spans) :]
+    coefs = refs[: 2 + groups]
+    state_out = refs[2 + groups]
+    region, far_coef, result = refs[3 + groups :]
 
     def store(at, ref, start):
         for n in range(3):
             tile = ref[start + n * SUB : start + (n + 1) * SUB, :]
             region[pl.ds(at, SUB), n * LANES : (n + 1) * LANES] = tile
 
-    place_region(groups, blocks, coefs, 3 * SUB, store)
-    clear_tail(region, 3 * slab)
+    place_region(groups, blocks, coefs, 3 * SUB, region, store)
     result[...] = jnp.zeros_like(result)
     values = parts_of(region[...])
     half = tiles * SUB
@@ -378,20 +384,23 @@
 
     far_fields(left, right, keep)
 
-    def slot(d, carry):
+    def slot(first, slopes, d, carry):
+        at = first + d
         for g in range(width // SUB):
             total = [jnp.zeros((SUB, LANES), jnp.float32) for _ in range(3)]
             for t in range(tiles):
                 ex, ey, ez = [slopes[a, d, g, t] for a in range(3)]
-                xx, yy, zz, xy, xz, yz = [far_row(far_coef, n, tiles, d, t) for n in range(6)]
+                xx, yy, zz, xy, xz, yz = [far_row(far_coef, n, tiles, at, t) for n in range(6)]
                 total[0] += xx * ex + xy * ey + xz * ez
                 total[1] += xy * ex + yy * ey + yz * ez
                 total[2] += xz * ex + yz * ey + zz * ez
             for n in range(3):
-                put(result, g, n * blocks + d, total[n])
+                put(result, g, n * blocks + at, total[n])
         return carry
 
-    lax.fori_loop(0, blocks, slot, 0)
+    for n, (first, count) in enumerate(spans):
+        lax.fori_loop(0, count, functools.partial(slot, first, pieces[2 * n + 1]), 0)
+    moments = [sum(pieces[2 * n][m] for n in range(len(spans))) for m in range(9)]
     sums = jnp.transpose(result[...])
     field = lambda n: own_rows[n, :, 0:width]
     live = jnp.where(lane_iota()[:, 0:width].astype(jnp.float32) < field(10), 1.0, 0.0)
@@ -420,11 +429,16 @@
         seg.append(lax.ppermute(own, "seg", [(i, i ^ k) for i in range(groups)]))
     whole = jnp.concatenate([part[:send_rows] for part in seg], axis=0)
     first = [(i, i ^ 1) for i in range(ranges)]
-    second = [(i, ((i + 1) ^ 1) - 1) for i in range(1, ranges - 1)]
-    return seg + [lax.ppermute(whole, "dom", first), lax.ppermute(whole, "dom", second)]
-
-
-def local(state, counts, neighbours, new_place):
+    second = []
+    for r in range(ranges):
+        for s in range(groups):
+            inside = 0 < r < ranges - 1
+            other = (((r + 1) ^ 1) - 1) * groups + s if inside else r * groups + (s ^ 1)
+            second.append((r * groups + s, other))
+    return seg + [lax.ppermute(whole, "dom", first), lax.ppermute(whole, ("dom", "seg"), second)]
+
+
+def step(state, counts, neighbours, new_place):
     blocks, fields, width = state.shape
     nbr = neighbours.shape[1]
     groups = lax.axis_size("seg")
@@ -448,8 +462,10 @@
             SMEM((blocks,), i32),
             pltpu.SemaphoreType.DMA((4,)),
         ),
-        name="pack",
-    )(counts, new_place, jnp.swapaxes(state, 0, 1), neighbours)
+    )(*[
+        pltpu.with_memory_space_constraint(value, pltpu.HBM)
+        for value in (counts, new_place, jnp.swapaxes(state, 0, 1), neighbours)
+    ])
     parts = exchange(packed, 5 * SUB)
     vol, rho, far, cols, own_rows, meta, hot, dist = call(
         functools.partial(density_body, groups, blocks, width, tiles),
@@ -472,7 +488,6 @@
             columns,
             columns,
         ),
-        name="density",
     )(*parts)
     vols = exchange(vol, SUB)
     factor, placed = call(
@@ -481,7 +496,6 @@
         in_specs=[vm] * 5,
         out_specs=(vm, vm),
         scratch=(columns,),
-        name="factor",
     )(far, cols, meta, hot, dist)
     coef, corr = call(
         functools.partial(tensor_body, groups, blocks, width, tiles),
@@ -489,35 +503,36 @@
         in_specs=[vm] * (6 + groups + 2),
         out_specs=(vm, vm),
         scratch=(columns, VMEM((size, LANES), f32), VMEM((tiles * SUB, LANES), f32), columns),
-        name="tensor",
     )(far, cols, own_rows, factor, placed, rho, *vols)
     coefs = exchange(coef, 3 * SUB)
-    moments, slopes = call(
-        functools.partial(moment_body, blocks, width, tiles),
-        (shape(9, blocks, width), shape(3, *many)),
-        in_specs=[vm] * 3,
-        out_specs=(vm, vm),
-        scratch=(columns, columns),
-        name="moments",
-    )(far, cols, factor)
+    ends = [blocks * n // SUB for n in (0,) + SPLIT]
+    spans = [(low, high - low) for low, high in zip(ends, ends[1:])]
+    pieces = []
+    for first_slot, count in spans:
+        pieces += call(
+            functools.partial(moment_body, first_slot, count, blocks, width, tiles),
+            (shape(9, blocks, width), shape(3, count, *many[1:])),
+            in_specs=[vm] * 3,
+            out_specs=(vm, vm),
+            scratch=(columns, columns),
+        )(far, cols, factor)
     moved = call(
-        functools.partial(update_body, groups, blocks, width, tiles),
+        functools.partial(update_body, spans, groups, blocks, width, tiles),
         shape(fields, blocks, width),
-        in_specs=[vm] * (5 + groups + 2),
+        in_specs=[vm] * (3 + len(pieces) + groups + 2),
         out_specs=vm,
         scratch=(
             VMEM((size, 3 * LANES), f32),
             VMEM((6 * tiles * SUB, LANES), f32),
             columns,
         ),
-        name="update",
-    )(own_rows, slopes, placed, corr, moments, *coefs)
+    )(own_rows, placed, corr, *pieces, *coefs)
     return (jnp.swapaxes(moved, 0, 1), rho)
 
 
 def solution(mesh):
     return jax.shard_map(
-        local,
+        step,
         mesh=mesh,
         in_specs=(
             P(("dom", "seg"), None, None),

time: 62.4 us -> 55.4 us (0.89)
  starting transfers between devices: 23.3 us -> 17.8 us
  local copies, waits for them, and re-layouts: 2.79 us -> 0.03 us
  Pallas kernels: 25.7 us -> 26.4 us
    ppermute x3, starting transfers between devices: 12.1 us -> 2.44 us  [exchange(): lax.ppermute(whole, ('dom', 'seg'), second)]
    ppermute x3, starting transfers between devices: 2.46 us -> 6.65 us  [exchange(): lax.ppermute(whole, 'dom', first)]
    unnamed x16 -> x8, local copies, waits for them, and re-layouts: 2.77 us -> 0.02 us
    pallas_call x6 -> x8, Pallas kernels: 25.7 us -> 26.4 us  [the longest x3 7.39 us: step(): call(functools.partial(moment_body, first_slot, count, blocks, width, til...]
  transfers between devices with their start and end apart: 15 -> 15, of which waited for: 7 -> 8; matrix products, arithmetic and copies ran while one was open for 0% -> 0% of each run, Pallas kernels for 15% -> 18%
where the time goes in v4:
time: 55.4 us; the launch traced here: 55 us
  Pallas kernels  26.4 us (48%)
  starting transfers between devices  17.8 us (32%)
  waiting for transfers between devices  10 us (18%)
  between operations  0.71 us (1%)
    ppermute x9, starting transfers between devices, exchange(): seg.append(lax.ppermute(own, 'seg', [(i, i ^ k) for i in range(groups)]))  8.72 us
    pallas_call x3, Pallas kernels, step(): call(functools.partial(moment_body, first_slot, count, blocks, width, til...  7.39 us
    ppermute x9, waiting for transfers between devices, exchange(): seg.append(lax.ppermute(own, 'seg', [(i, i ^ k) for i in range(groups)]))  6.95 us
    ppermute x3, starting transfers between devices, exchange(): lax.ppermute(whole, 'dom', first)  6.65 us
    pallas_call x1, Pallas kernels, step(): call(functools.partial(density_body, groups, blocks, width, tiles), (shap...  5.76 us
    pallas_call x1, Pallas kernels, step(): call(functools.partial(tensor_body, groups, blocks, width, tiles), (shape...  5.06 us
    pallas_call x1, Pallas kernels, step(): call(functools.partial(update_body, spans, groups, blocks, width, tiles),...  4.75 us
    ppermute x3, waiting for transfers between devices, exchange(): lax.ppermute(whole, ('dom', 'seg'), second)  3.07 us
  transfers between devices with their start and end apart: 15, of which 8 were waited for; matrix products, arithmetic and copies ran while one was open for 0% of the time, Pallas kernels for 18%

profile of v4, /device:TPU:1, one launch (start us, length us, event | category | flops | bytes accessed | tf_op | source)
XLA Modules:
  0.0 55.0 jit_solution(6677496415946794149)
XLA Ops:
  0.6 0.9 %shard_map.59.refs_0_ = f32[48,128]{1,0:T(8,128)S(1)} custom-call(s32[8]{0:T(128)} %refs_0_.1, s32[8]{0:T(128)} %refs_1_.1, f32[9,8,64]{2,1,0:T(8,128)} %bitcast.3, s32[8,26]{1,0:T(8,128)} %refs_3_.1), custom_call_target="tpu_custom_call" | custom-call | tf_op jit(solution)/shard_map/pallas_call | solution.py:453
  1.6 3.0 %collective-permute-start.2 = (f32[48,128]{1,0:T(8,128)S(1)}, f32[48,128]{1,0:T(8,128)S(1)}, u32[]{:S(2)}, u32[]{:S(2)}) collective-permute-start(f32[48,128]{1,0:T(8,128)S(1)} %shard_map.59.refs_0_), channel_id=1, source_target_pairs={{0,3},{1,2},{2,1},{3,0},{4,7},{5,6},{6,5},{7,4},{8,11},{9,10},{10,... | collective-permute-start | bytes 73736 | tf_op jit(solution)/shard_map/ppermute | solution.py:429
  4.6 0.2 collective-permute-start.1
  4.8 0.1 collective-permute-start
  5.0 0.9 %collective-permute-done.2.refs_3_ = f32[48,128]{1,0:T(8,128)S(1)} collective-permute-done((f32[48,128]{1,0:T(8,128)S(1)}, f32[48,128]{1,0:T(8,128)S(1)}, u32[]{:S(2)}, u32[]{:S(2)}) %collective-permute-start.2) | collective-permute-done | bytes 24608 | tf_op jit(solution)/shard_map/ppermute | solution.py:429
  5.8 1.5 %collective-permute-done.1.refs_2_ = f32[48,128]{1,0:T(8,128)S(1)} collective-permute-done((f32[48,128]{1,0:T(8,128)S(1)}, f32[48,128]{1,0:T(8,128)S(1)}, u32[]{:S(2)}, u32[]{:S(2)}) %collective-permute-start.1) | collective-permute-done | bytes 24608 | tf_op jit(solution)/shard_map/ppermute | solution.py:429
  7.3 0.2 collective-permute-done.refs_1_
  7.5 2.5 %collective-permute-start.3 = (f32[160,128]{1,0:T(8,128)S(1)}, f32[160,128]{1,0:T(8,128)S(1)}, u32[]{:S(2)}, u32[]{:S(2)}) collective-permute-start(f32[160,128]{1,0:T(8,128)S(1)} %pad_maximum_fusion), channel_id=1, source_target_pairs={{0,4},{4,0},{8,12},{12,8},{16,20},{20,16},{24,28},{28,24},{1,5},{5... | collective-permute-start | bytes 245768 | tf_op jit(solution)/shard_map/ppermute | solution.py:438
  10.0 1.3 %collective-permute-start.4 = (f32[160,128]{1,0:T(8,128)S(1)}, f32[160,128]{1,0:T(8,128)S(1)}, u32[]{:S(2)}, u32[]{:S(2)}) collective-permute-start(f32[160,128]{1,0:T(8,128)S(1)} %pad_maximum_fusion), channel_id=1, source_target_pairs={{0,1},{1,0},{2,3},{3,2},{4,8},{5,9},{6,10},{7,11},{8,4},{9,5},{10,... | collective-permute-start | bytes 245768 | tf_op jit(solution)/shard_map/ppermute | solution.py:438
  11.2 2.9 %collective-permute-done.4.refs_5_ = f32[160,128]{1,0:T(8,128)S(1)} collective-permute-done((f32[160,128]{1,0:T(8,128)S(1)}, f32[160,128]{1,0:T(8,128)S(1)}, u32[]{:S(2)}, u32[]{:S(2)}) %collective-permute-start.4) | collective-permute-done | bytes 81952 | tf_op jit(solution)/shard_map/ppermute | solution.py:438
  14.1 5.8 %shard_map.60 = (f32[8,128]{1,0:T(8,128)S(1)}, f32[8,64]{1,0:T(8,128)}, f32[896,128]{1,0:T(8,128)S(1)}, f32[64,128]{1,0:T(8,128)S(1)}, f32[11,8,128]{2,1,0:T(8,1...) custom-call(f32[48,128]{1,0:T(8,128)S(1)} %shard_map.59.refs_0_, ...), custom_call_target="tpu_custom_call" | custom-call | tf_op jit(solution)/shard_map/pallas_call | solution.py:470
  19.9 1.5 %collective-permute-start.6 = (f32[8,128]{1,0:T(8,128)S(1)}, f32[8,128]{1,0:T(8,128)S(1)}, u32[]{:S(2)}, u32[]{:S(2)}) collective-permute-start(f32[8,128]{1,0:T(8,128)S(1)} %get-tuple-element.29.refs_6_), channel_id=1, source_target_pairs={{0,2},{1,3},{2,0},{3,1},{4,6},{5,7},{6,4},{7,5},{8,10},{9,11},{10,... | collective-permute-start | bytes 12296 | tf_op jit(solution)/shard_map/ppermute | solution.py:429
  21.4 1.2 %collective-permute-start.7 = (f32[8,128]{1,0:T(8,128)S(1)}, f32[8,128]{1,0:T(8,128)S(1)}, u32[]{:S(2)}, u32[]{:S(2)}) collective-permute-start(f32[8,128]{1,0:T(8,128)S(1)} %get-tuple-element.29.refs_6_), channel_id=1, source_target_pairs={{0,3},{1,2},{2,1},{3,0},{4,7},{5,6},{6,5},{7,4},{8,11},{9,10},{10,... | collective-permute-start | bytes 12296 | tf_op jit(solution)/shard_map/ppermute | solution.py:429
  22.5 2.2 %collective-permute-done.7.refs_9_ = f32[8,128]{1,0:T(8,128)S(1)} collective-permute-done((f32[8,128]{1,0:T(8,128)S(1)}, f32[8,128]{1,0:T(8,128)S(1)}, u32[]{:S(2)}, u32[]{:S(2)}) %collective-permute-start.7) | collective-permute-done | bytes 4128 | tf_op jit(solution)/shard_map/ppermute | solution.py:429
  24.7 2.1 %collective-permute-start.8 = (f32[32,128]{1,0:T(8,128)S(1)}, f32[32,128]{1,0:T(8,128)S(1)}, u32[]{:S(2)}, u32[]{:S(2)}) collective-permute-start(f32[32,128]{1,0:T(8,128)S(1)} %constant_dynamic-update-slice_fusion), channel_id=1, source_target_pairs={{0,4},{4,0},{8,12},{12,8},{16,20},{20,16},{24,28},{28,24},{1,5},{5... | collective-permute-start | bytes 49160 | tf_op jit(solution)/shard_map/ppermute | solution.py:438
  26.8 0.6 %collective-permute-start.9 = (f32[32,128]{1,0:T(8,128)S(1)}, f32[32,128]{1,0:T(8,128)S(1)}, u32[]{:S(2)}, u32[]{:S(2)}) collective-permute-start(f32[32,128]{1,0:T(8,128)S(1)} %constant_dynamic-update-slice_fusion), channel_id=1, source_target_pairs={{0,1},{1,0},{2,3},{3,2},{4,8},{5,9},{6,10},{7,11},{8,4},{9,5},{10,... | collective-permute-start | bytes 49160 | tf_op jit(solution)/shard_map/ppermute | solution.py:438
  27.4 2.5 %shard_map.61 = (f32[8,8,14,8,128]{4,3,2,1,0:T(8,128)S(1)}, f32[224,128]{1,0:T(8,128)S(1)}) custom-call(f32[896,128]{1,0:T(8,128)S(1)} %get-tuple-element.21.far.refs_0_, f32[64,128]{1,0:T(8,128)S(1)} %get-tuple-element.22.cols.refs_1_, f32[128,128]{1,0:T(8,128)S(1)} %get-tuple-element.23.meta, f32[224,128]{1,0:T(8,128)S(1)} %get-tuple-element.24.hot, ...), custom_call_target="tpu_custom_call" | custom-call | tf_op jit(solution)/shard_map/pallas_call | solution.py:493
  30.0 0.0 collective-permute-done.8.refs_10_
  30.0 0.2 collective-permute-done.9.refs_11_
  30.2 5.1 %shard_map.62 = (f32[24,128]{1,0:T(8,128)S(1)}, f32[7,8,64]{2,1,0:T(8,128)S(1)}) custom-call(f32[896,128]{1,0:T(8,128)S(1)} %get-tuple-element.21.far.refs_0_, f32[64,128]{1,0:T(8,128)S(1)} %get-tuple-element.22.cols.refs_1_, f32[11,8,128]{2,1,0:T(8,128)S(1)} %get-tuple-element.20.refs_2_.refs_0_, ...), custom_call_target="tpu_custom_call" | custom-call | tf_op jit(solution)/shard_map/pallas_call | solution.py:500
  35.2 1.2 %collective-permute-start.10 = (f32[24,128]{1,0:T(8,128)S(1)}, f32[24,128]{1,0:T(8,128)S(1)}, u32[]{:S(2)}, u32[]{:S(2)}) collective-permute-start(f32[24,128]{1,0:T(8,128)S(1)} %get-tuple-element.37.refs_9_), channel_id=1, source_target_pairs={{0,1},{1,0},{2,3},{3,2},{4,5},{5,4},{6,7},{7,6},{8,9},{9,8},{10,11... | collective-permute-start | bytes 36872 | tf_op jit(solution)/shard_map/ppermute | solution.py:429
  36.5 0.2 collective-permute-start.11
  36.7 1.2 %collective-permute-start.12 = (f32[24,128]{1,0:T(8,128)S(1)}, f32[24,128]{1,0:T(8,128)S(1)}, u32[]{:S(2)}, u32[]{:S(2)}) collective-permute-start(f32[24,128]{1,0:T(8,128)S(1)} %get-tuple-element.37.refs_9_), channel_id=1, source_target_pairs={{0,3},{1,2},{2,1},{3,0},{4,7},{5,6},{6,5},{7,4},{8,11},{9,10},{10,... | collective-permute-start | bytes 36872 | tf_op jit(solution)/shard_map/ppermute | solution.py:429
  37.9 1.4 %collective-permute-done.11.refs_11_ = f32[24,128]{1,0:T(8,128)S(1)} collective-permute-done((f32[24,128]{1,0:T(8,128)S(1)}, f32[24,128]{1,0:T(8,128)S(1)}, u32[]{:S(2)}, u32[]{:S(2)}) %collective-permute-start.11) | collective-permute-done | bytes 12320 | tf_op jit(solution)/shard_map/ppermute | solution.py:429
  39.3 0.9 %collective-permute-done.12.refs_12_ = f32[24,128]{1,0:T(8,128)S(1)} collective-permute-done((f32[24,128]{1,0:T(8,128)S(1)}, f32[24,128]{1,0:T(8,128)S(1)}, u32[]{:S(2)}, u32[]{:S(2)}) %collective-permute-start.12) | collective-permute-done | bytes 12320 | tf_op jit(solution)/shard_map/ppermute | solution.py:429
  40.1 2.1 %collective-permute-start.13 = (f32[96,128]{1,0:T(8,128)S(1)}, f32[96,128]{1,0:T(8,128)S(1)}, u32[]{:S(2)}, u32[]{:S(2)}) collective-permute-start(f32[96,128]{1,0:T(8,128)S(1)} %constant_dynamic-update-slice_fusion.4), channel_id=1, source_target_pairs={{0,4},{4,0},{8,12},{12,8},{16,20},{20,16},{24,28},{28,24},{1,5},{5... | collective-permute-start | bytes 147464 | tf_op jit(solution)/shard_map/ppermute | solution.py:438
  42.2 0.6 %collective-permute-start.14 = (f32[96,128]{1,0:T(8,128)S(1)}, f32[96,128]{1,0:T(8,128)S(1)}, u32[]{:S(2)}, u32[]{:S(2)}) collective-permute-start(f32[96,128]{1,0:T(8,128)S(1)} %constant_dynamic-update-slice_fusion.4), channel_id=1, source_target_pairs={{0,1},{1,0},{2,3},{3,2},{4,8},{5,9},{6,10},{7,11},{8,4},{9,5},{10,... | collective-permute-start | bytes 147464 | tf_op jit(solution)/shard_map/ppermute | solution.py:438
  42.8 1.9 %shard_map.63 = (f32[9,8,64]{2,1,0:T(8,128)S(1)}, f32[3,2,8,14,8,128]{5,4,3,2,1,0:T(8,128)S(1)}) custom-call(f32[896,128]{1,0:T(8,128)S(1)} %get-tuple-element.21.far.refs_0_, f32[64,128]{1,0:T(8,128)S(1)} %get-tuple-element.22.cols.refs_1_, f32[8,8,14,8,128]{4,3,2,1,0:T(8,128)S(1)} %get-tuple-element.27.refs_3_.factor), custom_call_target="tpu_custom_call" | custom-call | tf_op jit(solution)/shard_map/pallas_call | solution.py:512
  44.7 3.7 %shard_map.64 = (f32[9,8,64]{2,1,0:T(8,128)S(1)}, f32[3,4,8,14,8,128]{5,4,3,2,1,0:T(8,128)S(1)}) custom-call(f32[896,128]{1,0:T(8,128)S(1)} %get-tuple-element.21.far.refs_0_, f32[64,128]{1,0:T(8,128)S(1)} %get-tuple-element.22.cols.refs_1_, f32[8,8,14,8,128]{4,3,2,1,0:T(8,128)S(1)} %get-tuple-element.27.refs_3_.factor), custom_call_target="tpu_custom_call" | custom-call | tf_op jit(solution)/shard_map/pallas_call | solution.py:512
  48.3 1.9 %shard_map.65 = (f32[9,8,64]{2,1,0:T(8,128)S(1)}, f32[3,2,8,14,8,128]{5,4,3,2,1,0:T(8,128)S(1)}) custom-call(f32[896,128]{1,0:T(8,128)S(1)} %get-tuple-element.21.far.refs_0_, f32[64,128]{1,0:T(8,128)S(1)} %get-tuple-element.22.cols.refs_1_, f32[8,8,14,8,128]{4,3,2,1,0:T(8,128)S(1)} %get-tuple-element.27.refs_3_.factor), custom_call_target="tpu_custom_call" | custom-call | tf_op jit(solution)/shard_map/pallas_call | solution.py:512
  50.2 0.0 collective-permute-done.13.refs_13_
  50.2 4.7 %shard_map.66 = f32[9,8,64]{2,1,0:T(8,128)} custom-call(f32[11,8,128]{2,1,0:T(8,128)S(1)} %get-tuple-element.20.refs_2_.refs_0_, f32[224,128]{1,0:T(8,128)S(1)} %get-tuple-element.26.refs_4_.refs_1_, f32[7,8,64]{2,1,0:T(8,128)S(1)} %get-tuple-element.30.refs_2_, f32[9,8,64]{2,1,0:T(8,128)S(1)} %get-tuple-element.31.refs_3_, ...), custom_call_target="tpu_custom_call" | custom-call | tf_op jit(solution)/shard_map/pallas_call | solution.py:519
  (21 shorter events, 0.1 us)
Async XLA Ops:
  1.6 4.3 %collective-permute-start.2 = (f32[48,128]{1,0:T(8,128)S(1)}, f32[48,128]{1,0:T(8,128)S(1)}, u32[]{:S(2)}, u32[]{:S(2)}) collective-permute-start(f32[48,128]{1,0:T(8,128)S(1)} %shard_map.59.refs_0_), channel_id=1, source_target_pairs={{0,3},{1,2},{2,1},{3,0},{4,7},{5,6},{6,5},{7,4},{8,11},{9,10},{10,... | collective-permute-start | bytes 73736 | tf_op jit(solution)/shard_map/ppermute | solution.py:429
  4.6 2.7 %collective-permute-start.1 = (f32[48,128]{1,0:T(8,128)S(1)}, f32[48,128]{1,0:T(8,128)S(1)}, u32[]{:S(2)}, u32[]{:S(2)}) collective-permute-start(f32[48,128]{1,0:T(8,128)S(1)} %shard_map.59.refs_0_), channel_id=1, source_target_pairs={{0,2},{1,3},{2,0},{3,1},{4,6},{5,7},{6,4},{7,5},{8,10},{9,11},{10,... | collective-permute-start | bytes 73736 | tf_op jit(solution)/shard_map/ppermute | solution.py:429
  4.8 2.7 %collective-permute-start = (f32[48,128]{1,0:T(8,128)S(1)}, f32[48,128]{1,0:T(8,128)S(1)}, u32[]{:S(2)}, u32[]{:S(2)}) collective-permute-start(f32[48,128]{1,0:T(8,128)S(1)} %shard_map.59.refs_0_), channel_id=1, source_target_pairs={{0,1},{1,0},{2,3},{3,2},{4,5},{5,4},{6,7},{7,6},{8,9},{9,8},{10,11... | collective-permute-start | bytes 73736 | tf_op jit(solution)/shard_map/ppermute | solution.py:429
  7.5 3.7 %collective-permute-start.3 = (f32[160,128]{1,0:T(8,128)S(1)}, f32[160,128]{1,0:T(8,128)S(1)}, u32[]{:S(2)}, u32[]{:S(2)}) collective-permute-start(f32[160,128]{1,0:T(8,128)S(1)} %pad_maximum_fusion), channel_id=1, source_target_pairs={{0,4},{4,0},{8,12},{12,8},{16,20},{20,16},{24,28},{28,24},{1,5},{5... | collective-permute-start | bytes 245768 | tf_op jit(solution)/shard_map/ppermute | solution.py:438
  10.0 4.1 %collective-permute-start.4 = (f32[160,128]{1,0:T(8,128)S(1)}, f32[160,128]{1,0:T(8,128)S(1)}, u32[]{:S(2)}, u32[]{:S(2)}) collective-permute-start(f32[160,128]{1,0:T(8,128)S(1)} %pad_maximum_fusion), channel_id=1, source_target_pairs={{0,1},{1,0},{2,3},{3,2},{4,8},{5,9},{6,10},{7,11},{8,4},{9,5},{10,... | collective-permute-start | bytes 245768 | tf_op jit(solution)/shard_map/ppermute | solution.py:438
  19.9 10.3 %copy-start = (f32[8,64]{1,0:T(8,128)S(1)}, f32[8,64]{1,0:T(8,128)}, u32[]{:S(2)}) copy-start(f32[8,64]{1,0:T(8,128)} %get-tuple-element.19.refs_5_) | copy-start | bytes 6148
  19.9 2.7 %collective-permute-start.5 = (f32[8,128]{1,0:T(8,128)S(1)}, f32[8,128]{1,0:T(8,128)S(1)}, u32[]{:S(2)}, u32[]{:S(2)}) collective-permute-start(f32[8,128]{1,0:T(8,128)S(1)} %get-tuple-element.29.refs_6_), channel_id=1, source_target_pairs={{0,1},{1,0},{2,3},{3,2},{4,5},{5,4},{6,7},{7,6},{8,9},{9,8},{10,11... | collective-permute-start | bytes 12296 | tf_op jit(solution)/shard_map/ppermute | solution.py:429
  19.9 2.7 %collective-permute-start.6 = (f32[8,128]{1,0:T(8,128)S(1)}, f32[8,128]{1,0:T(8,128)S(1)}, u32[]{:S(2)}, u32[]{:S(2)}) collective-permute-start(f32[8,128]{1,0:T(8,128)S(1)} %get-tuple-element.29.refs_6_), channel_id=1, source_target_pairs={{0,2},{1,3},{2,0},{3,1},{4,6},{5,7},{6,4},{7,5},{8,10},{9,11},{10,... | collective-permute-start | bytes 12296 | tf_op jit(solution)/shard_map/ppermute | solution.py:429
  21.4 3.4 %collective-permute-start.7 = (f32[8,128]{1,0:T(8,128)S(1)}, f32[8,128]{1,0:T(8,128)S(1)}, u32[]{:S(2)}, u32[]{:S(2)}) collective-permute-start(f32[8,128]{1,0:T(8,128)S(1)} %get-tuple-element.29.refs_6_), channel_id=1, source_target_pairs={{0,3},{1,2},{2,1},{3,0},{4,7},{5,6},{6,5},{7,4},{8,11},{9,10},{10,... | collective-permute-start | bytes 12296 | tf_op jit(solution)/shard_map/ppermute | solution.py:429
  24.7 5.2 %collective-permute-start.8 = (f32[32,128]{1,0:T(8,128)S(1)}, f32[32,128]{1,0:T(8,128)S(1)}, u32[]{:S(2)}, u32[]{:S(2)}) collective-permute-start(f32[32,128]{1,0:T(8,128)S(1)} %constant_dynamic-update-slice_fusion), channel_id=1, source_target_pairs={{0,4},{4,0},{8,12},{12,8},{16,20},{20,16},{24,28},{28,24},{1,5},{5... | collective-permute-start | bytes 49160 | tf_op jit(solution)/shard_map/ppermute | solution.py:438
  26.8 3.3 %collective-permute-start.9 = (f32[32,128]{1,0:T(8,128)S(1)}, f32[32,128]{1,0:T(8,128)S(1)}, u32[]{:S(2)}, u32[]{:S(2)}) collective-permute-start(f32[32,128]{1,0:T(8,128)S(1)} %constant_dynamic-update-slice_fusion), channel_id=1, source_target_pairs={{0,1},{1,0},{2,3},{3,2},{4,8},{5,9},{6,10},{7,11},{8,4},{9,5},{10,... | collective-permute-start | bytes 49160 | tf_op jit(solution)/shard_map/ppermute | solution.py:438
  35.2 2.7 %collective-permute-start.10 = (f32[24,128]{1,0:T(8,128)S(1)}, f32[24,128]{1,0:T(8,128)S(1)}, u32[]{:S(2)}, u32[]{:S(2)}) collective-permute-start(f32[24,128]{1,0:T(8,128)S(1)} %get-tuple-element.37.refs_9_), channel_id=1, source_target_pairs={{0,1},{1,0},{2,3},{3,2},{4,5},{5,4},{6,7},{7,6},{8,9},{9,8},{10,11... | collective-permute-start | bytes 36872 | tf_op jit(solution)/shard_map/ppermute | solution.py:429
  36.5 2.8 %collective-permute-start.11 = (f32[24,128]{1,0:T(8,128)S(1)}, f32[24,128]{1,0:T(8,128)S(1)}, u32[]{:S(2)}, u32[]{:S(2)}) collective-permute-start(f32[24,128]{1,0:T(8,128)S(1)} %get-tuple-element.37.refs_9_), channel_id=1, source_target_pairs={{0,2},{1,3},{2,0},{3,1},{4,6},{5,7},{6,4},{7,5},{8,10},{9,11},{10,... | collective-permute-start | bytes 36872 | tf_op jit(solution)/shard_map/ppermute | solution.py:429
  36.7 3.5 %collective-permute-start.12 = (f32[24,128]{1,0:T(8,128)S(1)}, f32[24,128]{1,0:T(8,128)S(1)}, u32[]{:S(2)}, u32[]{:S(2)}) collective-permute-start(f32[24,128]{1,0:T(8,128)S(1)} %get-tuple-element.37.refs_9_), channel_id=1, source_target_pairs={{0,3},{1,2},{2,1},{3,0},{4,7},{5,6},{6,5},{7,4},{8,11},{9,10},{10,... | collective-permute-start | bytes 36872 | tf_op jit(solution)/shard_map/ppermute | solution.py:429
  40.1 10.1 %collective-permute-start.13 = (f32[96,128]{1,0:T(8,128)S(1)}, f32[96,128]{1,0:T(8,128)S(1)}, u32[]{:S(2)}, u32[]{:S(2)}) collective-permute-start(f32[96,128]{1,0:T(8,128)S(1)} %constant_dynamic-update-slice_fusion.4), channel_id=1, source_target_pairs={{0,4},{4,0},{8,12},{12,8},{16,20},{20,16},{24,28},{28,24},{1,5},{5... | collective-permute-start | bytes 147464 | tf_op jit(solution)/shard_map/ppermute | solution.py:438
  42.2 8.0 %collective-permute-start.14 = (f32[96,128]{1,0:T(8,128)S(1)}, f32[96,128]{1,0:T(8,128)S(1)}, u32[]{:S(2)}, u32[]{:S(2)}) collective-permute-start(f32[96,128]{1,0:T(8,128)S(1)} %constant_dynamic-update-slice_fusion.4), channel_id=1, source_target_pairs={{0,1},{1,0},{2,3},{3,2},{4,8},{5,9},{6,10},{7,11},{8,4},{9,5},{10,... | collective-permute-start | bytes 147464 | tf_op jit(solution)/shard_map/ppermute | solution.py:438

commit v5 on v4

--- a/solution.py
+++ b/solution.py
@@ -14,7 +14,8 @@
 STEP_DT = 0.1
 SLOPE = -5.0 * SIGMA * 32.0
 TINY = 1e-37
-SPLIT = (2, 6, 8)
+FACTOR_SPLIT = (5, 8)
+MOMENT_SPLIT = (5, 8)
 SUB = 8
 LANES = 128
 X, SMOOTH, MASS, VEL = 0, 3, 4, 5
@@ -140,32 +141,36 @@
     return jnp.broadcast_to(value[:, at : at + 1], (SUB, LANES))
 
 
-def own_columns(cols, turned, d):
-    turned[...] = pltpu.roll(cols[...], lax.rem(LANES - d, LANES), axis=1)
-
-
 def group_rows(g):
     return slice(g * SUB, (g + 1) * SUB)
 
 
-def put(result, g, slot, value):
-    rows = group_rows(g)
-    total = jnp.sum(value, axis=1, keepdims=True)
-    result[rows, :] = jnp.where(lane_iota() == slot, total, result[rows, :])
-
-
 def far_row(ref, field, tiles, d, t):
     return jnp.broadcast_to(ref[pl.ds((field * tiles + t) * SUB + d, 1), :], (SUB, LANES))
 
 
-def each_slot(first, count, width, cols, turned, group):
-    def slot(d, carry):
-        own_columns(cols, turned, first + d)
+def each_slot(first, count, blocks, width, cols, result, group):
+    together = 2 if count % 2 == 0 else 1
+    lane = lane_iota()
+
+    def body(step, carry):
+        found = [[] for _ in range(width // SUB)]
+        for n in range(together):
+            d = step * together + n
+            at = first + d
+            own = pltpu.roll(cols[...], lax.rem(LANES - at, LANES), axis=1)
+            for g in range(width // SUB):
+                for m, value in enumerate(group(d, at, g, own[group_rows(g), :])):
+                    found[g].append((m * blocks + at, jnp.sum(value, axis=1, keepdims=True)))
         for g in range(width // SUB):
-            group(d, g, turned[group_rows(g), :])
+            if found[g]:
+                rows = result[group_rows(g), :]
+                for at, total in found[g]:
+                    rows = jnp.where(lane == at, total, rows)
+                result[group_rows(g), :] = rows
         return carry
 
-    lax.fori_loop(0, count, slot, 0)
+    lax.fori_loop(0, count // together, body, 0)
 
 
 def sums_of(result, n, blocks, width):
@@ -175,7 +180,7 @@
 def density_body(groups, blocks, width, tiles, *refs):
     parts = refs[: groups + 2]
     vol_out, rho_out, far, cols, own_rows, meta, hot, dist_out = refs[groups + 2 : groups + 10]
-    region, own_range, own_tiles, turned, result = refs[groups + 10 :]
+    region, own_range, own_tiles, result = refs[groups + 10 :]
     slab = groups * blocks
     me = lax.axis_index("seg")
     kept = parts[groups].shape[0] // groups
@@ -229,7 +234,7 @@
 
     far_fields(left, right, keep)
 
-    def group(d, g, own):
+    def group(d, at, g, own):
         pos = [column(own, X + a) for a in range(3)]
         scale = 0.5 / column(own, SMOOTH)
         total = jnp.zeros((SUB, LANES), jnp.float32)
@@ -243,9 +248,9 @@
             shell = shell * shell
             shell = shell * shell
             total += shell * (far_row(far, MASS, tiles, d, t) * (0.25 + ratio))
-        put(result, g, d, total)
-
-    each_slot(0, blocks, width, cols, turned, group)
+        return [total]
+
+    each_slot(0, blocks, blocks, width, cols, result, group)
     sums = sums_of(result, 0, blocks, width)
     smooth, mass, count = [own_rows[n, :, 0:width] for n in (SMOOTH, MASS, 10)]
     live = jnp.where(lane_iota()[:, 0:width].astype(jnp.float32) < count, 1.0, 0.0)
@@ -255,34 +260,49 @@
     vol_out[...] = jnp.concatenate([vol, vol], axis=1)
 
 
-def factor_body(groups, blocks, width, tiles, far, cols, meta, hot, dist, out, hot_out, turned):
-    slab = groups * blocks
+def placed_lists(slab, tiles, meta, hot):
     size = hot.shape[1]
     spot = meta[:, 2 * tiles : 2 * tiles + 1].astype(jnp.int32)
     rows = lax.broadcasted_iota(jnp.int32, (size, size), 0)
     start = jnp.where(rows < slab, 0, jnp.where(rows < 2 * slab, slab, 2 * slab))
     chosen = start + spot == lax.broadcasted_iota(jnp.int32, (size, size), 1)
     moves = jnp.where(chosen, 1.0, 0.0).astype(jnp.bfloat16)
-    hot_out[...] = jnp.dot(
-        hot[...].astype(jnp.bfloat16), moves, preferred_element_type=jnp.float32
-    )
-
-    def group(d, g, own):
+    return jnp.dot(hot[...].astype(jnp.bfloat16), moves, preferred_element_type=jnp.float32)
+
+
+def factor_body(first, count, blocks, slab, width, tiles, *refs):
+    far, cols, dist = refs[:3]
+    if first == 0:
+        meta, hot = refs[3:5]
+        refs[-1][...] = placed_lists(slab, tiles, meta, hot)
+        slopes, products = refs[5:7]
+    else:
+        slopes, products = refs[3:5]
+
+    def group(d, at, g, own):
+        pos = [column(own, X + a) for a in range(3)]
         smooth = column(own, SMOOTH)
         for t in range(tiles):
-            inv = 1.0 / (smooth + far_row(far, SMOOTH, tiles, d, t))
+            dx, dy, dz = [pos[a] - far_row(far, X + a, tiles, at, t) for a in range(3)]
+            inv = 1.0 / (smooth + far_row(far, SMOOTH, tiles, at, t))
             inv2 = inv * inv
-            part = jnp.maximum(inv - dist[d, g, t] * inv2, 0.0)
-            out[d, g, t] = part * part * part * inv2
-
-    each_slot(0, blocks, width, cols, turned, group)
-
-
-def tensor_body(groups, blocks, width, tiles, *refs):
-    far, cols, own_rows, factor, hot, rho = refs[:6]
-    vols = refs[6 : 8 + groups]
-    coef_out, corr_out = refs[8 + groups : 10 + groups]
-    turned, region, far_vol, result = refs[10 + groups :]
+            part = jnp.maximum(inv - dist[at, g, t] * inv2, 0.0)
+            weight = part * part * part * inv2
+            ex, ey, ez = weight * dx, weight * dy, weight * dz
+            slopes[0, d, g, t], slopes[1, d, g, t], slopes[2, d, g, t] = ex, ey, ez
+            for n, term in enumerate((ex * dx, ey * dy, ez * dz, ex * dy, ex * dz, ey * dz)):
+                products[n, d, g, t] = term
+        return []
+
+    each_slot(first, count, blocks, width, cols, None, group)
+
+
+def tensor_body(spans, groups, blocks, width, tiles, *refs):
+    cols, own_rows, hot, rho = refs[:4]
+    products, refs = refs[4 : 4 + len(spans)], refs[4 + len(spans) :]
+    vols = refs[: 2 + groups]
+    coef_out, corr_out = refs[2 + groups : 4 + groups]
+    region, far_vol, result = refs[4 + groups :]
 
     def store(at, ref, start):
         region[pl.ds(at, SUB), :] = ref[start : start + SUB, :]
@@ -295,19 +315,16 @@
     right = select(hot[half:, :].astype(jnp.bfloat16), values)
     far_vol[...] = jnp.where(lane_iota(half) < HALF, left, right)
 
-    def group(d, g, own):
-        pos = [column(own, X + a) for a in range(3)]
+    def group(product, d, at, g, own):
         total = [jnp.zeros((SUB, LANES), jnp.float32) for _ in range(6)]
         for t in range(tiles):
-            dx, dy, dz = [pos[a] - far_row(far, X + a, tiles, d, t) for a in range(3)]
-            weight = factor[d, g, t] * far_row(far_vol, 0, tiles, d, t)
-            wx, wy, wz = weight * dx, weight * dy, weight * dz
-            for n, term in enumerate((wx * dx, wy * dy, wz * dz, wx * dy, wx * dz, wy * dz)):
-                total[n] += term
-        for n in range(6):
-            put(result, g, n * blocks + d, total[n])
-
-    each_slot(0, blocks, width, cols, turned, group)
+            weight = far_row(far_vol, 0, tiles, at, t)
+            for n in range(6):
+                total[n] += product[n, d, g, t] * weight
+        return total
+
+    for (first, count), product in zip(spans, products):
+        each_slot(first, count, blocks, width, cols, result, functools.partial(group, product))
     sums = jnp.transpose(result[...])
     press = GAMMA_LESS * own_rows[8, :, 0:width] / rho[...]
     scale = own_rows[MASS, :, 0:width] * press
@@ -322,21 +339,16 @@
         coef_out[n * SUB : (n + 1) * SUB, :] = jnp.concatenate(coefs[2 * n : 2 * n + 2], axis=1)
 
 
-def moment_body(first, count, blocks, width, tiles, far, cols, factor, out, slopes, turned, result):
+def moment_body(blocks, width, tiles, spans, far, cols, *refs):
+    slopes, out, result = refs[: len(spans)], refs[-2], refs[-1]
     result[...] = jnp.zeros_like(result)
 
-    def group(d, g, own):
-        at = first + d
-        pos = [column(own, X + a) for a in range(3)]
+    def group(slope, start, d, at, g, own):
         vel = [column(own, VEL + a) for a in range(3)]
         total = [jnp.zeros((SUB, LANES), jnp.float32) for _ in range(9)]
         for t in range(tiles):
-            weight = factor[at, g, t]
             mass = far_row(far, MASS, tiles, at, t)
-            slope = [weight * (pos[a] - far_row(far, X + a, tiles, at, t)) for a in range(3)]
-            for a in range(3):
-                slopes[a, d, g, t] = slope[a]
-            px, py, pz = [mass * slope[a] for a in range(3)]
+            px, py, pz = [mass * slope[a, at - start, g, t] for a in range(3)]
             vx, vy, vz = [vel[a] - far_row(far, VEL + a, tiles, at, t) for a in range(3)]
             terms = (
                 px,
@@ -351,18 +363,19 @@
             )
             for n, term in enumerate(terms):
                 total[n] += term
-        for n in range(9):
-            put(result, g, n * blocks + at, total[n])
-
-    each_slot(first, count, width, cols, turned, group)
+        return total
+
+    for (low, count, start), slope in zip(spans, slopes):
+        each_slot(low, count, blocks, width, cols, result, functools.partial(group, slope, start))
     sums = jnp.transpose(result[...])
     for n in range(9):
         out[n] = sums[n * blocks : (n + 1) * blocks, 0:width]
 
 
-def update_body(spans, groups, blocks, width, tiles, *refs):
-    own_rows, hot, corr = refs[:3]
-    pieces, refs = refs[3 : 3 + 2 * len(spans)], refs[3 + 2 * len(spans) :]
+def update_body(spans, moment_count, groups, blocks, width, tiles, *refs):
+    cols, own_rows, hot, corr = refs[:4]
+    slopes, refs = refs[4 : 4 + len(spans)], refs[4 + len(spans) :]
+    pieces, refs = refs[:moment_count], refs[moment_count:]
     coefs = refs[: 2 + groups]
     state_out = refs[2 + groups]
     region, far_coef, result = refs[3 + groups :]
@@ -384,23 +397,19 @@
 
     far_fields(left, right, keep)
 
-    def slot(first, slopes, d, carry):
-        at = first + d
-        for g in range(width // SUB):
-            total = [jnp.zeros((SUB, LANES), jnp.float32) for _ in range(3)]
-            for t in range(tiles):
-                ex, ey, ez = [slopes[a, d, g, t] for a in range(3)]
-                xx, yy, zz, xy, xz, yz = [far_row(far_coef, n, tiles, at, t) for n in range(6)]
-                total[0] += xx * ex + xy * ey + xz * ez
-                total[1] += xy * ex + yy * ey + yz * ez
-                total[2] += xz * ex + yz * ey + zz * ez
-            for n in range(3):
-                put(result, g, n * blocks + at, total[n])
-        return carry
-
-    for n, (first, count) in enumerate(spans):
-        lax.fori_loop(0, count, functools.partial(slot, first, pieces[2 * n + 1]), 0)
-    moments = [sum(pieces[2 * n][m] for n in range(len(spans))) for m in range(9)]
+    def group(slope, d, at, g, own):
+        total = [jnp.zeros((SUB, LANES), jnp.float32) for _ in range(3)]
+        for t in range(tiles):
+            ex, ey, ez = [slope[a, d, g, t] for a in range(3)]
+            xx, yy, zz, xy, xz, yz = [far_row(far_coef, n, tiles, at, t) for n in range(6)]
+            total[0] += xx * ex + xy * ey + xz * ez
+            total[1] += xy * ex + yy * ey + yz * ez
+            total[2] += xz * ex + yz * ey + zz * ez
+        return total
+
+    for (first, count), slope in zip(spans, slopes):
+        each_slot(first, count, blocks, width, cols, result, functools.partial(group, slope))
+    moments = [sum(piece[m] for piece in pieces) for m in range(9)]
     sums = jnp.transpose(result[...])
     field = lambda n: own_rows[n, :, 0:width]
     live = jnp.where(lane_iota()[:, 0:width].astype(jnp.float32) < field(10), 1.0, 0.0)
@@ -436,6 +445,11 @@
             other = (((r + 1) ^ 1) - 1) * groups + s if inside else r * groups + (s ^ 1)
             second.append((r * groups + s, other))
     return seg + [lax.ppermute(whole, "dom", first), lax.ppermute(whole, ("dom", "seg"), second)]
+
+
+def spans_of(blocks, split):
+    ends = [blocks * n // SUB for n in (0,) + split]
+    return [(low, high - low) for low, high in zip(ends, ends[1:])]
 
 
 def step(state, counts, neighbours, new_place):
@@ -486,47 +500,62 @@
             VMEM((slab, 6 * LANES), f32),
             VMEM((LANES, LANES), f32),
             columns,
-            columns,
         ),
     )(*parts)
     vols = exchange(vol, SUB)
-    factor, placed = call(
-        functools.partial(factor_body, groups, blocks, width, tiles),
-        (shape(*many), shape(2 * tiles * SUB, size)),
-        in_specs=[vm] * 5,
+    spans = spans_of(blocks, FACTOR_SPLIT)
+    slopes, products = [], []
+    for n, (low, count) in enumerate(spans):
+        outs = (shape(3, count, *many[1:]), shape(6, count, *many[1:]))
+        extra = (meta, hot) if n == 0 else ()
+        if n == 0:
+            outs += (shape(2 * tiles * SUB, size),)
+        found = call(
+            functools.partial(factor_body, low, count, blocks, slab, width, tiles),
+            outs,
+            in_specs=[vm] * (3 + len(extra)),
+            out_specs=(vm,) * len(outs),
+        )(far, cols, dist, *extra)
+        slopes.append(found[0])
+        products.append(found[1])
+        if n == 0:
+            placed = found[2]
+    coef, corr = call(
+        functools.partial(tensor_body, spans, groups, blocks, width, tiles),
+        (shape(3 * SUB, LANES), shape(7, blocks, width)),
+        in_specs=[vm] * (4 + len(spans) + groups + 2),
         out_specs=(vm, vm),
-        scratch=(columns,),
-    )(far, cols, meta, hot, dist)
-    coef, corr = call(
-        functools.partial(tensor_body, groups, blocks, width, tiles),
-        (shape(3 * SUB, LANES), shape(7, blocks, width)),
-        in_specs=[vm] * (6 + groups + 2),
-        out_specs=(vm, vm),
-        scratch=(columns, VMEM((size, LANES), f32), VMEM((tiles * SUB, LANES), f32), columns),
-    )(far, cols, own_rows, factor, placed, rho, *vols)
+        scratch=(VMEM((size, LANES), f32), VMEM((tiles * SUB, LANES), f32), columns),
+    )(cols, own_rows, placed, rho, *products, *vols)
     coefs = exchange(coef, 3 * SUB)
-    ends = [blocks * n // SUB for n in (0,) + SPLIT]
-    spans = [(low, high - low) for low, high in zip(ends, ends[1:])]
-    pieces = []
-    for first_slot, count in spans:
-        pieces += call(
-            functools.partial(moment_body, first_slot, count, blocks, width, tiles),
-            (shape(9, blocks, width), shape(3, count, *many[1:])),
-            in_specs=[vm] * 3,
-            out_specs=(vm, vm),
-            scratch=(columns, columns),
-        )(far, cols, factor)
+    moments = []
+    for low, count in spans_of(blocks, MOMENT_SPLIT):
+        parts, used = [], []
+        for (start, length), slope in zip(spans, slopes):
+            begin, end = max(low, start), min(low + count, start + length)
+            if begin < end:
+                parts.append((begin, end - begin, start))
+                used.append(slope)
+        moments.append(
+            call(
+                functools.partial(moment_body, blocks, width, tiles, parts),
+                shape(9, blocks, width),
+                in_specs=[vm] * (2 + len(used)),
+                out_specs=vm,
+                scratch=(columns,),
+            )(far, cols, *used)
+        )
     moved = call(
-        functools.partial(update_body, spans, groups, blocks, width, tiles),
+        functools.partial(update_body, spans, len(moments), groups, blocks, width, tiles),
         shape(fields, blocks, width),
-        in_specs=[vm] * (3 + len(pieces) + groups + 2),
+        in_specs=[vm] * (4 + len(spans) + len(moments) + groups + 2),
         out_specs=vm,
         scratch=(
             VMEM((size, 3 * LANES), f32),
             VMEM((6 * tiles * SUB, LANES), f32),
             columns,
         ),
-    )(own_rows, placed, corr, *pieces, *coefs)
+    )(cols, own_rows, placed, corr, *slopes, *moments, *coefs)
     return (jnp.swapaxes(moved, 0, 1), rho)
 
 

time: 55.4 us -> 51.6 us (0.931)
  Pallas kernels: 26.4 us -> 22.5 us
    pallas_call x6, Pallas kernels: 19.7 us -> 16.5 us  [the longest x2 5.22 us: step(): call(functools.partial(moment_body, blocks, width, tiles, parts), shape(9...]
    ppermute x3, starting transfers between devices: 2.44 us -> 3.48 us  [exchange(): lax.ppermute(whole, ('dom', 'seg'), second)]
    ppermute x3, starting transfers between devices: 6.65 us -> 5.81 us  [exchange(): lax.ppermute(whole, 'dom', first)]
    pallas_call x1, Pallas kernels: 5.76 us -> 5.09 us  [step(): call(functools.partial(density_body, groups, blocks, width, tiles), (shap...]
  transfers between devices with their start and end apart: 15 -> 15, of which waited for: 8 -> 7; matrix products, arithmetic and copies ran while one was open for 0% -> 0% of each run, Pallas kernels for 18% -> 20%
where the time goes in v5:
time: 51.6 us; the launch traced here: 51.1 us
  Pallas kernels  22.5 us (44%)
  starting transfers between devices  18 us (35%)
  waiting for transfers between devices  9.81 us (19%)
  between operations  0.76 us (1%)
    ppermute x9, starting transfers between devices, exchange(): seg.append(lax.ppermute(own, 'seg', [(i, i ^ k) for i in range(groups)]))  8.72 us
    ppermute x9, waiting for transfers between devices, exchange(): seg.append(lax.ppermute(own, 'seg', [(i, i ^ k) for i in range(groups)]))  6.93 us
    ppermute x3, starting transfers between devices, exchange(): lax.ppermute(whole, 'dom', first)  5.81 us
    pallas_call x2, Pallas kernels, step(): call(functools.partial(moment_body, blocks, width, tiles, parts), shape(9...  5.22 us
    pallas_call x1, Pallas kernels, step(): call(functools.partial(density_body, groups, blocks, width, tiles), (shap...  5.09 us
    pallas_call x2, Pallas kernels, step(): call(functools.partial(factor_body, low, count, blocks, slab, width, tile...  4.79 us
    pallas_call x1, Pallas kernels, step(): call(functools.partial(update_body, spans, len(moments), groups, blocks,...  3.99 us
    ppermute x3, starting transfers between devices, exchange(): lax.ppermute(whole, ('dom', 'seg'), second)  3.48 us
  transfers between devices with their start and end apart: 15, of which 7 were waited for; matrix products, arithmetic and copies ran while one was open for 0% of the time, Pallas kernels for 20%

profile of v5, /device:TPU:1, one launch (start us, length us, event | category | flops | bytes accessed | tf_op | source)
XLA Modules:
  0.0 51.1 jit_solution(12939662505944081889)
XLA Ops:
  0.6 0.9 %shard_map.59.refs_0_ = f32[48,128]{1,0:T(8,128)S(1)} custom-call(s32[8]{0:T(128)} %refs_0_.1, s32[8]{0:T(128)} %refs_1_.1, f32[9,8,64]{2,1,0:T(8,128)} %bitcast.3, s32[8,26]{1,0:T(8,128)} %refs_3_.1), custom_call_target="tpu_custom_call" | custom-call | tf_op jit(solution)/shard_map/pallas_call | solution.py:467
  1.6 3.0 %collective-permute-start.2 = (f32[48,128]{1,0:T(8,128)S(1)}, f32[48,128]{1,0:T(8,128)S(1)}, u32[]{:S(2)}, u32[]{:S(2)}) collective-permute-start(f32[48,128]{1,0:T(8,128)S(1)} %shard_map.59.refs_0_), channel_id=1, source_target_pairs={{0,3},{1,2},{2,1},{3,0},{4,7},{5,6},{6,5},{7,4},{8,11},{9,10},{10,... | collective-permute-start | bytes 73736 | tf_op jit(solution)/shard_map/ppermute | solution.py:438
  4.6 0.2 collective-permute-start.1
  4.8 0.1 collective-permute-start
  5.0 0.9 %collective-permute-done.2.refs_3_ = f32[48,128]{1,0:T(8,128)S(1)} collective-permute-done((f32[48,128]{1,0:T(8,128)S(1)}, f32[48,128]{1,0:T(8,128)S(1)}, u32[]{:S(2)}, u32[]{:S(2)}) %collective-permute-start.2) | collective-permute-done | bytes 24608 | tf_op jit(solution)/shard_map/ppermute | solution.py:438
  5.8 1.5 %collective-permute-done.1.refs_2_ = f32[48,128]{1,0:T(8,128)S(1)} collective-permute-done((f32[48,128]{1,0:T(8,128)S(1)}, f32[48,128]{1,0:T(8,128)S(1)}, u32[]{:S(2)}, u32[]{:S(2)}) %collective-permute-start.1) | collective-permute-done | bytes 24608 | tf_op jit(solution)/shard_map/ppermute | solution.py:438
  7.3 0.2 collective-permute-done.refs_1_
  7.5 2.5 %collective-permute-start.3 = (f32[160,128]{1,0:T(8,128)S(1)}, f32[160,128]{1,0:T(8,128)S(1)}, u32[]{:S(2)}, u32[]{:S(2)}) collective-permute-start(f32[160,128]{1,0:T(8,128)S(1)} %pad_maximum_fusion), channel_id=1, source_target_pairs={{0,4},{4,0},{8,12},{12,8},{16,20},{20,16},{24,28},{28,24},{1,5},{5... | collective-permute-start | bytes 245768 | tf_op jit(solution)/shard_map/ppermute | solution.py:447
  10.0 1.3 %collective-permute-start.4 = (f32[160,128]{1,0:T(8,128)S(1)}, f32[160,128]{1,0:T(8,128)S(1)}, u32[]{:S(2)}, u32[]{:S(2)}) collective-permute-start(f32[160,128]{1,0:T(8,128)S(1)} %pad_maximum_fusion), channel_id=1, source_target_pairs={{0,1},{1,0},{2,3},{3,2},{4,8},{5,9},{6,10},{7,11},{8,4},{9,5},{10,... | collective-permute-start | bytes 245768 | tf_op jit(solution)/shard_map/ppermute | solution.py:447
  11.2 2.9 %collective-permute-done.4.refs_5_ = f32[160,128]{1,0:T(8,128)S(1)} collective-permute-done((f32[160,128]{1,0:T(8,128)S(1)}, f32[160,128]{1,0:T(8,128)S(1)}, u32[]{:S(2)}, u32[]{:S(2)}) %collective-permute-start.4) | collective-permute-done | bytes 81952 | tf_op jit(solution)/shard_map/ppermute | solution.py:447
  14.1 5.1 %shard_map.60 = (f32[8,128]{1,0:T(8,128)S(1)}, f32[8,64]{1,0:T(8,128)}, f32[896,128]{1,0:T(8,128)S(1)}, f32[64,128]{1,0:T(8,128)S(1)}, f32[11,8,128]{2,1,0:T(8,1...) custom-call(f32[48,128]{1,0:T(8,128)S(1)} %shard_map.59.refs_0_, ...), custom_call_target="tpu_custom_call" | custom-call | tf_op jit(solution)/shard_map/pallas_call | solution.py:484
  19.2 1.5 %collective-permute-start.6 = (f32[8,128]{1,0:T(8,128)S(1)}, f32[8,128]{1,0:T(8,128)S(1)}, u32[]{:S(2)}, u32[]{:S(2)}) collective-permute-start(f32[8,128]{1,0:T(8,128)S(1)} %get-tuple-element.27.refs_6_), channel_id=1, source_target_pairs={{0,2},{1,3},{2,0},{3,1},{4,6},{5,7},{6,4},{7,5},{8,10},{9,11},{10,... | collective-permute-start | bytes 12296 | tf_op jit(solution)/shard_map/ppermute | solution.py:438
  20.7 1.2 %collective-permute-start.7 = (f32[8,128]{1,0:T(8,128)S(1)}, f32[8,128]{1,0:T(8,128)S(1)}, u32[]{:S(2)}, u32[]{:S(2)}) collective-permute-start(f32[8,128]{1,0:T(8,128)S(1)} %get-tuple-element.27.refs_6_), channel_id=1, source_target_pairs={{0,3},{1,2},{2,1},{3,0},{4,7},{5,6},{6,5},{7,4},{8,11},{9,10},{10,... | collective-permute-start | bytes 12296 | tf_op jit(solution)/shard_map/ppermute | solution.py:438
  21.8 0.0 collective-permute-done.6.refs_8_
  21.9 2.2 %collective-permute-done.7.refs_9_ = f32[8,128]{1,0:T(8,128)S(1)} collective-permute-done((f32[8,128]{1,0:T(8,128)S(1)}, f32[8,128]{1,0:T(8,128)S(1)}, u32[]{:S(2)}, u32[]{:S(2)}) %collective-permute-start.7) | collective-permute-done | bytes 4128 | tf_op jit(solution)/shard_map/ppermute | solution.py:438
  24.0 2.1 %collective-permute-start.8 = (f32[32,128]{1,0:T(8,128)S(1)}, f32[32,128]{1,0:T(8,128)S(1)}, u32[]{:S(2)}, u32[]{:S(2)}) collective-permute-start(f32[32,128]{1,0:T(8,128)S(1)} %constant_dynamic-update-slice_fusion), channel_id=1, source_target_pairs={{0,4},{4,0},{8,12},{12,8},{16,20},{20,16},{24,28},{28,24},{1,5},{5... | collective-permute-start | bytes 49160 | tf_op jit(solution)/shard_map/ppermute | solution.py:447
  26.2 0.6 %collective-permute-start.9 = (f32[32,128]{1,0:T(8,128)S(1)}, f32[32,128]{1,0:T(8,128)S(1)}, u32[]{:S(2)}, u32[]{:S(2)}) collective-permute-start(f32[32,128]{1,0:T(8,128)S(1)} %constant_dynamic-update-slice_fusion), channel_id=1, source_target_pairs={{0,1},{1,0},{2,3},{3,2},{4,8},{5,9},{6,10},{7,11},{8,4},{9,5},{10,... | collective-permute-start | bytes 49160 | tf_op jit(solution)/shard_map/ppermute | solution.py:447
  26.8 1.7 %shard_map.62 = (f32[3,3,8,14,8,128]{5,4,3,2,1,0:T(8,128)S(1)}, f32[6,3,8,14,8,128]{5,4,3,2,1,0:T(8,128)S(1)}) custom-call(f32[896,128]{1,0:T(8,128)S(1)} %get-tuple-element.19.refs_0_.far, f32[64,128]{1,0:T(8,128)S(1)} %get-tuple-element.17.refs_1_.refs_0_.cols, f32[8,8,14,8,128]{4,3,2,1,0:T(8,128)S(1)} %get-tuple-element.20.refs_2_), custom_call_target="tpu_custom_call" | custom-call | tf_op jit(solution)/shard_map/pallas_call | solution.py:513
  28.5 3.1 %shard_map.61 = (f32[3,5,8,14,8,128]{5,4,3,2,1,0:T(8,128)S(1)}, f32[6,5,8,14,8,128]{5,4,3,2,1,0:T(8,128)S(1)}, f32[224,128]{1,0:T(8,128)S(1)}) custom-call(f32[896,128]{1,0:T(8,128)S(1)} %get-tuple-element.19.refs_0_.far, f32[64,128]{1,0:T(8,128)S(1)} %get-tuple-element.17.refs_1_.refs_0_.cols, f32[8,8,14,8,128]{4,3,2,1,0:T(8,128)S(1)} %get-tuple-element.20.refs_2_, ...), custom_call_target="tpu_custom_call" | custom-call | tf_op jit(solution)/shard_map/pallas_call | solution.py:513
  31.6 0.0 collective-permute-done.8.refs_10_
  31.6 2.5 %shard_map.63 = (f32[24,128]{1,0:T(8,128)S(1)}, f32[7,8,64]{2,1,0:T(8,128)S(1)}) custom-call(f32[64,128]{1,0:T(8,128)S(1)} %get-tuple-element.17.refs_1_.refs_0_.cols, f32[11,8,128]{2,1,0:T(8,128)S(1)} %get-tuple-element.18.refs_1_, f32[224,128]{1,0:T(8,128)S(1)} %get-tuple-element.23.refs_2_, f32[8,64]{1,0:T(8,128)S(1)} %copy-done, ...), custom_call_target="tpu_custom_call" | custom-call | tf_op jit(solution)/shard_map/pallas_call | solution.py:523
  34.1 1.2 %collective-permute-start.10 = (f32[24,128]{1,0:T(8,128)S(1)}, f32[24,128]{1,0:T(8,128)S(1)}, u32[]{:S(2)}, u32[]{:S(2)}) collective-permute-start(f32[24,128]{1,0:T(8,128)S(1)} %get-tuple-element.31.refs_8_), channel_id=1, source_target_pairs={{0,1},{1,0},{2,3},{3,2},{4,5},{5,4},{6,7},{7,6},{8,9},{9,8},{10,11... | collective-permute-start | bytes 36872 | tf_op jit(solution)/shard_map/ppermute | solution.py:438
  35.3 0.2 collective-permute-start.11
  35.6 1.2 %collective-permute-start.12 = (f32[24,128]{1,0:T(8,128)S(1)}, f32[24,128]{1,0:T(8,128)S(1)}, u32[]{:S(2)}, u32[]{:S(2)}) collective-permute-start(f32[24,128]{1,0:T(8,128)S(1)} %get-tuple-element.31.refs_8_), channel_id=1, source_target_pairs={{0,3},{1,2},{2,1},{3,0},{4,7},{5,6},{6,5},{7,4},{8,11},{9,10},{10,... | collective-permute-start | bytes 36872 | tf_op jit(solution)/shard_map/ppermute | solution.py:438
  36.8 1.1 %collective-permute-done.11.refs_10_ = f32[24,128]{1,0:T(8,128)S(1)} collective-permute-done((f32[24,128]{1,0:T(8,128)S(1)}, f32[24,128]{1,0:T(8,128)S(1)}, u32[]{:S(2)}, u32[]{:S(2)}) %collective-permute-start.11) | collective-permute-done | bytes 12320 | tf_op jit(solution)/shard_map/ppermute | solution.py:438
  37.9 1.1 %collective-permute-done.12.refs_11_ = f32[24,128]{1,0:T(8,128)S(1)} collective-permute-done((f32[24,128]{1,0:T(8,128)S(1)}, f32[24,128]{1,0:T(8,128)S(1)}, u32[]{:S(2)}, u32[]{:S(2)}) %collective-permute-start.12) | collective-permute-done | bytes 12320 | tf_op jit(solution)/shard_map/ppermute | solution.py:438
  39.0 1.2 %collective-permute-start.13 = (f32[96,128]{1,0:T(8,128)S(1)}, f32[96,128]{1,0:T(8,128)S(1)}, u32[]{:S(2)}, u32[]{:S(2)}) collective-permute-start(f32[96,128]{1,0:T(8,128)S(1)} %constant_dynamic-update-slice_fusion.4), channel_id=1, source_target_pairs={{0,4},{4,0},{8,12},{12,8},{16,20},{20,16},{24,28},{28,24},{1,5},{5... | collective-permute-start | bytes 147464 | tf_op jit(solution)/shard_map/ppermute | solution.py:447
  40.3 1.6 %collective-permute-start.14 = (f32[96,128]{1,0:T(8,128)S(1)}, f32[96,128]{1,0:T(8,128)S(1)}, u32[]{:S(2)}, u32[]{:S(2)}) collective-permute-start(f32[96,128]{1,0:T(8,128)S(1)} %constant_dynamic-update-slice_fusion.4), channel_id=1, source_target_pairs={{0,1},{1,0},{2,3},{3,2},{4,8},{5,9},{6,10},{7,11},{8,4},{9,5},{10,... | collective-permute-start | bytes 147464 | tf_op jit(solution)/shard_map/ppermute | solution.py:447
  41.9 3.2 %shard_map.64.refs_6_ = f32[9,8,64]{2,1,0:T(8,128)S(1)} custom-call(f32[896,128]{1,0:T(8,128)S(1)} %get-tuple-element.19.refs_0_.far, f32[64,128]{1,0:T(8,128)S(1)} %get-tuple-element.17.refs_1_.refs_0_.cols, f32[3,5,8,14,8,128]{5,4,3,2,1,0:T(8,128)S(1)} %get-tuple-element.29.refs_0_.refs_4_), custom_call_target="tpu_custom_call" | custom-call | tf_op jit(solution)/shard_map/pallas_call | solution.py:540
  45.1 2.0 %shard_map.65.refs_7_ = f32[9,8,64]{2,1,0:T(8,128)S(1)} custom-call(f32[896,128]{1,0:T(8,128)S(1)} %get-tuple-element.19.refs_0_.far, f32[64,128]{1,0:T(8,128)S(1)} %get-tuple-element.17.refs_1_.refs_0_.cols, f32[3,3,8,14,8,128]{5,4,3,2,1,0:T(8,128)S(1)} %get-tuple-element.30.refs_0_.refs_5_), custom_call_target="tpu_custom_call" | custom-call | tf_op jit(solution)/shard_map/pallas_call | solution.py:540
  47.1 0.0 collective-permute-done.13.refs_12_
  47.1 4.0 %shard_map.66 = f32[9,8,64]{2,1,0:T(8,128)} custom-call(f32[64,128]{1,0:T(8,128)S(1)} %get-tuple-element.17.refs_1_.refs_0_.cols, f32[11,8,128]{2,1,0:T(8,128)S(1)} %get-tuple-element.18.refs_1_, f32[224,128]{1,0:T(8,128)S(1)} %get-tuple-element.23.refs_2_, f32[7,8,64]{2,1,0:T(8,128)S(1)} %get-tuple-element.28.refs_3_, ...), custom_call_target="tpu_custom_call" | custom-call | tf_op jit(solution)/shard_map/pallas_call | solution.py:548
  (21 shorter events, 0.1 us)
Async XLA Ops:
  1.6 4.3 %collective-permute-start.2 = (f32[48,128]{1,0:T(8,128)S(1)}, f32[48,128]{1,0:T(8,128)S(1)}, u32[]{:S(2)}, u32[]{:S(2)}) collective-permute-start(f32[48,128]{1,0:T(8,128)S(1)} %shard_map.59.refs_0_), channel_id=1, source_target_pairs={{0,3},{1,2},{2,1},{3,0},{4,7},{5,6},{6,5},{7,4},{8,11},{9,10},{10,... | collective-permute-start | bytes 73736 | tf_op jit(solution)/shard_map/ppermute | solution.py:438
  4.6 2.7 %collective-permute-start.1 = (f32[48,128]{1,0:T(8,128)S(1)}, f32[48,128]{1,0:T(8,128)S(1)}, u32[]{:S(2)}, u32[]{:S(2)}) collective-permute-start(f32[48,128]{1,0:T(8,128)S(1)} %shard_map.59.refs_0_), channel_id=1, source_target_pairs={{0,2},{1,3},{2,0},{3,1},{4,6},{5,7},{6,4},{7,5},{8,10},{9,11},{10,... | collective-permute-start | bytes 73736 | tf_op jit(solution)/shard_map/ppermute | solution.py:438
  4.8 2.7 %collective-permute-start = (f32[48,128]{1,0:T(8,128)S(1)}, f32[48,128]{1,0:T(8,128)S(1)}, u32[]{:S(2)}, u32[]{:S(2)}) collective-permute-start(f32[48,128]{1,0:T(8,128)S(1)} %shard_map.59.refs_0_), channel_id=1, source_target_pairs={{0,1},{1,0},{2,3},{3,2},{4,5},{5,4},{6,7},{7,6},{8,9},{9,8},{10,11... | collective-permute-start | bytes 73736 | tf_op jit(solution)/shard_map/ppermute | solution.py:438
  7.5 3.7 %collective-permute-start.3 = (f32[160,128]{1,0:T(8,128)S(1)}, f32[160,128]{1,0:T(8,128)S(1)}, u32[]{:S(2)}, u32[]{:S(2)}) collective-permute-start(f32[160,128]{1,0:T(8,128)S(1)} %pad_maximum_fusion), channel_id=1, source_target_pairs={{0,4},{4,0},{8,12},{12,8},{16,20},{20,16},{24,28},{28,24},{1,5},{5... | collective-permute-start | bytes 245768 | tf_op jit(solution)/shard_map/ppermute | solution.py:447
  10.0 4.1 %collective-permute-start.4 = (f32[160,128]{1,0:T(8,128)S(1)}, f32[160,128]{1,0:T(8,128)S(1)}, u32[]{:S(2)}, u32[]{:S(2)}) collective-permute-start(f32[160,128]{1,0:T(8,128)S(1)} %pad_maximum_fusion), channel_id=1, source_target_pairs={{0,1},{1,0},{2,3},{3,2},{4,8},{5,9},{6,10},{7,11},{8,4},{9,5},{10,... | collective-permute-start | bytes 245768 | tf_op jit(solution)/shard_map/ppermute | solution.py:447
  19.2 12.4 %copy-start = (f32[8,64]{1,0:T(8,128)S(1)}, f32[8,64]{1,0:T(8,128)}, u32[]{:S(2)}) copy-start(f32[8,64]{1,0:T(8,128)} %get-tuple-element.16.refs_3_) | copy-start | bytes 6148
  19.2 2.7 %collective-permute-start.5 = (f32[8,128]{1,0:T(8,128)S(1)}, f32[8,128]{1,0:T(8,128)S(1)}, u32[]{:S(2)}, u32[]{:S(2)}) collective-permute-start(f32[8,128]{1,0:T(8,128)S(1)} %get-tuple-element.27.refs_6_), channel_id=1, source_target_pairs={{0,1},{1,0},{2,3},{3,2},{4,5},{5,4},{6,7},{7,6},{8,9},{9,8},{10,11... | collective-permute-start | bytes 12296 | tf_op jit(solution)/shard_map/ppermute | solution.py:438
  19.2 2.7 %collective-permute-start.6 = (f32[8,128]{1,0:T(8,128)S(1)}, f32[8,128]{1,0:T(8,128)S(1)}, u32[]{:S(2)}, u32[]{:S(2)}) collective-permute-start(f32[8,128]{1,0:T(8,128)S(1)} %get-tuple-element.27.refs_6_), channel_id=1, source_target_pairs={{0,2},{1,3},{2,0},{3,1},{4,6},{5,7},{6,4},{7,5},{8,10},{9,11},{10,... | collective-permute-start | bytes 12296 | tf_op jit(solution)/shard_map/ppermute | solution.py:438
  20.7 3.4 %collective-permute-start.7 = (f32[8,128]{1,0:T(8,128)S(1)}, f32[8,128]{1,0:T(8,128)S(1)}, u32[]{:S(2)}, u32[]{:S(2)}) collective-permute-start(f32[8,128]{1,0:T(8,128)S(1)} %get-tuple-element.27.refs_6_), channel_id=1, source_target_pairs={{0,3},{1,2},{2,1},{3,0},{4,7},{5,6},{6,5},{7,4},{8,11},{9,10},{10,... | collective-permute-start | bytes 12296 | tf_op jit(solution)/shard_map/ppermute | solution.py:438
  24.0 7.5 %collective-permute-start.8 = (f32[32,128]{1,0:T(8,128)S(1)}, f32[32,128]{1,0:T(8,128)S(1)}, u32[]{:S(2)}, u32[]{:S(2)}) collective-permute-start(f32[32,128]{1,0:T(8,128)S(1)} %constant_dynamic-update-slice_fusion), channel_id=1, source_target_pairs={{0,4},{4,0},{8,12},{12,8},{16,20},{20,16},{24,28},{28,24},{1,5},{5... | collective-permute-start | bytes 49160 | tf_op jit(solution)/shard_map/ppermute | solution.py:447
  26.2 5.4 %collective-permute-start.9 = (f32[32,128]{1,0:T(8,128)S(1)}, f32[32,128]{1,0:T(8,128)S(1)}, u32[]{:S(2)}, u32[]{:S(2)}) collective-permute-start(f32[32,128]{1,0:T(8,128)S(1)} %constant_dynamic-update-slice_fusion), channel_id=1, source_target_pairs={{0,1},{1,0},{2,3},{3,2},{4,8},{5,9},{6,10},{7,11},{8,4},{9,5},{10,... | collective-permute-start | bytes 49160 | tf_op jit(solution)/shard_map/ppermute | solution.py:447
  34.1 2.7 %collective-permute-start.10 = (f32[24,128]{1,0:T(8,128)S(1)}, f32[24,128]{1,0:T(8,128)S(1)}, u32[]{:S(2)}, u32[]{:S(2)}) collective-permute-start(f32[24,128]{1,0:T(8,128)S(1)} %get-tuple-element.31.refs_8_), channel_id=1, source_target_pairs={{0,1},{1,0},{2,3},{3,2},{4,5},{5,4},{6,7},{7,6},{8,9},{9,8},{10,11... | collective-permute-start | bytes 36872 | tf_op jit(solution)/shard_map/ppermute | solution.py:438
  35.3 2.5 %collective-permute-start.11 = (f32[24,128]{1,0:T(8,128)S(1)}, f32[24,128]{1,0:T(8,128)S(1)}, u32[]{:S(2)}, u32[]{:S(2)}) collective-permute-start(f32[24,128]{1,0:T(8,128)S(1)} %get-tuple-element.31.refs_8_), channel_id=1, source_target_pairs={{0,2},{1,3},{2,0},{3,1},{4,6},{5,7},{6,4},{7,5},{8,10},{9,11},{10,... | collective-permute-start | bytes 36872 | tf_op jit(solution)/shard_map/ppermute | solution.py:438
  35.6 3.4 %collective-permute-start.12 = (f32[24,128]{1,0:T(8,128)S(1)}, f32[24,128]{1,0:T(8,128)S(1)}, u32[]{:S(2)}, u32[]{:S(2)}) collective-permute-start(f32[24,128]{1,0:T(8,128)S(1)} %get-tuple-element.31.refs_8_), channel_id=1, source_target_pairs={{0,3},{1,2},{2,1},{3,0},{4,7},{5,6},{6,5},{7,4},{8,11},{9,10},{10,... | collective-permute-start | bytes 36872 | tf_op jit(solution)/shard_map/ppermute | solution.py:438
  39.0 8.1 %collective-permute-start.13 = (f32[96,128]{1,0:T(8,128)S(1)}, f32[96,128]{1,0:T(8,128)S(1)}, u32[]{:S(2)}, u32[]{:S(2)}) collective-permute-start(f32[96,128]{1,0:T(8,128)S(1)} %constant_dynamic-update-slice_fusion.4), channel_id=1, source_target_pairs={{0,4},{4,0},{8,12},{12,8},{16,20},{20,16},{24,28},{28,24},{1,5},{5... | collective-permute-start | bytes 147464 | tf_op jit(solution)/shard_map/ppermute | solution.py:447
  40.3 6.9 %collective-permute-start.14 = (f32[96,128]{1,0:T(8,128)S(1)}, f32[96,128]{1,0:T(8,128)S(1)}, u32[]{:S(2)}, u32[]{:S(2)}) collective-permute-start(f32[96,128]{1,0:T(8,128)S(1)} %constant_dynamic-update-slice_fusion.4), channel_id=1, source_target_pairs={{0,1},{1,0},{2,3},{3,2},{4,8},{5,9},{6,10},{7,11},{8,4},{9,5},{10,... | collective-permute-start | bytes 147464 | tf_op jit(solution)/shard_map/ppermute | solution.py:447

commit v6 on v5

--- a/solution.py
+++ b/solution.py
@@ -15,7 +15,7 @@
 SLOPE = -5.0 * SIGMA * 32.0
 TINY = 1e-37
 FACTOR_SPLIT = (5, 8)
-MOMENT_SPLIT = (5, 8)
+MOMENT_SPLIT = (4, 8)
 SUB = 8
 LANES = 128
 X, SMOOTH, MASS, VEL = 0, 3, 4, 5
@@ -149,14 +149,13 @@
     return jnp.broadcast_to(ref[pl.ds((field * tiles + t) * SUB + d, 1), :], (SUB, LANES))
 
 
-def each_slot(first, count, blocks, width, cols, result, group):
-    together = 2 if count % 2 == 0 else 1
+def each_slot(first, count, blocks, width, cols, result, group, together=2):
     lane = lane_iota()
 
-    def body(step, carry):
+    def body(start, together):
         found = [[] for _ in range(width // SUB)]
         for n in range(together):
-            d = step * together + n
+            d = start + n
             at = first + d
             own = pltpu.roll(cols[...], lax.rem(LANES - at, LANES), axis=1)
             for g in range(width // SUB):
@@ -168,37 +167,30 @@
                 for at, total in found[g]:
                     rows = jnp.where(lane == at, total, rows)
                 result[group_rows(g), :] = rows
+
+    def step(i, carry):
+        body(i * together, together)
         return carry
 
-    lax.fori_loop(0, count // together, body, 0)
+    lax.fori_loop(0, count // together, step, 0)
+    if count % together:
+        body(count - count % together, count % together)
 
 
 def sums_of(result, n, blocks, width):
     return jnp.transpose(result[...])[n * blocks : (n + 1) * blocks, 0:width]
 
 
-def density_body(groups, blocks, width, tiles, *refs):
-    parts = refs[: groups + 2]
-    vol_out, rho_out, far, cols, own_rows, meta, hot, dist_out = refs[groups + 2 : groups + 10]
-    region, own_range, own_tiles, result = refs[groups + 10 :]
+def lists_body(groups, blocks, width, tiles, *refs):
+    parts = refs[:groups]
+    cols, own_rows, hot, own_range, own_tiles = refs[groups:]
     slab = groups * blocks
     me = lax.axis_index("seg")
-    kept = parts[groups].shape[0] // groups
-
-    def store(at, ref, start):
-        rows = pl.ds(at, SUB)
-        for n in range(4):
-            region[rows, n * LANES : (n + 1) * LANES] = ref[start + n * SUB : start + (n + 1) * SUB, :]
-        meta[rows, :] = ref[start + 4 * SUB : start + 5 * SUB, :]
-
-    place_region(groups, blocks, parts, kept, region, store)
-    clear_tail(meta, 3 * slab)
     for k in range(groups):
         rows = pl.ds(pl.multiple_of(jnp.bitwise_xor(me, k) * blocks, SUB), SUB)
         for n in range(6):
             own_range[rows, n * LANES : (n + 1) * LANES] = parts[k][n * SUB : (n + 1) * SUB, :]
     own_tiles[...] = jnp.zeros_like(own_tiles)
-    result[...] = jnp.zeros_like(result)
     places = own_range[:, 4 * LANES + 2 * tiles : 4 * LANES + 2 * tiles + 1].astype(jnp.int32)
     wanted = me * blocks + lane_iota(slab)
     picks = jnp.where(jnp.broadcast_to(places, (slab, LANES)) == wanted, 1.0, 0.0)
@@ -218,16 +210,34 @@
     for n in range(8):
         own_tiles[n * SUB : (n + 1) * SUB, :] = own_rows[n]
     cols[...] = jnp.transpose(own_tiles[...])[0:width, :]
-    size = region.shape[0]
+    size = hot.shape[1]
     column_ids = lax.broadcasted_iota(jnp.int32, (SUB, size), 1)
     index = entries.astype(jnp.int32)
     for n in range(2 * tiles):
         chosen = jnp.broadcast_to(index[:, n : n + 1], (SUB, size)) == column_ids
         hot[n * SUB : (n + 1) * SUB, :] = jnp.where(chosen, 1.0, 0.0)
+
+
+def density_body(groups, blocks, width, tiles, *refs):
+    cols, own_rows, hot = refs[:3]
+    parts = refs[3 : groups + 5]
+    vol_out, rho_out, far, meta, dist_out, region, result = refs[groups + 5 :]
+    slab = groups * blocks
+    kept = parts[groups].shape[0] // groups
+
+    def store(at, ref, start):
+        rows = pl.ds(at, SUB)
+        for n in range(4):
+            region[rows, n * LANES : (n + 1) * LANES] = ref[start + n * SUB : start + (n + 1) * SUB, :]
+        meta[rows, :] = ref[start + 4 * SUB : start + 5 * SUB, :]
+
+    place_region(groups, blocks, parts, kept, region, store)
+    clear_tail(meta, 3 * slab)
+    result[...] = jnp.zeros_like(result)
     values = parts_of(region[...])
     half = tiles * SUB
-    left = select(hot[0:half, :].astype(jnp.bfloat16), values)
-    right = select(hot[half:, :].astype(jnp.bfloat16), values)
+    both = select(hot[...].astype(jnp.bfloat16), values)
+    left, right = both[0:half], both[half:]
 
     def keep(n, value):
         far[n * half : (n + 1) * half, :] = value
@@ -252,12 +262,12 @@
 
     each_slot(0, blocks, blocks, width, cols, result, group)
     sums = sums_of(result, 0, blocks, width)
-    smooth, mass, count = [own_rows[n, :, 0:width] for n in (SMOOTH, MASS, 10)]
+    smooth, count = [own_rows[n, :, 0:width] for n in (SMOOTH, 10)]
     live = jnp.where(lane_iota()[:, 0:width].astype(jnp.float32) < count, 1.0, 0.0)
     rho = 4.0 * SIGMA / (smooth * smooth * smooth) * sums + (1.0 - live)
     rho_out[...] = rho
-    vol = mass / rho
-    vol_out[...] = jnp.concatenate([vol, vol], axis=1)
+    share = 1.0 / rho
+    vol_out[...] = jnp.concatenate([share, share], axis=1)
 
 
 def placed_lists(slab, tiles, meta, hot):
@@ -287,7 +297,7 @@
             inv = 1.0 / (smooth + far_row(far, SMOOTH, tiles, at, t))
             inv2 = inv * inv
             part = jnp.maximum(inv - dist[at, g, t] * inv2, 0.0)
-            weight = part * part * part * inv2
+            weight = part * part * part * inv2 * far_row(far, MASS, tiles, at, t)
             ex, ey, ez = weight * dx, weight * dy, weight * dz
             slopes[0, d, g, t], slopes[1, d, g, t], slopes[2, d, g, t] = ex, ey, ez
             for n, term in enumerate((ex * dx, ey * dy, ez * dz, ex * dy, ex * dz, ey * dz)):
@@ -311,8 +321,8 @@
     result[...] = jnp.zeros_like(result)
     values = parts_of(region[...])
     half = tiles * SUB
-    left = select(hot[0:half, :].astype(jnp.bfloat16), values)
-    right = select(hot[half:, :].astype(jnp.bfloat16), values)
+    both = select(hot[...].astype(jnp.bfloat16), values)
+    left, right = both[0:half], both[half:]
     far_vol[...] = jnp.where(lane_iota(half) < HALF, left, right)
 
     def group(product, d, at, g, own):
@@ -327,13 +337,12 @@
         each_slot(first, count, blocks, width, cols, result, functools.partial(group, product))
     sums = jnp.transpose(result[...])
     press = GAMMA_LESS * own_rows[8, :, 0:width] / rho[...]
-    scale = own_rows[MASS, :, 0:width] * press
     coefs = []
     for n in range(6):
         tensor = SLOPE * sums[n * blocks : (n + 1) * blocks, 0:width]
         corr = (2.0 + tensor) if n < 3 else tensor
         corr_out[n] = corr
-        coefs.append(scale * corr)
+        coefs.append(press * corr)
     corr_out[6] = press
     for n in range(3):
         coef_out[n * SUB : (n + 1) * SUB, :] = jnp.concatenate(coefs[2 * n : 2 * n + 2], axis=1)
@@ -347,8 +356,7 @@
         vel = [column(own, VEL + a) for a in range(3)]
         total = [jnp.zeros((SUB, LANES), jnp.float32) for _ in range(9)]
         for t in range(tiles):
-            mass = far_row(far, MASS, tiles, at, t)
-            px, py, pz = [mass * slope[a, at - start, g, t] for a in range(3)]
+            px, py, pz = [slope[a, at - start, g, t] for a in range(3)]
             vx, vy, vz = [vel[a] - far_row(far, VEL + a, tiles, at, t) for a in range(3)]
             terms = (
                 px,
@@ -366,7 +374,7 @@
         return total
 
     for (low, count, start), slope in zip(spans, slopes):
-        each_slot(low, count, blocks, width, cols, result, functools.partial(group, slope, start))
+        each_slot(low, count, blocks, width, cols, result, functools.partial(group, slope, start), 1)
     sums = jnp.transpose(result[...])
     for n in range(9):
         out[n] = sums[n * blocks : (n + 1) * blocks, 0:width]
@@ -389,8 +397,8 @@
     result[...] = jnp.zeros_like(result)
     values = parts_of(region[...])
     half = tiles * SUB
-    left = select(hot[0:half, :].astype(jnp.bfloat16), values)
-    right = select(hot[half:, :].astype(jnp.bfloat16), values)
+    both = select(hot[...].astype(jnp.bfloat16), values)
+    left, right = both[0:half], both[half:]
 
     def keep(n, value):
         far_coef[n * half : (n + 1) * half, :] = value
@@ -444,7 +452,9 @@
             inside = 0 < r < ranges - 1
             other = (((r + 1) ^ 1) - 1) * groups + s if inside else r * groups + (s ^ 1)
             second.append((r * groups + s, other))
-    return seg + [lax.ppermute(whole, "dom", first), lax.ppermute(whole, ("dom", "seg"), second)]
+    near = lax.ppermute(whole, "dom", first)
+    beside = lax.ppermute(whole, ("dom", "seg"), second)
+    return seg + [near, beside]
 
 
 def spans_of(blocks, split):
@@ -481,27 +491,30 @@
         for value in (counts, new_place, jnp.swapaxes(state, 0, 1), neighbours)
     ])
     parts = exchange(packed, 5 * SUB)
-    vol, rho, far, cols, own_rows, meta, hot, dist = call(
+    cols, own_rows, hot = call(
+        functools.partial(lists_body, groups, blocks, width, tiles),
+        (
+            shape(width, LANES),
+            shape(11, SUB, LANES),
+            shape(2 * tiles * SUB, size),
+        ),
+        in_specs=[vm] * groups,
+        out_specs=(vm,) * 3,
+        scratch=(VMEM((slab, 6 * LANES), f32), VMEM((LANES, LANES), f32)),
+    )(*parts[:groups])
+    vol, rho, far, meta, dist = call(
         functools.partial(density_body, groups, blocks, width, tiles),
         (
             shape(SUB, LANES),
             shape(blocks, width),
             shape(8 * tiles * SUB, LANES),
-            shape(width, LANES),
-            shape(11, SUB, LANES),
             shape(size, LANES),
-            shape(2 * tiles * SUB, size),
             shape(*many),
         ),
-        in_specs=[vm] * (groups + 2),
-        out_specs=(vm,) * 8,
-        scratch=(
-            VMEM((size, 4 * LANES), f32),
-            VMEM((slab, 6 * LANES), f32),
-            VMEM((LANES, LANES), f32),
-            columns,
-        ),
-    )(*parts)
+        in_specs=[vm] * (groups + 5),
+        out_specs=(vm,) * 5,
+        scratch=(VMEM((size, 4 * LANES), f32), columns),
+    )(cols, own_rows, hot, *parts)
     vols = exchange(vol, SUB)
     spans = spans_of(blocks, FACTOR_SPLIT)
     slopes, products = [], []

time: 51.6 us -> 51.2 us (level)
  Pallas kernels: 22.5 us -> 21.7 us
    ppermute x9, waiting for transfers between devices: 6.93 us -> 7.78 us  [exchange(): seg.append(lax.ppermute(own, 'seg', [(i, i ^ k) for i in range(groups)]))]
where the time goes in v6:
time: 51.2 us; the launch traced here: 50.8 us
  Pallas kernels  21.7 us (42%)
  starting transfers between devices  18.1 us (35%)
  waiting for transfers between devices  10.2 us (20%)
  between operations  0.75 us (1%)
    ppermute x9, starting transfers between devices, exchange(): seg.append(lax.ppermute(own, 'seg', [(i, i ^ k) for i in range(groups)]))  8.66 us
    ppermute x9, waiting for transfers between devices, exchange(): seg.append(lax.ppermute(own, 'seg', [(i, i ^ k) for i in range(groups)]))  7.78 us
    ppermute x3, starting transfers between devices, exchange(): near = lax.ppermute(whole, 'dom', first)  5.94 us
    pallas_call x2, Pallas kernels, step(): call(functools.partial(moment_body, blocks, width, tiles, parts), shape(9...  5.19 us
    pallas_call x1, Pallas kernels, step(): call(functools.partial(density_body, groups, blocks, width, tiles), (shap...  4.78 us
    pallas_call x2, Pallas kernels, step(): call(functools.partial(factor_body, low, count, blocks, slab, width, tile...  4.46 us
    pallas_call x1, Pallas kernels, step(): call(functools.partial(update_body, spans, len(moments), groups, blocks,...  3.68 us
    ppermute x3, starting transfers between devices, exchange(): beside = lax.ppermute(whole, ('dom', 'seg'), second)  3.53 us
  transfers between devices with their start and end apart: 15, of which 7 were waited for; matrix products, arithmetic and copies ran while one was open for 0% of the time, Pallas kernels for 20%

profile of v6, /device:TPU:1, one launch (start us, length us, event | category | flops | bytes accessed | tf_op | source)
XLA Modules:
  0.0 50.8 jit_solution(18298792117836097763)
XLA Ops:
  0.6 0.9 %shard_map.59.refs_0_.refs_3_ = f32[48,128]{1,0:T(8,128)S(1)} custom-call(s32[8]{0:T(128)} %refs_0_.1, s32[8]{0:T(128)} %refs_1_.1, f32[9,8,64]{2,1,0:T(8,128)} %bitcast.3, s32[8,26]{1,0:T(8,128)} %refs_3_.1), custom_call_target="tpu_custom_call" | custom-call | tf_op jit(solution)/shard_map/pallas_call | solution.py:477
  1.6 2.1 %collective-permute-start = (f32[48,128]{1,0:T(8,128)S(1)}, f32[48,128]{1,0:T(8,128)S(1)}, u32[]{:S(2)}, u32[]{:S(2)}) collective-permute-start(f32[48,128]{1,0:T(8,128)S(1)} %shard_map.59.refs_0_.refs_3_), channel_id=1, source_target_pairs={{0,1},{1,0},{2,3},{3,2},{4,5},{5,4},{6,7},{7,6},{8,9},{9,8},{10,11... | collective-permute-start | bytes 73736 | tf_op jit(solution)/shard_map/ppermute | solution.py:446
  3.6 1.2 %collective-permute-start.1 = (f32[48,128]{1,0:T(8,128)S(1)}, f32[48,128]{1,0:T(8,128)S(1)}, u32[]{:S(2)}, u32[]{:S(2)}) collective-permute-start(f32[48,128]{1,0:T(8,128)S(1)} %shard_map.59.refs_0_.refs_3_), channel_id=1, source_target_pairs={{0,2},{1,3},{2,0},{3,1},{4,6},{5,7},{6,4},{7,5},{8,10},{9,11},{10,... | collective-permute-start | bytes 73736 | tf_op jit(solution)/shard_map/ppermute | solution.py:446
  4.9 0.0 collective-permute-start.2
  4.9 1.4 %collective-permute-done.1.refs_2_.refs_5_ = f32[48,128]{1,0:T(8,128)S(1)} collective-permute-done((f32[48,128]{1,0:T(8,128)S(1)}, f32[48,128]{1,0:T(8,128)S(1)}, u32[]{:S(2)}, u32[]{:S(2)}) %collective-permute-start.1) | collective-permute-done | bytes 24608 | tf_op jit(solution)/shard_map/ppermute | solution.py:446
  6.3 2.1 %collective-permute-done.2.refs_3_.refs_6_ = f32[48,128]{1,0:T(8,128)S(1)} collective-permute-done((f32[48,128]{1,0:T(8,128)S(1)}, f32[48,128]{1,0:T(8,128)S(1)}, u32[]{:S(2)}, u32[]{:S(2)}) %collective-permute-start.2) | collective-permute-done | bytes 24608 | tf_op jit(solution)/shard_map/ppermute | solution.py:446
  8.5 2.5 %collective-permute-start.3 = (f32[160,128]{1,0:T(8,128)S(1)}, f32[160,128]{1,0:T(8,128)S(1)}, u32[]{:S(2)}, u32[]{:S(2)}) collective-permute-start(f32[160,128]{1,0:T(8,128)S(1)} %pad_maximum_fusion), channel_id=1, source_target_pairs={{0,4},{4,0},{8,12},{12,8},{16,20},{20,16},{24,28},{28,24},{1,5},{5... | collective-permute-start | bytes 245768 | tf_op jit(solution)/shard_map/ppermute | solution.py:455
  10.9 1.3 %collective-permute-start.4 = (f32[160,128]{1,0:T(8,128)S(1)}, f32[160,128]{1,0:T(8,128)S(1)}, u32[]{:S(2)}, u32[]{:S(2)}) collective-permute-start(f32[160,128]{1,0:T(8,128)S(1)} %pad_maximum_fusion), channel_id=1, source_target_pairs={{0,1},{1,0},{2,3},{3,2},{4,8},{5,9},{6,10},{7,11},{8,4},{9,5},{10,... | collective-permute-start | bytes 245768 | tf_op jit(solution)/shard_map/ppermute | solution.py:456
  12.2 0.5 shard_map.60
  12.6 0.0 collective-permute-done.3.refs_7_
  12.6 2.4 %collective-permute-done.4.refs_8_ = f32[160,128]{1,0:T(8,128)S(1)} collective-permute-done((f32[160,128]{1,0:T(8,128)S(1)}, f32[160,128]{1,0:T(8,128)S(1)}, u32[]{:S(2)}, u32[]{:S(2)}) %collective-permute-start.4) | collective-permute-done | bytes 81952 | tf_op jit(solution)/shard_map/ppermute | solution.py:456
  15.1 4.8 %shard_map.61 = (f32[8,128]{1,0:T(8,128)S(1)}, f32[8,64]{1,0:T(8,128)}, f32[896,128]{1,0:T(8,128)S(1)}, f32[128,128]{1,0:T(8,128)S(1)}, f32[8,8,14,8,128]{4,3,2,1,0:T(8,128)S(1)}) custom-call(f32[64,128]{1,0:T(8,128)S(1)} %get-tuple-element.17.refs_0_.refs_1_.cols, f32[11,8,128]{2,1,0:T(8,128)S(1)} %get-tuple-element.18.refs_1_, ...), custom_call_target="tpu_custom_call" | custom-call | tf_op jit(solution)/shard_map/pallas_call | solution.py:505
  19.8 0.3 collective-permute-start.5
  20.1 2.4 %collective-permute-start.7 = (f32[8,128]{1,0:T(8,128)S(1)}, f32[8,128]{1,0:T(8,128)S(1)}, u32[]{:S(2)}, u32[]{:S(2)}) collective-permute-start(f32[8,128]{1,0:T(8,128)S(1)} %get-tuple-element.27.refs_6_), channel_id=1, source_target_pairs={{0,3},{1,2},{2,1},{3,0},{4,7},{5,6},{6,5},{7,4},{8,11},{9,10},{10,... | collective-permute-start | bytes 12296 | tf_op jit(solution)/shard_map/ppermute | solution.py:446
  22.5 0.1 collective-permute-done.6.refs_8_
  22.6 0.9 %collective-permute-done.7.refs_9_ = f32[8,128]{1,0:T(8,128)S(1)} collective-permute-done((f32[8,128]{1,0:T(8,128)S(1)}, f32[8,128]{1,0:T(8,128)S(1)}, u32[]{:S(2)}, u32[]{:S(2)}) %collective-permute-start.7) | collective-permute-done | bytes 4128 | tf_op jit(solution)/shard_map/ppermute | solution.py:446
  23.5 1.8 %collective-permute-start.8 = (f32[32,128]{1,0:T(8,128)S(1)}, f32[32,128]{1,0:T(8,128)S(1)}, u32[]{:S(2)}, u32[]{:S(2)}) collective-permute-start(f32[32,128]{1,0:T(8,128)S(1)} %constant_dynamic-update-slice_fusion), channel_id=1, source_target_pairs={{0,4},{4,0},{8,12},{12,8},{16,20},{20,16},{24,28},{28,24},{1,5},{5... | collective-permute-start | bytes 49160 | tf_op jit(solution)/shard_map/ppermute | solution.py:455
  25.3 1.1 %collective-permute-start.9 = (f32[32,128]{1,0:T(8,128)S(1)}, f32[32,128]{1,0:T(8,128)S(1)}, u32[]{:S(2)}, u32[]{:S(2)}) collective-permute-start(f32[32,128]{1,0:T(8,128)S(1)} %constant_dynamic-update-slice_fusion), channel_id=1, source_target_pairs={{0,1},{1,0},{2,3},{3,2},{4,8},{5,9},{6,10},{7,11},{8,4},{9,5},{10,... | collective-permute-start | bytes 49160 | tf_op jit(solution)/shard_map/ppermute | solution.py:456
  26.4 1.6 %shard_map.63 = (f32[3,3,8,14,8,128]{5,4,3,2,1,0:T(8,128)S(1)}, f32[6,3,8,14,8,128]{5,4,3,2,1,0:T(8,128)S(1)}) custom-call(f32[896,128]{1,0:T(8,128)S(1)} %get-tuple-element.20.refs_0_.far, f32[64,128]{1,0:T(8,128)S(1)} %get-tuple-element.17.refs_0_.refs_1_.cols, f32[8,8,14,8,128]{4,3,2,1,0:T(8,128)S(1)} %get-tuple-element.21.refs_2_), custom_call_target="tpu_custom_call" | custom-call | tf_op jit(solution)/shard_map/pallas_call | solution.py:526
  28.0 2.9 %shard_map.62 = (f32[3,5,8,14,8,128]{5,4,3,2,1,0:T(8,128)S(1)}, f32[6,5,8,14,8,128]{5,4,3,2,1,0:T(8,128)S(1)}, f32[224,128]{1,0:T(8,128)S(1)}) custom-call(f32[896,128]{1,0:T(8,128)S(1)} %get-tuple-element.20.refs_0_.far, f32[64,128]{1,0:T(8,128)S(1)} %get-tuple-element.17.refs_0_.refs_1_.cols, f32[8,8,14,8,128]{4,3,2,1,0:T(8,128)S(1)} %get-tuple-element.21.refs_2_, ...), custom_call_target="tpu_custom_call" | custom-call | tf_op jit(solution)/shard_map/pallas_call | solution.py:526
  30.9 2.2 %shard_map.64 = (f32[24,128]{1,0:T(8,128)S(1)}, f32[7,8,64]{2,1,0:T(8,128)S(1)}) custom-call(f32[64,128]{1,0:T(8,128)S(1)} %get-tuple-element.17.refs_0_.refs_1_.cols, f32[11,8,128]{2,1,0:T(8,128)S(1)} %get-tuple-element.18.refs_1_, f32[224,128]{1,0:T(8,128)S(1)} %get-tuple-element.23.refs_2_, f32[8,64]{1,0:T(8,128)S(1)} %copy-done, ...), custom_call_target="tpu_custom_call" | custom-call | tf_op jit(solution)/shard_map/pallas_call | solution.py:536
  33.1 1.2 %collective-permute-start.10 = (f32[24,128]{1,0:T(8,128)S(1)}, f32[24,128]{1,0:T(8,128)S(1)}, u32[]{:S(2)}, u32[]{:S(2)}) collective-permute-start(f32[24,128]{1,0:T(8,128)S(1)} %get-tuple-element.31.refs_8_), channel_id=1, source_target_pairs={{0,1},{1,0},{2,3},{3,2},{4,5},{5,4},{6,7},{7,6},{8,9},{9,8},{10,11... | collective-permute-start | bytes 36872 | tf_op jit(solution)/shard_map/ppermute | solution.py:446
  34.3 1.2 %collective-permute-start.11 = (f32[24,128]{1,0:T(8,128)S(1)}, f32[24,128]{1,0:T(8,128)S(1)}, u32[]{:S(2)}, u32[]{:S(2)}) collective-permute-start(f32[24,128]{1,0:T(8,128)S(1)} %get-tuple-element.31.refs_8_), channel_id=1, source_target_pairs={{0,2},{1,3},{2,0},{3,1},{4,6},{5,7},{6,4},{7,5},{8,10},{9,11},{10,... | collective-permute-start | bytes 36872 | tf_op jit(solution)/shard_map/ppermute | solution.py:446
  35.5 0.2 collective-permute-start.12
  35.7 1.1 %collective-permute-done.11.refs_10_ = f32[24,128]{1,0:T(8,128)S(1)} collective-permute-done((f32[24,128]{1,0:T(8,128)S(1)}, f32[24,128]{1,0:T(8,128)S(1)}, u32[]{:S(2)}, u32[]{:S(2)}) %collective-permute-start.11) | collective-permute-done | bytes 12320 | tf_op jit(solution)/shard_map/ppermute | solution.py:446
  36.9 2.1 %collective-permute-done.12.refs_11_ = f32[24,128]{1,0:T(8,128)S(1)} collective-permute-done((f32[24,128]{1,0:T(8,128)S(1)}, f32[24,128]{1,0:T(8,128)S(1)}, u32[]{:S(2)}, u32[]{:S(2)}) %collective-permute-start.12) | collective-permute-done | bytes 12320 | tf_op jit(solution)/shard_map/ppermute | solution.py:446
  39.0 1.6 %collective-permute-start.13 = (f32[96,128]{1,0:T(8,128)S(1)}, f32[96,128]{1,0:T(8,128)S(1)}, u32[]{:S(2)}, u32[]{:S(2)}) collective-permute-start(f32[96,128]{1,0:T(8,128)S(1)} %constant_dynamic-update-slice_fusion.4), channel_id=1, source_target_pairs={{0,4},{4,0},{8,12},{12,8},{16,20},{20,16},{24,28},{28,24},{1,5},{5... | collective-permute-start | bytes 147464 | tf_op jit(solution)/shard_map/ppermute | solution.py:455
  40.6 1.2 %collective-permute-start.14 = (f32[96,128]{1,0:T(8,128)S(1)}, f32[96,128]{1,0:T(8,128)S(1)}, u32[]{:S(2)}, u32[]{:S(2)}) collective-permute-start(f32[96,128]{1,0:T(8,128)S(1)} %constant_dynamic-update-slice_fusion.4), channel_id=1, source_target_pairs={{0,1},{1,0},{2,3},{3,2},{4,8},{5,9},{6,10},{7,11},{8,4},{9,5},{10,... | collective-permute-start | bytes 147464 | tf_op jit(solution)/shard_map/ppermute | solution.py:456
  41.9 2.5 %shard_map.65.refs_6_ = f32[9,8,64]{2,1,0:T(8,128)S(1)} custom-call(f32[896,128]{1,0:T(8,128)S(1)} %get-tuple-element.20.refs_0_.far, f32[64,128]{1,0:T(8,128)S(1)} %get-tuple-element.17.refs_0_.refs_1_.cols, f32[3,5,8,14,8,128]{5,4,3,2,1,0:T(8,128)S(1)} %get-tuple-element.29.refs_0_.refs_4_), custom_call_target="tpu_custom_call" | custom-call | tf_op jit(solution)/shard_map/pallas_call | solution.py:553
  44.4 2.6 %shard_map.66.refs_7_ = f32[9,8,64]{2,1,0:T(8,128)S(1)} custom-call(f32[896,128]{1,0:T(8,128)S(1)} %get-tuple-element.20.refs_0_.far, f32[64,128]{1,0:T(8,128)S(1)} %get-tuple-element.17.refs_0_.refs_1_.cols, f32[3,5,8,14,8,128]{5,4,3,2,1,0:T(8,128)S(1)} %get-tuple-element.29.refs_0_.refs_4_, f32[3,3,8,14,8,128]{5,4,3,2,1,0:T(8,128)S(1)} %get-tuple-element.30.refs_1_.refs_5_), custom_call_target="tpu_custom_call" | custom-call | tf_op jit(solution)/shard_map/pallas_call | solution.py:553
  47.1 0.0 collective-permute-done.13.refs_12_
  47.1 3.7 %shard_map.67 = f32[9,8,64]{2,1,0:T(8,128)} custom-call(f32[64,128]{1,0:T(8,128)S(1)} %get-tuple-element.17.refs_0_.refs_1_.cols, f32[11,8,128]{2,1,0:T(8,128)S(1)} %get-tuple-element.18.refs_1_, f32[224,128]{1,0:T(8,128)S(1)} %get-tuple-element.23.refs_2_, f32[7,8,64]{2,1,0:T(8,128)S(1)} %get-tuple-element.28.refs_3_, ...), custom_call_target="tpu_custom_call" | custom-call | tf_op jit(solution)/shard_map/pallas_call | solution.py:561
  (22 shorter events, 0.1 us)
Async XLA Ops:
  1.6 3.4 %collective-permute-start = (f32[48,128]{1,0:T(8,128)S(1)}, f32[48,128]{1,0:T(8,128)S(1)}, u32[]{:S(2)}, u32[]{:S(2)}) collective-permute-start(f32[48,128]{1,0:T(8,128)S(1)} %shard_map.59.refs_0_.refs_3_), channel_id=1, source_target_pairs={{0,1},{1,0},{2,3},{3,2},{4,5},{5,4},{6,7},{7,6},{8,9},{9,8},{10,11... | collective-permute-start | bytes 73736 | tf_op jit(solution)/shard_map/ppermute | solution.py:446
  3.6 2.7 %collective-permute-start.1 = (f32[48,128]{1,0:T(8,128)S(1)}, f32[48,128]{1,0:T(8,128)S(1)}, u32[]{:S(2)}, u32[]{:S(2)}) collective-permute-start(f32[48,128]{1,0:T(8,128)S(1)} %shard_map.59.refs_0_.refs_3_), channel_id=1, source_target_pairs={{0,2},{1,3},{2,0},{3,1},{4,6},{5,7},{6,4},{7,5},{8,10},{9,11},{10,... | collective-permute-start | bytes 73736 | tf_op jit(solution)/shard_map/ppermute | solution.py:446
  4.9 3.6 %collective-permute-start.2 = (f32[48,128]{1,0:T(8,128)S(1)}, f32[48,128]{1,0:T(8,128)S(1)}, u32[]{:S(2)}, u32[]{:S(2)}) collective-permute-start(f32[48,128]{1,0:T(8,128)S(1)} %shard_map.59.refs_0_.refs_3_), channel_id=1, source_target_pairs={{0,3},{1,2},{2,1},{3,0},{4,7},{5,6},{6,5},{7,4},{8,11},{9,10},{10,... | collective-permute-start | bytes 73736 | tf_op jit(solution)/shard_map/ppermute | solution.py:446
  8.5 4.2 %collective-permute-start.3 = (f32[160,128]{1,0:T(8,128)S(1)}, f32[160,128]{1,0:T(8,128)S(1)}, u32[]{:S(2)}, u32[]{:S(2)}) collective-permute-start(f32[160,128]{1,0:T(8,128)S(1)} %pad_maximum_fusion), channel_id=1, source_target_pairs={{0,4},{4,0},{8,12},{12,8},{16,20},{20,16},{24,28},{28,24},{1,5},{5... | collective-permute-start | bytes 245768 | tf_op jit(solution)/shard_map/ppermute | solution.py:455
  10.9 4.1 %collective-permute-start.4 = (f32[160,128]{1,0:T(8,128)S(1)}, f32[160,128]{1,0:T(8,128)S(1)}, u32[]{:S(2)}, u32[]{:S(2)}) collective-permute-start(f32[160,128]{1,0:T(8,128)S(1)} %pad_maximum_fusion), channel_id=1, source_target_pairs={{0,1},{1,0},{2,3},{3,2},{4,8},{5,9},{6,10},{7,11},{8,4},{9,5},{10,... | collective-permute-start | bytes 245768 | tf_op jit(solution)/shard_map/ppermute | solution.py:456
  19.8 11.1 %copy-start = (f32[8,64]{1,0:T(8,128)S(1)}, f32[8,64]{1,0:T(8,128)}, u32[]{:S(2)}) copy-start(f32[8,64]{1,0:T(8,128)} %get-tuple-element.16.refs_3_) | copy-start | bytes 6148
  19.8 2.7 %collective-permute-start.5 = (f32[8,128]{1,0:T(8,128)S(1)}, f32[8,128]{1,0:T(8,128)S(1)}, u32[]{:S(2)}, u32[]{:S(2)}) collective-permute-start(f32[8,128]{1,0:T(8,128)S(1)} %get-tuple-element.27.refs_6_), channel_id=1, source_target_pairs={{0,1},{1,0},{2,3},{3,2},{4,5},{5,4},{6,7},{7,6},{8,9},{9,8},{10,11... | collective-permute-start | bytes 12296 | tf_op jit(solution)/shard_map/ppermute | solution.py:446
  20.1 2.5 %collective-permute-start.6 = (f32[8,128]{1,0:T(8,128)S(1)}, f32[8,128]{1,0:T(8,128)S(1)}, u32[]{:S(2)}, u32[]{:S(2)}) collective-permute-start(f32[8,128]{1,0:T(8,128)S(1)} %get-tuple-element.27.refs_6_), channel_id=1, source_target_pairs={{0,2},{1,3},{2,0},{3,1},{4,6},{5,7},{6,4},{7,5},{8,10},{9,11},{10,... | collective-permute-start | bytes 12296 | tf_op jit(solution)/shard_map/ppermute | solution.py:446
  20.1 3.4 %collective-permute-start.7 = (f32[8,128]{1,0:T(8,128)S(1)}, f32[8,128]{1,0:T(8,128)S(1)}, u32[]{:S(2)}, u32[]{:S(2)}) collective-permute-start(f32[8,128]{1,0:T(8,128)S(1)} %get-tuple-element.27.refs_6_), channel_id=1, source_target_pairs={{0,3},{1,2},{2,1},{3,0},{4,7},{5,6},{6,5},{7,4},{8,11},{9,10},{10,... | collective-permute-start | bytes 12296 | tf_op jit(solution)/shard_map/ppermute | solution.py:446
  23.5 7.4 %collective-permute-start.8 = (f32[32,128]{1,0:T(8,128)S(1)}, f32[32,128]{1,0:T(8,128)S(1)}, u32[]{:S(2)}, u32[]{:S(2)}) collective-permute-start(f32[32,128]{1,0:T(8,128)S(1)} %constant_dynamic-update-slice_fusion), channel_id=1, source_target_pairs={{0,4},{4,0},{8,12},{12,8},{16,20},{20,16},{24,28},{28,24},{1,5},{5... | collective-permute-start | bytes 49160 | tf_op jit(solution)/shard_map/ppermute | solution.py:455
  25.3 5.5 %collective-permute-start.9 = (f32[32,128]{1,0:T(8,128)S(1)}, f32[32,128]{1,0:T(8,128)S(1)}, u32[]{:S(2)}, u32[]{:S(2)}) collective-permute-start(f32[32,128]{1,0:T(8,128)S(1)} %constant_dynamic-update-slice_fusion), channel_id=1, source_target_pairs={{0,1},{1,0},{2,3},{3,2},{4,8},{5,9},{6,10},{7,11},{8,4},{9,5},{10,... | collective-permute-start | bytes 49160 | tf_op jit(solution)/shard_map/ppermute | solution.py:456
  33.1 2.7 %collective-permute-start.10 = (f32[24,128]{1,0:T(8,128)S(1)}, f32[24,128]{1,0:T(8,128)S(1)}, u32[]{:S(2)}, u32[]{:S(2)}) collective-permute-start(f32[24,128]{1,0:T(8,128)S(1)} %get-tuple-element.31.refs_8_), channel_id=1, source_target_pairs={{0,1},{1,0},{2,3},{3,2},{4,5},{5,4},{6,7},{7,6},{8,9},{9,8},{10,11... | collective-permute-start | bytes 36872 | tf_op jit(solution)/shard_map/ppermute | solution.py:446
  34.3 2.5 %collective-permute-start.11 = (f32[24,128]{1,0:T(8,128)S(1)}, f32[24,128]{1,0:T(8,128)S(1)}, u32[]{:S(2)}, u32[]{:S(2)}) collective-permute-start(f32[24,128]{1,0:T(8,128)S(1)} %get-tuple-element.31.refs_8_), channel_id=1, source_target_pairs={{0,2},{1,3},{2,0},{3,1},{4,6},{5,7},{6,4},{7,5},{8,10},{9,11},{10,... | collective-permute-start | bytes 36872 | tf_op jit(solution)/shard_map/ppermute | solution.py:446
  35.5 3.4 %collective-permute-start.12 = (f32[24,128]{1,0:T(8,128)S(1)}, f32[24,128]{1,0:T(8,128)S(1)}, u32[]{:S(2)}, u32[]{:S(2)}) collective-permute-start(f32[24,128]{1,0:T(8,128)S(1)} %get-tuple-element.31.refs_8_), channel_id=1, source_target_pairs={{0,3},{1,2},{2,1},{3,0},{4,7},{5,6},{6,5},{7,4},{8,11},{9,10},{10,... | collective-permute-start | bytes 36872 | tf_op jit(solution)/shard_map/ppermute | solution.py:446
  39.0 8.1 %collective-permute-start.13 = (f32[96,128]{1,0:T(8,128)S(1)}, f32[96,128]{1,0:T(8,128)S(1)}, u32[]{:S(2)}, u32[]{:S(2)}) collective-permute-start(f32[96,128]{1,0:T(8,128)S(1)} %constant_dynamic-update-slice_fusion.4), channel_id=1, source_target_pairs={{0,4},{4,0},{8,12},{12,8},{16,20},{20,16},{24,28},{28,24},{1,5},{5... | collective-permute-start | bytes 147464 | tf_op jit(solution)/shard_map/ppermute | solution.py:455
  40.6 6.4 %collective-permute-start.14 = (f32[96,128]{1,0:T(8,128)S(1)}, f32[96,128]{1,0:T(8,128)S(1)}, u32[]{:S(2)}, u32[]{:S(2)}) collective-permute-start(f32[96,128]{1,0:T(8,128)S(1)} %constant_dynamic-update-slice_fusion.4), channel_id=1, source_target_pairs={{0,1},{1,0},{2,3},{3,2},{4,8},{5,9},{6,10},{7,11},{8,4},{9,5},{10,... | collective-permute-start | bytes 147464 | tf_op jit(solution)/shard_map/ppermute | solution.py:456

commit v7 on v6

--- a/solution.py
+++ b/solution.py
@@ -149,7 +149,7 @@
     return jnp.broadcast_to(ref[pl.ds((field * tiles + t) * SUB + d, 1), :], (SUB, LANES))
 
 
-def each_slot(first, count, blocks, width, cols, result, group, together=2):
+def each_slot(first, count, blocks, width, cols, result, group, together=2, batch=1):
     lane = lane_iota()
 
     def body(start, together):
@@ -158,9 +158,16 @@
             d = start + n
             at = first + d
             own = pltpu.roll(cols[...], lax.rem(LANES - at, LANES), axis=1)
-            for g in range(width // SUB):
-                for m, value in enumerate(group(d, at, g, own[group_rows(g), :])):
-                    found[g].append((m * blocks + at, jnp.sum(value, axis=1, keepdims=True)))
+            for low in range(0, width // SUB, batch):
+                rows = [own[group_rows(low + n), :] for n in range(batch)]
+                if batch == 1:
+                    values = [group(d, at, low, rows[0])]
+                else:
+                    values = group(d, at, low, rows)
+                for n, totals in enumerate(values):
+                    for m, value in enumerate(totals):
+                        total = jnp.sum(value, axis=1, keepdims=True)
+                        found[low + n].append((m * blocks + at, total))
         for g in range(width // SUB):
             if found[g]:
                 rows = result[group_rows(g), :]
@@ -244,23 +251,26 @@
 
     far_fields(left, right, keep)
 
-    def group(d, at, g, own):
-        pos = [column(own, X + a) for a in range(3)]
-        scale = 0.5 / column(own, SMOOTH)
-        total = jnp.zeros((SUB, LANES), jnp.float32)
+    def group(d, at, low, owns):
+        pos = [[column(own, X + a) for a in range(3)] for own in owns]
+        scale = [0.5 / column(own, SMOOTH) for own in owns]
+        total = [jnp.zeros((SUB, LANES), jnp.float32) for _ in owns]
         for t in range(tiles):
-            dx, dy, dz = [pos[a] - far_row(far, X + a, tiles, d, t) for a in range(3)]
-            square = dx * dx + dy * dy + dz * dz
-            dist = square * lax.rsqrt(jnp.maximum(square, TINY))
-            dist_out[d, g, t] = dist
-            ratio = dist * scale
-            shell = jnp.maximum(1.0 - ratio, 0.0)
-            shell = shell * shell
-            shell = shell * shell
-            total += shell * (far_row(far, MASS, tiles, d, t) * (0.25 + ratio))
-        return [total]
-
-    each_slot(0, blocks, blocks, width, cols, result, group)
+            far_pos = [far_row(far, X + a, tiles, at, t) for a in range(3)]
+            mass = far_row(far, MASS, tiles, at, t)
+            for n in range(len(owns)):
+                dx, dy, dz = [pos[n][a] - far_pos[a] for a in range(3)]
+                square = dx * dx + dy * dy + dz * dz
+                dist = square * lax.rsqrt(jnp.maximum(square, TINY))
+                dist_out[at, low + n, t] = dist
+                ratio = dist * scale[n]
+                shell = jnp.maximum(1.0 - ratio, 0.0)
+                shell = shell * shell
+                shell = shell * shell
+                total[n] += shell * (mass * (0.25 + ratio))
+        return [[value] for value in total]
+
+    each_slot(0, blocks, blocks, width, cols, result, group, 2, 4)
     sums = sums_of(result, 0, blocks, width)
     smooth, count = [own_rows[n, :, 0:width] for n in (SMOOTH, 10)]
     live = jnp.where(lane_iota()[:, 0:width].astype(jnp.float32) < count, 1.0, 0.0)
@@ -289,22 +299,27 @@
     else:
         slopes, products = refs[3:5]
 
-    def group(d, at, g, own):
-        pos = [column(own, X + a) for a in range(3)]
-        smooth = column(own, SMOOTH)
+    def group(d, at, low, owns):
+        pos = [[column(own, X + a) for a in range(3)] for own in owns]
+        smooth = [column(own, SMOOTH) for own in owns]
         for t in range(tiles):
-            dx, dy, dz = [pos[a] - far_row(far, X + a, tiles, at, t) for a in range(3)]
-            inv = 1.0 / (smooth + far_row(far, SMOOTH, tiles, at, t))
-            inv2 = inv * inv
-            part = jnp.maximum(inv - dist[at, g, t] * inv2, 0.0)
-            weight = part * part * part * inv2 * far_row(far, MASS, tiles, at, t)
-            ex, ey, ez = weight * dx, weight * dy, weight * dz
-            slopes[0, d, g, t], slopes[1, d, g, t], slopes[2, d, g, t] = ex, ey, ez
-            for n, term in enumerate((ex * dx, ey * dy, ez * dz, ex * dy, ex * dz, ey * dz)):
-                products[n, d, g, t] = term
-        return []
-
-    each_slot(first, count, blocks, width, cols, None, group)
+            far_pos = [far_row(far, X + a, tiles, at, t) for a in range(3)]
+            far_smooth = far_row(far, SMOOTH, tiles, at, t)
+            mass = far_row(far, MASS, tiles, at, t)
+            for n in range(len(owns)):
+                g = low + n
+                dx, dy, dz = [pos[n][a] - far_pos[a] for a in range(3)]
+                inv = 1.0 / (smooth[n] + far_smooth)
+                inv2 = inv * inv
+                part = jnp.maximum(inv - dist[at, g, t] * inv2, 0.0)
+                weight = part * part * part * inv2 * mass
+                ex, ey, ez = weight * dx, weight * dy, weight * dz
+                slopes[0, d, g, t], slopes[1, d, g, t], slopes[2, d, g, t] = ex, ey, ez
+                for m, term in enumerate((ex * dx, ey * dy, ez * dz, ex * dy, ex * dz, ey * dz)):
+                    products[m, d, g, t] = term
+        return [[] for _ in owns]
+
+    each_slot(first, count, blocks, width, cols, None, group, 2, 8)
 
 
 def tensor_body(spans, groups, blocks, width, tiles, *refs):
@@ -352,29 +367,31 @@
     slopes, out, result = refs[: len(spans)], refs[-2], refs[-1]
     result[...] = jnp.zeros_like(result)
 
-    def group(slope, start, d, at, g, own):
-        vel = [column(own, VEL + a) for a in range(3)]
-        total = [jnp.zeros((SUB, LANES), jnp.float32) for _ in range(9)]
+    def group(slope, start, d, at, low, owns):
+        vel = [[column(own, VEL + a) for a in range(3)] for own in owns]
+        total = [[jnp.zeros((SUB, LANES), jnp.float32) for _ in range(9)] for _ in owns]
         for t in range(tiles):
-            px, py, pz = [slope[a, at - start, g, t] for a in range(3)]
-            vx, vy, vz = [vel[a] - far_row(far, VEL + a, tiles, at, t) for a in range(3)]
-            terms = (
-                px,
-                py,
-                pz,
-                vx * px,
-                vy * py,
-                vz * pz,
-                vx * py + vy * px,
-                vx * pz + vz * px,
-                vy * pz + vz * py,
-            )
-            for n, term in enumerate(terms):
-                total[n] += term
+            far_vel = [far_row(far, VEL + a, tiles, at, t) for a in range(3)]
+            for k in range(len(owns)):
+                px, py, pz = [slope[a, at - start, low + k, t] for a in range(3)]
+                vx, vy, vz = [vel[k][a] - far_vel[a] for a in range(3)]
+                terms = (
+                    px,
+                    py,
+                    pz,
+                    vx * px,
+                    vy * py,
+                    vz * pz,
+                    vx * py + vy * px,
+                    vx * pz + vz * px,
+                    vy * pz + vz * py,
+                )
+                for n, term in enumerate(terms):
+                    total[k][n] += term
         return total
 
     for (low, count, start), slope in zip(spans, slopes):
-        each_slot(low, count, blocks, width, cols, result, functools.partial(group, slope, start), 1)
+        each_slot(low, count, blocks, width, cols, result, functools.partial(group, slope, start), 1, 4)
     sums = jnp.transpose(result[...])
     for n in range(9):
         out[n] = sums[n * blocks : (n + 1) * blocks, 0:width]

time: 51.2 us -> 50.7 us (level)
  Pallas kernels: 21.7 us -> 21.1 us
where the time goes in v7:
time: 50.7 us; the launch traced here: 50.2 us
  Pallas kernels  21.1 us (42%)
  starting transfers between devices  18.1 us (36%)
  waiting for transfers between devices  10.2 us (20%)
  between operations  0.72 us (1%)
    ppermute x9, starting transfers between devices, exchange(): seg.append(lax.ppermute(own, 'seg', [(i, i ^ k) for i in range(groups)]))  8.66 us
    ppermute x9, waiting for transfers between devices, exchange(): seg.append(lax.ppermute(own, 'seg', [(i, i ^ k) for i in range(groups)]))  7.78 us
    ppermute x3, starting transfers between devices, exchange(): near = lax.ppermute(whole, 'dom', first)  5.94 us
    pallas_call x2, Pallas kernels, step(): call(functools.partial(moment_body, blocks, width, tiles, parts), shape(9...  4.83 us
    pallas_call x1, Pallas kernels, step(): call(functools.partial(density_body, groups, blocks, width, tiles), (shap...  4.54 us
    pallas_call x2, Pallas kernels, step(): call(functools.partial(factor_body, low, count, blocks, slab, width, tile...  4.53 us
    pallas_call x1, Pallas kernels, step(): call(functools.partial(update_body, spans, len(moments), groups, blocks,...  3.69 us
    ppermute x3, starting transfers between devices, exchange(): beside = lax.ppermute(whole, ('dom', 'seg'), second)  3.53 us
  transfers between devices with their start and end apart: 15, of which 7 were waited for; matrix products, arithmetic and copies ran while one was open for 0% of the time, Pallas kernels for 20%

profile of v7, /device:TPU:1, one launch (start us, length us, event | category | flops | bytes accessed | tf_op | source)
XLA Modules:
  0.0 50.2 jit_solution(17866909355100396237)
XLA Ops:
  0.6 0.9 %shard_map.59.refs_0_.refs_3_ = f32[48,128]{1,0:T(8,128)S(1)} custom-call(s32[8]{0:T(128)} %refs_0_.1, s32[8]{0:T(128)} %refs_1_.1, f32[9,8,64]{2,1,0:T(8,128)} %bitcast.3, s32[8,26]{1,0:T(8,128)} %refs_3_.1), custom_call_target="tpu_custom_call" | custom-call | tf_op jit(solution)/shard_map/pallas_call | solution.py:494
  1.6 2.1 %collective-permute-start = (f32[48,128]{1,0:T(8,128)S(1)}, f32[48,128]{1,0:T(8,128)S(1)}, u32[]{:S(2)}, u32[]{:S(2)}) collective-permute-start(f32[48,128]{1,0:T(8,128)S(1)} %shard_map.59.refs_0_.refs_3_), channel_id=1, source_target_pairs={{0,1},{1,0},{2,3},{3,2},{4,5},{5,4},{6,7},{7,6},{8,9},{9,8},{10,11... | collective-permute-start | bytes 73736 | tf_op jit(solution)/shard_map/ppermute | solution.py:463
  3.6 1.2 %collective-permute-start.1 = (f32[48,128]{1,0:T(8,128)S(1)}, f32[48,128]{1,0:T(8,128)S(1)}, u32[]{:S(2)}, u32[]{:S(2)}) collective-permute-start(f32[48,128]{1,0:T(8,128)S(1)} %shard_map.59.refs_0_.refs_3_), channel_id=1, source_target_pairs={{0,2},{1,3},{2,0},{3,1},{4,6},{5,7},{6,4},{7,5},{8,10},{9,11},{10,... | collective-permute-start | bytes 73736 | tf_op jit(solution)/shard_map/ppermute | solution.py:463
  4.9 0.0 collective-permute-start.2
  4.9 1.4 %collective-permute-done.1.refs_2_.refs_5_ = f32[48,128]{1,0:T(8,128)S(1)} collective-permute-done((f32[48,128]{1,0:T(8,128)S(1)}, f32[48,128]{1,0:T(8,128)S(1)}, u32[]{:S(2)}, u32[]{:S(2)}) %collective-permute-start.1) | collective-permute-done | bytes 24608 | tf_op jit(solution)/shard_map/ppermute | solution.py:463
  6.3 2.1 %collective-permute-done.2.refs_3_.refs_6_ = f32[48,128]{1,0:T(8,128)S(1)} collective-permute-done((f32[48,128]{1,0:T(8,128)S(1)}, f32[48,128]{1,0:T(8,128)S(1)}, u32[]{:S(2)}, u32[]{:S(2)}) %collective-permute-start.2) | collective-permute-done | bytes 24608 | tf_op jit(solution)/shard_map/ppermute | solution.py:463
  8.5 2.5 %collective-permute-start.3 = (f32[160,128]{1,0:T(8,128)S(1)}, f32[160,128]{1,0:T(8,128)S(1)}, u32[]{:S(2)}, u32[]{:S(2)}) collective-permute-start(f32[160,128]{1,0:T(8,128)S(1)} %pad_maximum_fusion), channel_id=1, source_target_pairs={{0,4},{4,0},{8,12},{12,8},{16,20},{20,16},{24,28},{28,24},{1,5},{5... | collective-permute-start | bytes 245768 | tf_op jit(solution)/shard_map/ppermute | solution.py:472
  10.9 1.3 %collective-permute-start.4 = (f32[160,128]{1,0:T(8,128)S(1)}, f32[160,128]{1,0:T(8,128)S(1)}, u32[]{:S(2)}, u32[]{:S(2)}) collective-permute-start(f32[160,128]{1,0:T(8,128)S(1)} %pad_maximum_fusion), channel_id=1, source_target_pairs={{0,1},{1,0},{2,3},{3,2},{4,8},{5,9},{6,10},{7,11},{8,4},{9,5},{10,... | collective-permute-start | bytes 245768 | tf_op jit(solution)/shard_map/ppermute | solution.py:473
  12.2 0.5 shard_map.60
  12.6 0.0 collective-permute-done.3.refs_7_
  12.6 2.4 %collective-permute-done.4.refs_8_ = f32[160,128]{1,0:T(8,128)S(1)} collective-permute-done((f32[160,128]{1,0:T(8,128)S(1)}, f32[160,128]{1,0:T(8,128)S(1)}, u32[]{:S(2)}, u32[]{:S(2)}) %collective-permute-start.4) | collective-permute-done | bytes 81952 | tf_op jit(solution)/shard_map/ppermute | solution.py:473
  15.1 4.5 %shard_map.61 = (f32[8,128]{1,0:T(8,128)S(1)}, f32[8,64]{1,0:T(8,128)}, f32[896,128]{1,0:T(8,128)S(1)}, f32[128,128]{1,0:T(8,128)S(1)}, f32[8,8,14,8,128]{4,3,2,1,0:T(8,128)S(1)}) custom-call(f32[64,128]{1,0:T(8,128)S(1)} %get-tuple-element.17.refs_0_.refs_1_.cols, f32[11,8,128]{2,1,0:T(8,128)S(1)} %get-tuple-element.18.refs_1_, ...), custom_call_target="tpu_custom_call" | custom-call | tf_op jit(solution)/shard_map/pallas_call | solution.py:522
  19.6 0.3 collective-permute-start.5
  19.9 2.4 %collective-permute-start.7 = (f32[8,128]{1,0:T(8,128)S(1)}, f32[8,128]{1,0:T(8,128)S(1)}, u32[]{:S(2)}, u32[]{:S(2)}) collective-permute-start(f32[8,128]{1,0:T(8,128)S(1)} %get-tuple-element.27.refs_6_), channel_id=1, source_target_pairs={{0,3},{1,2},{2,1},{3,0},{4,7},{5,6},{6,5},{7,4},{8,11},{9,10},{10,... | collective-permute-start | bytes 12296 | tf_op jit(solution)/shard_map/ppermute | solution.py:463
  22.2 0.0 collective-permute-done.5.refs_7_
  22.2 0.1 collective-permute-done.6.refs_8_
  22.3 0.9 %collective-permute-done.7.refs_9_ = f32[8,128]{1,0:T(8,128)S(1)} collective-permute-done((f32[8,128]{1,0:T(8,128)S(1)}, f32[8,128]{1,0:T(8,128)S(1)}, u32[]{:S(2)}, u32[]{:S(2)}) %collective-permute-start.7) | collective-permute-done | bytes 4128 | tf_op jit(solution)/shard_map/ppermute | solution.py:463
  23.2 1.8 %collective-permute-start.8 = (f32[32,128]{1,0:T(8,128)S(1)}, f32[32,128]{1,0:T(8,128)S(1)}, u32[]{:S(2)}, u32[]{:S(2)}) collective-permute-start(f32[32,128]{1,0:T(8,128)S(1)} %constant_dynamic-update-slice_fusion), channel_id=1, source_target_pairs={{0,4},{4,0},{8,12},{12,8},{16,20},{20,16},{24,28},{28,24},{1,5},{5... | collective-permute-start | bytes 49160 | tf_op jit(solution)/shard_map/ppermute | solution.py:472
  25.1 1.1 %collective-permute-start.9 = (f32[32,128]{1,0:T(8,128)S(1)}, f32[32,128]{1,0:T(8,128)S(1)}, u32[]{:S(2)}, u32[]{:S(2)}) collective-permute-start(f32[32,128]{1,0:T(8,128)S(1)} %constant_dynamic-update-slice_fusion), channel_id=1, source_target_pairs={{0,1},{1,0},{2,3},{3,2},{4,8},{5,9},{6,10},{7,11},{8,4},{9,5},{10,... | collective-permute-start | bytes 49160 | tf_op jit(solution)/shard_map/ppermute | solution.py:473
  26.2 1.6 %shard_map.63 = (f32[3,3,8,14,8,128]{5,4,3,2,1,0:T(8,128)S(1)}, f32[6,3,8,14,8,128]{5,4,3,2,1,0:T(8,128)S(1)}) custom-call(f32[896,128]{1,0:T(8,128)S(1)} %get-tuple-element.20.refs_0_.far, f32[64,128]{1,0:T(8,128)S(1)} %get-tuple-element.17.refs_0_.refs_1_.cols, f32[8,8,14,8,128]{4,3,2,1,0:T(8,128)S(1)} %get-tuple-element.21.refs_2_), custom_call_target="tpu_custom_call" | custom-call | tf_op jit(solution)/shard_map/pallas_call | solution.py:543
  27.8 2.9 %shard_map.62 = (f32[3,5,8,14,8,128]{5,4,3,2,1,0:T(8,128)S(1)}, f32[6,5,8,14,8,128]{5,4,3,2,1,0:T(8,128)S(1)}, f32[224,128]{1,0:T(8,128)S(1)}) custom-call(f32[896,128]{1,0:T(8,128)S(1)} %get-tuple-element.20.refs_0_.far, f32[64,128]{1,0:T(8,128)S(1)} %get-tuple-element.17.refs_0_.refs_1_.cols, f32[8,8,14,8,128]{4,3,2,1,0:T(8,128)S(1)} %get-tuple-element.21.refs_2_, ...), custom_call_target="tpu_custom_call" | custom-call | tf_op jit(solution)/shard_map/pallas_call | solution.py:543
  30.7 2.2 %shard_map.64 = (f32[24,128]{1,0:T(8,128)S(1)}, f32[7,8,64]{2,1,0:T(8,128)S(1)}) custom-call(f32[64,128]{1,0:T(8,128)S(1)} %get-tuple-element.17.refs_0_.refs_1_.cols, f32[11,8,128]{2,1,0:T(8,128)S(1)} %get-tuple-element.18.refs_1_, f32[224,128]{1,0:T(8,128)S(1)} %get-tuple-element.23.refs_2_, f32[8,64]{1,0:T(8,128)S(1)} %copy-done, ...), custom_call_target="tpu_custom_call" | custom-call | tf_op jit(solution)/shard_map/pallas_call | solution.py:553
  32.9 1.2 %collective-permute-start.10 = (f32[24,128]{1,0:T(8,128)S(1)}, f32[24,128]{1,0:T(8,128)S(1)}, u32[]{:S(2)}, u32[]{:S(2)}) collective-permute-start(f32[24,128]{1,0:T(8,128)S(1)} %get-tuple-element.31.refs_8_), channel_id=1, source_target_pairs={{0,1},{1,0},{2,3},{3,2},{4,5},{5,4},{6,7},{7,6},{8,9},{9,8},{10,11... | collective-permute-start | bytes 36872 | tf_op jit(solution)/shard_map/ppermute | solution.py:463
  34.1 1.2 %collective-permute-start.11 = (f32[24,128]{1,0:T(8,128)S(1)}, f32[24,128]{1,0:T(8,128)S(1)}, u32[]{:S(2)}, u32[]{:S(2)}) collective-permute-start(f32[24,128]{1,0:T(8,128)S(1)} %get-tuple-element.31.refs_8_), channel_id=1, source_target_pairs={{0,2},{1,3},{2,0},{3,1},{4,6},{5,7},{6,4},{7,5},{8,10},{9,11},{10,... | collective-permute-start | bytes 36872 | tf_op jit(solution)/shard_map/ppermute | solution.py:463
  35.4 0.2 collective-permute-start.12
  35.6 1.1 %collective-permute-done.11.refs_10_ = f32[24,128]{1,0:T(8,128)S(1)} collective-permute-done((f32[24,128]{1,0:T(8,128)S(1)}, f32[24,128]{1,0:T(8,128)S(1)}, u32[]{:S(2)}, u32[]{:S(2)}) %collective-permute-start.11) | collective-permute-done | bytes 12320 | tf_op jit(solution)/shard_map/ppermute | solution.py:463
  36.7 2.1 %collective-permute-done.12.refs_11_ = f32[24,128]{1,0:T(8,128)S(1)} collective-permute-done((f32[24,128]{1,0:T(8,128)S(1)}, f32[24,128]{1,0:T(8,128)S(1)}, u32[]{:S(2)}, u32[]{:S(2)}) %collective-permute-start.12) | collective-permute-done | bytes 12320 | tf_op jit(solution)/shard_map/ppermute | solution.py:463
  38.8 1.6 %collective-permute-start.13 = (f32[96,128]{1,0:T(8,128)S(1)}, f32[96,128]{1,0:T(8,128)S(1)}, u32[]{:S(2)}, u32[]{:S(2)}) collective-permute-start(f32[96,128]{1,0:T(8,128)S(1)} %constant_dynamic-update-slice_fusion.4), channel_id=1, source_target_pairs={{0,4},{4,0},{8,12},{12,8},{16,20},{20,16},{24,28},{28,24},{1,5},{5... | collective-permute-start | bytes 147464 | tf_op jit(solution)/shard_map/ppermute | solution.py:472
  40.5 1.2 %collective-permute-start.14 = (f32[96,128]{1,0:T(8,128)S(1)}, f32[96,128]{1,0:T(8,128)S(1)}, u32[]{:S(2)}, u32[]{:S(2)}) collective-permute-start(f32[96,128]{1,0:T(8,128)S(1)} %constant_dynamic-update-slice_fusion.4), channel_id=1, source_target_pairs={{0,1},{1,0},{2,3},{3,2},{4,8},{5,9},{6,10},{7,11},{8,4},{9,5},{10,... | collective-permute-start | bytes 147464 | tf_op jit(solution)/shard_map/ppermute | solution.py:473
  41.7 2.4 %shard_map.65.refs_6_ = f32[9,8,64]{2,1,0:T(8,128)S(1)} custom-call(f32[896,128]{1,0:T(8,128)S(1)} %get-tuple-element.20.refs_0_.far, f32[64,128]{1,0:T(8,128)S(1)} %get-tuple-element.17.refs_0_.refs_1_.cols, f32[3,5,8,14,8,128]{5,4,3,2,1,0:T(8,128)S(1)} %get-tuple-element.29.refs_0_.refs_4_), custom_call_target="tpu_custom_call" | custom-call | tf_op jit(solution)/shard_map/pallas_call | solution.py:570
  44.1 2.4 %shard_map.66.refs_7_ = f32[9,8,64]{2,1,0:T(8,128)S(1)} custom-call(f32[896,128]{1,0:T(8,128)S(1)} %get-tuple-element.20.refs_0_.far, f32[64,128]{1,0:T(8,128)S(1)} %get-tuple-element.17.refs_0_.refs_1_.cols, f32[3,5,8,14,8,128]{5,4,3,2,1,0:T(8,128)S(1)} %get-tuple-element.29.refs_0_.refs_4_, f32[3,3,8,14,8,128]{5,4,3,2,1,0:T(8,128)S(1)} %get-tuple-element.30.refs_1_.refs_5_), custom_call_target="tpu_custom_call" | custom-call | tf_op jit(solution)/shard_map/pallas_call | solution.py:570
  46.5 3.7 %shard_map.67 = f32[9,8,64]{2,1,0:T(8,128)} custom-call(f32[64,128]{1,0:T(8,128)S(1)} %get-tuple-element.17.refs_0_.refs_1_.cols, f32[11,8,128]{2,1,0:T(8,128)S(1)} %get-tuple-element.18.refs_1_, f32[224,128]{1,0:T(8,128)S(1)} %get-tuple-element.23.refs_2_, f32[7,8,64]{2,1,0:T(8,128)S(1)} %get-tuple-element.28.refs_3_, ...), custom_call_target="tpu_custom_call" | custom-call | tf_op jit(solution)/shard_map/pallas_call | solution.py:578
  (22 shorter events, 0.1 us)
Async XLA Ops:
  1.6 3.4 %collective-permute-start = (f32[48,128]{1,0:T(8,128)S(1)}, f32[48,128]{1,0:T(8,128)S(1)}, u32[]{:S(2)}, u32[]{:S(2)}) collective-permute-start(f32[48,128]{1,0:T(8,128)S(1)} %shard_map.59.refs_0_.refs_3_), channel_id=1, source_target_pairs={{0,1},{1,0},{2,3},{3,2},{4,5},{5,4},{6,7},{7,6},{8,9},{9,8},{10,11... | collective-permute-start | bytes 73736 | tf_op jit(solution)/shard_map/ppermute | solution.py:463
  3.6 2.7 %collective-permute-start.1 = (f32[48,128]{1,0:T(8,128)S(1)}, f32[48,128]{1,0:T(8,128)S(1)}, u32[]{:S(2)}, u32[]{:S(2)}) collective-permute-start(f32[48,128]{1,0:T(8,128)S(1)} %shard_map.59.refs_0_.refs_3_), channel_id=1, source_target_pairs={{0,2},{1,3},{2,0},{3,1},{4,6},{5,7},{6,4},{7,5},{8,10},{9,11},{10,... | collective-permute-start | bytes 73736 | tf_op jit(solution)/shard_map/ppermute | solution.py:463
  4.9 3.6 %collective-permute-start.2 = (f32[48,128]{1,0:T(8,128)S(1)}, f32[48,128]{1,0:T(8,128)S(1)}, u32[]{:S(2)}, u32[]{:S(2)}) collective-permute-start(f32[48,128]{1,0:T(8,128)S(1)} %shard_map.59.refs_0_.refs_3_), channel_id=1, source_target_pairs={{0,3},{1,2},{2,1},{3,0},{4,7},{5,6},{6,5},{7,4},{8,11},{9,10},{10,... | collective-permute-start | bytes 73736 | tf_op jit(solution)/shard_map/ppermute | solution.py:463
  8.5 4.2 %collective-permute-start.3 = (f32[160,128]{1,0:T(8,128)S(1)}, f32[160,128]{1,0:T(8,128)S(1)}, u32[]{:S(2)}, u32[]{:S(2)}) collective-permute-start(f32[160,128]{1,0:T(8,128)S(1)} %pad_maximum_fusion), channel_id=1, source_target_pairs={{0,4},{4,0},{8,12},{12,8},{16,20},{20,16},{24,28},{28,24},{1,5},{5... | collective-permute-start | bytes 245768 | tf_op jit(solution)/shard_map/ppermute | solution.py:472
  10.9 4.1 %collective-permute-start.4 = (f32[160,128]{1,0:T(8,128)S(1)}, f32[160,128]{1,0:T(8,128)S(1)}, u32[]{:S(2)}, u32[]{:S(2)}) collective-permute-start(f32[160,128]{1,0:T(8,128)S(1)} %pad_maximum_fusion), channel_id=1, source_target_pairs={{0,1},{1,0},{2,3},{3,2},{4,8},{5,9},{6,10},{7,11},{8,4},{9,5},{10,... | collective-permute-start | bytes 245768 | tf_op jit(solution)/shard_map/ppermute | solution.py:473
  19.6 11.1 %copy-start = (f32[8,64]{1,0:T(8,128)S(1)}, f32[8,64]{1,0:T(8,128)}, u32[]{:S(2)}) copy-start(f32[8,64]{1,0:T(8,128)} %get-tuple-element.16.refs_3_) | copy-start | bytes 6148
  19.6 2.7 %collective-permute-start.5 = (f32[8,128]{1,0:T(8,128)S(1)}, f32[8,128]{1,0:T(8,128)S(1)}, u32[]{:S(2)}, u32[]{:S(2)}) collective-permute-start(f32[8,128]{1,0:T(8,128)S(1)} %get-tuple-element.27.refs_6_), channel_id=1, source_target_pairs={{0,1},{1,0},{2,3},{3,2},{4,5},{5,4},{6,7},{7,6},{8,9},{9,8},{10,11... | collective-permute-start | bytes 12296 | tf_op jit(solution)/shard_map/ppermute | solution.py:463
  19.9 2.5 %collective-permute-start.6 = (f32[8,128]{1,0:T(8,128)S(1)}, f32[8,128]{1,0:T(8,128)S(1)}, u32[]{:S(2)}, u32[]{:S(2)}) collective-permute-start(f32[8,128]{1,0:T(8,128)S(1)} %get-tuple-element.27.refs_6_), channel_id=1, source_target_pairs={{0,2},{1,3},{2,0},{3,1},{4,6},{5,7},{6,4},{7,5},{8,10},{9,11},{10,... | collective-permute-start | bytes 12296 | tf_op jit(solution)/shard_map/ppermute | solution.py:463
  19.9 3.4 %collective-permute-start.7 = (f32[8,128]{1,0:T(8,128)S(1)}, f32[8,128]{1,0:T(8,128)S(1)}, u32[]{:S(2)}, u32[]{:S(2)}) collective-permute-start(f32[8,128]{1,0:T(8,128)S(1)} %get-tuple-element.27.refs_6_), channel_id=1, source_target_pairs={{0,3},{1,2},{2,1},{3,0},{4,7},{5,6},{6,5},{7,4},{8,11},{9,10},{10,... | collective-permute-start | bytes 12296 | tf_op jit(solution)/shard_map/ppermute | solution.py:463
  23.2 7.5 %collective-permute-start.8 = (f32[32,128]{1,0:T(8,128)S(1)}, f32[32,128]{1,0:T(8,128)S(1)}, u32[]{:S(2)}, u32[]{:S(2)}) collective-permute-start(f32[32,128]{1,0:T(8,128)S(1)} %constant_dynamic-update-slice_fusion), channel_id=1, source_target_pairs={{0,4},{4,0},{8,12},{12,8},{16,20},{20,16},{24,28},{28,24},{1,5},{5... | collective-permute-start | bytes 49160 | tf_op jit(solution)/shard_map/ppermute | solution.py:472
  25.1 5.6 %collective-permute-start.9 = (f32[32,128]{1,0:T(8,128)S(1)}, f32[32,128]{1,0:T(8,128)S(1)}, u32[]{:S(2)}, u32[]{:S(2)}) collective-permute-start(f32[32,128]{1,0:T(8,128)S(1)} %constant_dynamic-update-slice_fusion), channel_id=1, source_target_pairs={{0,1},{1,0},{2,3},{3,2},{4,8},{5,9},{6,10},{7,11},{8,4},{9,5},{10,... | collective-permute-start | bytes 49160 | tf_op jit(solution)/shard_map/ppermute | solution.py:473
  32.9 2.7 %collective-permute-start.10 = (f32[24,128]{1,0:T(8,128)S(1)}, f32[24,128]{1,0:T(8,128)S(1)}, u32[]{:S(2)}, u32[]{:S(2)}) collective-permute-start(f32[24,128]{1,0:T(8,128)S(1)} %get-tuple-element.31.refs_8_), channel_id=1, source_target_pairs={{0,1},{1,0},{2,3},{3,2},{4,5},{5,4},{6,7},{7,6},{8,9},{9,8},{10,11... | collective-permute-start | bytes 36872 | tf_op jit(solution)/shard_map/ppermute | solution.py:463
  34.1 2.5 %collective-permute-start.11 = (f32[24,128]{1,0:T(8,128)S(1)}, f32[24,128]{1,0:T(8,128)S(1)}, u32[]{:S(2)}, u32[]{:S(2)}) collective-permute-start(f32[24,128]{1,0:T(8,128)S(1)} %get-tuple-element.31.refs_8_), channel_id=1, source_target_pairs={{0,2},{1,3},{2,0},{3,1},{4,6},{5,7},{6,4},{7,5},{8,10},{9,11},{10,... | collective-permute-start | bytes 36872 | tf_op jit(solution)/shard_map/ppermute | solution.py:463
  35.4 3.4 %collective-permute-start.12 = (f32[24,128]{1,0:T(8,128)S(1)}, f32[24,128]{1,0:T(8,128)S(1)}, u32[]{:S(2)}, u32[]{:S(2)}) collective-permute-start(f32[24,128]{1,0:T(8,128)S(1)} %get-tuple-element.31.refs_8_), channel_id=1, source_target_pairs={{0,3},{1,2},{2,1},{3,0},{4,7},{5,6},{6,5},{7,4},{8,11},{9,10},{10,... | collective-permute-start | bytes 36872 | tf_op jit(solution)/shard_map/ppermute | solution.py:463
  38.8 7.7 %collective-permute-start.13 = (f32[96,128]{1,0:T(8,128)S(1)}, f32[96,128]{1,0:T(8,128)S(1)}, u32[]{:S(2)}, u32[]{:S(2)}) collective-permute-start(f32[96,128]{1,0:T(8,128)S(1)} %constant_dynamic-update-slice_fusion.4), channel_id=1, source_target_pairs={{0,4},{4,0},{8,12},{12,8},{16,20},{20,16},{24,28},{28,24},{1,5},{5... | collective-permute-start | bytes 147464 | tf_op jit(solution)/shard_map/ppermute | solution.py:472
  40.5 6.1 %collective-permute-start.14 = (f32[96,128]{1,0:T(8,128)S(1)}, f32[96,128]{1,0:T(8,128)S(1)}, u32[]{:S(2)}, u32[]{:S(2)}) collective-permute-start(f32[96,128]{1,0:T(8,128)S(1)} %constant_dynamic-update-slice_fusion.4), channel_id=1, source_target_pairs={{0,1},{1,0},{2,3},{3,2},{4,8},{5,9},{6,10},{7,11},{8,4},{9,5},{10,... | collective-permute-start | bytes 147464 | tf_op jit(solution)/shard_map/ppermute | solution.py:473

commit v8 on v7

--- a/solution.py
+++ b/solution.py
@@ -422,18 +422,19 @@
 
     far_fields(left, right, keep)
 
-    def group(slope, d, at, g, own):
-        total = [jnp.zeros((SUB, LANES), jnp.float32) for _ in range(3)]
+    def group(slope, d, at, low, owns):
+        total = [[jnp.zeros((SUB, LANES), jnp.float32) for _ in range(3)] for _ in owns]
         for t in range(tiles):
-            ex, ey, ez = [slope[a, d, g, t] for a in range(3)]
             xx, yy, zz, xy, xz, yz = [far_row(far_coef, n, tiles, at, t) for n in range(6)]
-            total[0] += xx * ex + xy * ey + xz * ez
-            total[1] += xy * ex + yy * ey + yz * ez
-            total[2] += xz * ex + yz * ey + zz * ez
+            for k in range(len(owns)):
+                ex, ey, ez = [slope[a, d, low + k, t] for a in range(3)]
+                total[k][0] += xx * ex + xy * ey + xz * ez
+                total[k][1] += xy * ex + yy * ey + yz * ez
+                total[k][2] += xz * ex + yz * ey + zz * ez
         return total
 
     for (first, count), slope in zip(spans, slopes):
-        each_slot(first, count, blocks, width, cols, result, functools.partial(group, slope))
+        each_slot(first, count, blocks, width, cols, result, functools.partial(group, slope), 2, 8)
     moments = [sum(piece[m] for piece in pieces) for m in range(9)]
     sums = jnp.transpose(result[...])
     field = lambda n: own_rows[n, :, 0:width]

time: 50.7 us -> 50.7 us (level)
  no operation moved by 1% of the time
where the time goes in v8:
time: 50.7 us; the launch traced here: 50.2 us
  Pallas kernels  21.1 us (42%)
  starting transfers between devices  18.1 us (36%)
  waiting for transfers between devices  10.2 us (20%)
  between operations  0.72 us (1%)
    ppermute x9, starting transfers between devices, exchange(): seg.append(lax.ppermute(own, 'seg', [(i, i ^ k) for i in range(groups)]))  8.66 us
    ppermute x9, waiting for transfers between devices, exchange(): seg.append(lax.ppermute(own, 'seg', [(i, i ^ k) for i in range(groups)]))  7.78 us
    ppermute x3, starting transfers between devices, exchange(): near = lax.ppermute(whole, 'dom', first)  5.94 us
    pallas_call x2, Pallas kernels, step(): call(functools.partial(moment_body, blocks, width, tiles, parts), shape(9...  4.83 us
    pallas_call x1, Pallas kernels, step(): call(functools.partial(density_body, groups, blocks, width, tiles), (shap...  4.54 us
    pallas_call x2, Pallas kernels, step(): call(functools.partial(factor_body, low, count, blocks, slab, width, tile...  4.53 us
    pallas_call x1, Pallas kernels, step(): call(functools.partial(update_body, spans, len(moments), groups, blocks,...  3.69 us
    ppermute x3, starting transfers between devices, exchange(): beside = lax.ppermute(whole, ('dom', 'seg'), second)  3.53 us
  transfers between devices with their start and end apart: 15, of which 7 were waited for; matrix products, arithmetic and copies ran while one was open for 0% of the time, Pallas kernels for 20%

profile of v8, /device:TPU:1, one launch (start us, length us, event | category | flops | bytes accessed | tf_op | source)
XLA Modules:
  0.0 50.2 jit_solution(7494025082428615619)
XLA Ops:
  0.6 0.9 %shard_map.59.refs_0_.refs_3_ = f32[48,128]{1,0:T(8,128)S(1)} custom-call(s32[8]{0:T(128)} %refs_0_.1, s32[8]{0:T(128)} %refs_1_.1, f32[9,8,64]{2,1,0:T(8,128)} %bitcast.3, s32[8,26]{1,0:T(8,128)} %refs_3_.1), custom_call_target="tpu_custom_call" | custom-call | tf_op jit(solution)/shard_map/pallas_call | solution.py:495
  1.6 2.1 %collective-permute-start = (f32[48,128]{1,0:T(8,128)S(1)}, f32[48,128]{1,0:T(8,128)S(1)}, u32[]{:S(2)}, u32[]{:S(2)}) collective-permute-start(f32[48,128]{1,0:T(8,128)S(1)} %shard_map.59.refs_0_.refs_3_), channel_id=1, source_target_pairs={{0,1},{1,0},{2,3},{3,2},{4,5},{5,4},{6,7},{7,6},{8,9},{9,8},{10,11... | collective-permute-start | bytes 73736 | tf_op jit(solution)/shard_map/ppermute | solution.py:464
  3.6 1.2 %collective-permute-start.1 = (f32[48,128]{1,0:T(8,128)S(1)}, f32[48,128]{1,0:T(8,128)S(1)}, u32[]{:S(2)}, u32[]{:S(2)}) collective-permute-start(f32[48,128]{1,0:T(8,128)S(1)} %shard_map.59.refs_0_.refs_3_), channel_id=1, source_target_pairs={{0,2},{1,3},{2,0},{3,1},{4,6},{5,7},{6,4},{7,5},{8,10},{9,11},{10,... | collective-permute-start | bytes 73736 | tf_op jit(solution)/shard_map/ppermute | solution.py:464
  4.9 0.0 collective-permute-start.2
  4.9 1.4 %collective-permute-done.1.refs_2_.refs_5_ = f32[48,128]{1,0:T(8,128)S(1)} collective-permute-done((f32[48,128]{1,0:T(8,128)S(1)}, f32[48,128]{1,0:T(8,128)S(1)}, u32[]{:S(2)}, u32[]{:S(2)}) %collective-permute-start.1) | collective-permute-done | bytes 24608 | tf_op jit(solution)/shard_map/ppermute | solution.py:464
  6.3 2.1 %collective-permute-done.2.refs_3_.refs_6_ = f32[48,128]{1,0:T(8,128)S(1)} collective-permute-done((f32[48,128]{1,0:T(8,128)S(1)}, f32[48,128]{1,0:T(8,128)S(1)}, u32[]{:S(2)}, u32[]{:S(2)}) %collective-permute-start.2) | collective-permute-done | bytes 24608 | tf_op jit(solution)/shard_map/ppermute | solution.py:464
  8.5 2.5 %collective-permute-start.3 = (f32[160,128]{1,0:T(8,128)S(1)}, f32[160,128]{1,0:T(8,128)S(1)}, u32[]{:S(2)}, u32[]{:S(2)}) collective-permute-start(f32[160,128]{1,0:T(8,128)S(1)} %pad_maximum_fusion), channel_id=1, source_target_pairs={{0,4},{4,0},{8,12},{12,8},{16,20},{20,16},{24,28},{28,24},{1,5},{5... | collective-permute-start | bytes 245768 | tf_op jit(solution)/shard_map/ppermute | solution.py:473
  10.9 1.3 %collective-permute-start.4 = (f32[160,128]{1,0:T(8,128)S(1)}, f32[160,128]{1,0:T(8,128)S(1)}, u32[]{:S(2)}, u32[]{:S(2)}) collective-permute-start(f32[160,128]{1,0:T(8,128)S(1)} %pad_maximum_fusion), channel_id=1, source_target_pairs={{0,1},{1,0},{2,3},{3,2},{4,8},{5,9},{6,10},{7,11},{8,4},{9,5},{10,... | collective-permute-start | bytes 245768 | tf_op jit(solution)/shard_map/ppermute | solution.py:474
  12.2 0.5 shard_map.60
  12.6 0.0 collective-permute-done.3.refs_7_
  12.6 2.4 %collective-permute-done.4.refs_8_ = f32[160,128]{1,0:T(8,128)S(1)} collective-permute-done((f32[160,128]{1,0:T(8,128)S(1)}, f32[160,128]{1,0:T(8,128)S(1)}, u32[]{:S(2)}, u32[]{:S(2)}) %collective-permute-start.4) | collective-permute-done | bytes 81952 | tf_op jit(solution)/shard_map/ppermute | solution.py:474
  15.1 4.5 %shard_map.61 = (f32[8,128]{1,0:T(8,128)S(1)}, f32[8,64]{1,0:T(8,128)}, f32[896,128]{1,0:T(8,128)S(1)}, f32[128,128]{1,0:T(8,128)S(1)}, f32[8,8,14,8,128]{4,3,2,1,0:T(8,128)S(1)}) custom-call(f32[64,128]{1,0:T(8,128)S(1)} %get-tuple-element.17.refs_0_.refs_1_.cols, f32[11,8,128]{2,1,0:T(8,128)S(1)} %get-tuple-element.18.refs_1_, ...), custom_call_target="tpu_custom_call" | custom-call | tf_op jit(solution)/shard_map/pallas_call | solution.py:523
  19.6 0.3 collective-permute-start.5
  19.9 2.4 %collective-permute-start.7 = (f32[8,128]{1,0:T(8,128)S(1)}, f32[8,128]{1,0:T(8,128)S(1)}, u32[]{:S(2)}, u32[]{:S(2)}) collective-permute-start(f32[8,128]{1,0:T(8,128)S(1)} %get-tuple-element.27.refs_6_), channel_id=1, source_target_pairs={{0,3},{1,2},{2,1},{3,0},{4,7},{5,6},{6,5},{7,4},{8,11},{9,10},{10,... | collective-permute-start | bytes 12296 | tf_op jit(solution)/shard_map/ppermute | solution.py:464
  22.2 0.0 collective-permute-done.5.refs_7_
  22.2 0.1 collective-permute-done.6.refs_8_
  22.3 0.9 %collective-permute-done.7.refs_9_ = f32[8,128]{1,0:T(8,128)S(1)} collective-permute-done((f32[8,128]{1,0:T(8,128)S(1)}, f32[8,128]{1,0:T(8,128)S(1)}, u32[]{:S(2)}, u32[]{:S(2)}) %collective-permute-start.7) | collective-permute-done | bytes 4128 | tf_op jit(solution)/shard_map/ppermute | solution.py:464
  23.2 1.8 %collective-permute-start.8 = (f32[32,128]{1,0:T(8,128)S(1)}, f32[32,128]{1,0:T(8,128)S(1)}, u32[]{:S(2)}, u32[]{:S(2)}) collective-permute-start(f32[32,128]{1,0:T(8,128)S(1)} %constant_dynamic-update-slice_fusion), channel_id=1, source_target_pairs={{0,4},{4,0},{8,12},{12,8},{16,20},{20,16},{24,28},{28,24},{1,5},{5... | collective-permute-start | bytes 49160 | tf_op jit(solution)/shard_map/ppermute | solution.py:473
  25.1 1.1 %collective-permute-start.9 = (f32[32,128]{1,0:T(8,128)S(1)}, f32[32,128]{1,0:T(8,128)S(1)}, u32[]{:S(2)}, u32[]{:S(2)}) collective-permute-start(f32[32,128]{1,0:T(8,128)S(1)} %constant_dynamic-update-slice_fusion), channel_id=1, source_target_pairs={{0,1},{1,0},{2,3},{3,2},{4,8},{5,9},{6,10},{7,11},{8,4},{9,5},{10,... | collective-permute-start | bytes 49160 | tf_op jit(solution)/shard_map/ppermute | solution.py:474
  26.2 1.6 %shard_map.63 = (f32[3,3,8,14,8,128]{5,4,3,2,1,0:T(8,128)S(1)}, f32[6,3,8,14,8,128]{5,4,3,2,1,0:T(8,128)S(1)}) custom-call(f32[896,128]{1,0:T(8,128)S(1)} %get-tuple-element.20.refs_0_.far, f32[64,128]{1,0:T(8,128)S(1)} %get-tuple-element.17.refs_0_.refs_1_.cols, f32[8,8,14,8,128]{4,3,2,1,0:T(8,128)S(1)} %get-tuple-element.21.refs_2_), custom_call_target="tpu_custom_call" | custom-call | tf_op jit(solution)/shard_map/pallas_call | solution.py:544
  27.8 2.9 %shard_map.62 = (f32[3,5,8,14,8,128]{5,4,3,2,1,0:T(8,128)S(1)}, f32[6,5,8,14,8,128]{5,4,3,2,1,0:T(8,128)S(1)}, f32[224,128]{1,0:T(8,128)S(1)}) custom-call(f32[896,128]{1,0:T(8,128)S(1)} %get-tuple-element.20.refs_0_.far, f32[64,128]{1,0:T(8,128)S(1)} %get-tuple-element.17.refs_0_.refs_1_.cols, f32[8,8,14,8,128]{4,3,2,1,0:T(8,128)S(1)} %get-tuple-element.21.refs_2_, ...), custom_call_target="tpu_custom_call" | custom-call | tf_op jit(solution)/shard_map/pallas_call | solution.py:544
  30.7 2.2 %shard_map.64 = (f32[24,128]{1,0:T(8,128)S(1)}, f32[7,8,64]{2,1,0:T(8,128)S(1)}) custom-call(f32[64,128]{1,0:T(8,128)S(1)} %get-tuple-element.17.refs_0_.refs_1_.cols, f32[11,8,128]{2,1,0:T(8,128)S(1)} %get-tuple-element.18.refs_1_, f32[224,128]{1,0:T(8,128)S(1)} %get-tuple-element.23.refs_2_, f32[8,64]{1,0:T(8,128)S(1)} %copy-done, ...), custom_call_target="tpu_custom_call" | custom-call | tf_op jit(solution)/shard_map/pallas_call | solution.py:554
  32.9 1.2 %collective-permute-start.10 = (f32[24,128]{1,0:T(8,128)S(1)}, f32[24,128]{1,0:T(8,128)S(1)}, u32[]{:S(2)}, u32[]{:S(2)}) collective-permute-start(f32[24,128]{1,0:T(8,128)S(1)} %get-tuple-element.31.refs_8_), channel_id=1, source_target_pairs={{0,1},{1,0},{2,3},{3,2},{4,5},{5,4},{6,7},{7,6},{8,9},{9,8},{10,11... | collective-permute-start | bytes 36872 | tf_op jit(solution)/shard_map/ppermute | solution.py:464
  34.1 1.2 %collective-permute-start.11 = (f32[24,128]{1,0:T(8,128)S(1)}, f32[24,128]{1,0:T(8,128)S(1)}, u32[]{:S(2)}, u32[]{:S(2)}) collective-permute-start(f32[24,128]{1,0:T(8,128)S(1)} %get-tuple-element.31.refs_8_), channel_id=1, source_target_pairs={{0,2},{1,3},{2,0},{3,1},{4,6},{5,7},{6,4},{7,5},{8,10},{9,11},{10,... | collective-permute-start | bytes 36872 | tf_op jit(solution)/shard_map/ppermute | solution.py:464
  35.4 0.2 collective-permute-start.12
  35.6 1.1 %collective-permute-done.11.refs_10_ = f32[24,128]{1,0:T(8,128)S(1)} collective-permute-done((f32[24,128]{1,0:T(8,128)S(1)}, f32[24,128]{1,0:T(8,128)S(1)}, u32[]{:S(2)}, u32[]{:S(2)}) %collective-permute-start.11) | collective-permute-done | bytes 12320 | tf_op jit(solution)/shard_map/ppermute | solution.py:464
  36.7 2.1 %collective-permute-done.12.refs_11_ = f32[24,128]{1,0:T(8,128)S(1)} collective-permute-done((f32[24,128]{1,0:T(8,128)S(1)}, f32[24,128]{1,0:T(8,128)S(1)}, u32[]{:S(2)}, u32[]{:S(2)}) %collective-permute-start.12) | collective-permute-done | bytes 12320 | tf_op jit(solution)/shard_map/ppermute | solution.py:464
  38.8 1.6 %collective-permute-start.13 = (f32[96,128]{1,0:T(8,128)S(1)}, f32[96,128]{1,0:T(8,128)S(1)}, u32[]{:S(2)}, u32[]{:S(2)}) collective-permute-start(f32[96,128]{1,0:T(8,128)S(1)} %constant_dynamic-update-slice_fusion.4), channel_id=1, source_target_pairs={{0,4},{4,0},{8,12},{12,8},{16,20},{20,16},{24,28},{28,24},{1,5},{5... | collective-permute-start | bytes 147464 | tf_op jit(solution)/shard_map/ppermute | solution.py:473
  40.5 1.2 %collective-permute-start.14 = (f32[96,128]{1,0:T(8,128)S(1)}, f32[96,128]{1,0:T(8,128)S(1)}, u32[]{:S(2)}, u32[]{:S(2)}) collective-permute-start(f32[96,128]{1,0:T(8,128)S(1)} %constant_dynamic-update-slice_fusion.4), channel_id=1, source_target_pairs={{0,1},{1,0},{2,3},{3,2},{4,8},{5,9},{6,10},{7,11},{8,4},{9,5},{10,... | collective-permute-start | bytes 147464 | tf_op jit(solution)/shard_map/ppermute | solution.py:474
  41.7 2.4 %shard_map.65.refs_6_ = f32[9,8,64]{2,1,0:T(8,128)S(1)} custom-call(f32[896,128]{1,0:T(8,128)S(1)} %get-tuple-element.20.refs_0_.far, f32[64,128]{1,0:T(8,128)S(1)} %get-tuple-element.17.refs_0_.refs_1_.cols, f32[3,5,8,14,8,128]{5,4,3,2,1,0:T(8,128)S(1)} %get-tuple-element.29.refs_0_.refs_4_), custom_call_target="tpu_custom_call" | custom-call | tf_op jit(solution)/shard_map/pallas_call | solution.py:571
  44.1 2.4 %shard_map.66.refs_7_ = f32[9,8,64]{2,1,0:T(8,128)S(1)} custom-call(f32[896,128]{1,0:T(8,128)S(1)} %get-tuple-element.20.refs_0_.far, f32[64,128]{1,0:T(8,128)S(1)} %get-tuple-element.17.refs_0_.refs_1_.cols, f32[3,5,8,14,8,128]{5,4,3,2,1,0:T(8,128)S(1)} %get-tuple-element.29.refs_0_.refs_4_, f32[3,3,8,14,8,128]{5,4,3,2,1,0:T(8,128)S(1)} %get-tuple-element.30.refs_1_.refs_5_), custom_call_target="tpu_custom_call" | custom-call | tf_op jit(solution)/shard_map/pallas_call | solution.py:571
  46.5 3.7 %shard_map.67 = f32[9,8,64]{2,1,0:T(8,128)} custom-call(f32[64,128]{1,0:T(8,128)S(1)} %get-tuple-element.17.refs_0_.refs_1_.cols, f32[11,8,128]{2,1,0:T(8,128)S(1)} %get-tuple-element.18.refs_1_, f32[224,128]{1,0:T(8,128)S(1)} %get-tuple-element.23.refs_2_, f32[7,8,64]{2,1,0:T(8,128)S(1)} %get-tuple-element.28.refs_3_, ...), custom_call_target="tpu_custom_call" | custom-call | tf_op jit(solution)/shard_map/pallas_call | solution.py:579
  (22 shorter events, 0.1 us)
Async XLA Ops:
  1.6 3.4 %collective-permute-start = (f32[48,128]{1,0:T(8,128)S(1)}, f32[48,128]{1,0:T(8,128)S(1)}, u32[]{:S(2)}, u32[]{:S(2)}) collective-permute-start(f32[48,128]{1,0:T(8,128)S(1)} %shard_map.59.refs_0_.refs_3_), channel_id=1, source_target_pairs={{0,1},{1,0},{2,3},{3,2},{4,5},{5,4},{6,7},{7,6},{8,9},{9,8},{10,11... | collective-permute-start | bytes 73736 | tf_op jit(solution)/shard_map/ppermute | solution.py:464
  3.6 2.7 %collective-permute-start.1 = (f32[48,128]{1,0:T(8,128)S(1)}, f32[48,128]{1,0:T(8,128)S(1)}, u32[]{:S(2)}, u32[]{:S(2)}) collective-permute-start(f32[48,128]{1,0:T(8,128)S(1)} %shard_map.59.refs_0_.refs_3_), channel_id=1, source_target_pairs={{0,2},{1,3},{2,0},{3,1},{4,6},{5,7},{6,4},{7,5},{8,10},{9,11},{10,... | collective-permute-start | bytes 73736 | tf_op jit(solution)/shard_map/ppermute | solution.py:464
  4.9 3.6 %collective-permute-start.2 = (f32[48,128]{1,0:T(8,128)S(1)}, f32[48,128]{1,0:T(8,128)S(1)}, u32[]{:S(2)}, u32[]{:S(2)}) collective-permute-start(f32[48,128]{1,0:T(8,128)S(1)} %shard_map.59.refs_0_.refs_3_), channel_id=1, source_target_pairs={{0,3},{1,2},{2,1},{3,0},{4,7},{5,6},{6,5},{7,4},{8,11},{9,10},{10,... | collective-permute-start | bytes 73736 | tf_op jit(solution)/shard_map/ppermute | solution.py:464
  8.5 4.2 %collective-permute-start.3 = (f32[160,128]{1,0:T(8,128)S(1)}, f32[160,128]{1,0:T(8,128)S(1)}, u32[]{:S(2)}, u32[]{:S(2)}) collective-permute-start(f32[160,128]{1,0:T(8,128)S(1)} %pad_maximum_fusion), channel_id=1, source_target_pairs={{0,4},{4,0},{8,12},{12,8},{16,20},{20,16},{24,28},{28,24},{1,5},{5... | collective-permute-start | bytes 245768 | tf_op jit(solution)/shard_map/ppermute | solution.py:473
  10.9 4.1 %collective-permute-start.4 = (f32[160,128]{1,0:T(8,128)S(1)}, f32[160,128]{1,0:T(8,128)S(1)}, u32[]{:S(2)}, u32[]{:S(2)}) collective-permute-start(f32[160,128]{1,0:T(8,128)S(1)} %pad_maximum_fusion), channel_id=1, source_target_pairs={{0,1},{1,0},{2,3},{3,2},{4,8},{5,9},{6,10},{7,11},{8,4},{9,5},{10,... | collective-permute-start | bytes 245768 | tf_op jit(solution)/shard_map/ppermute | solution.py:474
  19.6 11.1 %copy-start = (f32[8,64]{1,0:T(8,128)S(1)}, f32[8,64]{1,0:T(8,128)}, u32[]{:S(2)}) copy-start(f32[8,64]{1,0:T(8,128)} %get-tuple-element.16.refs_3_) | copy-start | bytes 6148
  19.6 2.7 %collective-permute-start.5 = (f32[8,128]{1,0:T(8,128)S(1)}, f32[8,128]{1,0:T(8,128)S(1)}, u32[]{:S(2)}, u32[]{:S(2)}) collective-permute-start(f32[8,128]{1,0:T(8,128)S(1)} %get-tuple-element.27.refs_6_), channel_id=1, source_target_pairs={{0,1},{1,0},{2,3},{3,2},{4,5},{5,4},{6,7},{7,6},{8,9},{9,8},{10,11... | collective-permute-start | bytes 12296 | tf_op jit(solution)/shard_map/ppermute | solution.py:464
  19.9 2.5 %collective-permute-start.6 = (f32[8,128]{1,0:T(8,128)S(1)}, f32[8,128]{1,0:T(8,128)S(1)}, u32[]{:S(2)}, u32[]{:S(2)}) collective-permute-start(f32[8,128]{1,0:T(8,128)S(1)} %get-tuple-element.27.refs_6_), channel_id=1, source_target_pairs={{0,2},{1,3},{2,0},{3,1},{4,6},{5,7},{6,4},{7,5},{8,10},{9,11},{10,... | collective-permute-start | bytes 12296 | tf_op jit(solution)/shard_map/ppermute | solution.py:464
  19.9 3.4 %collective-permute-start.7 = (f32[8,128]{1,0:T(8,128)S(1)}, f32[8,128]{1,0:T(8,128)S(1)}, u32[]{:S(2)}, u32[]{:S(2)}) collective-permute-start(f32[8,128]{1,0:T(8,128)S(1)} %get-tuple-element.27.refs_6_), channel_id=1, source_target_pairs={{0,3},{1,2},{2,1},{3,0},{4,7},{5,6},{6,5},{7,4},{8,11},{9,10},{10,... | collective-permute-start | bytes 12296 | tf_op jit(solution)/shard_map/ppermute | solution.py:464
  23.2 7.5 %collective-permute-start.8 = (f32[32,128]{1,0:T(8,128)S(1)}, f32[32,128]{1,0:T(8,128)S(1)}, u32[]{:S(2)}, u32[]{:S(2)}) collective-permute-start(f32[32,128]{1,0:T(8,128)S(1)} %constant_dynamic-update-slice_fusion), channel_id=1, source_target_pairs={{0,4},{4,0},{8,12},{12,8},{16,20},{20,16},{24,28},{28,24},{1,5},{5... | collective-permute-start | bytes 49160 | tf_op jit(solution)/shard_map/ppermute | solution.py:473
  25.1 5.6 %collective-permute-start.9 = (f32[32,128]{1,0:T(8,128)S(1)}, f32[32,128]{1,0:T(8,128)S(1)}, u32[]{:S(2)}, u32[]{:S(2)}) collective-permute-start(f32[32,128]{1,0:T(8,128)S(1)} %constant_dynamic-update-slice_fusion), channel_id=1, source_target_pairs={{0,1},{1,0},{2,3},{3,2},{4,8},{5,9},{6,10},{7,11},{8,4},{9,5},{10,... | collective-permute-start | bytes 49160 | tf_op jit(solution)/shard_map/ppermute | solution.py:474
  32.9 2.7 %collective-permute-start.10 = (f32[24,128]{1,0:T(8,128)S(1)}, f32[24,128]{1,0:T(8,128)S(1)}, u32[]{:S(2)}, u32[]{:S(2)}) collective-permute-start(f32[24,128]{1,0:T(8,128)S(1)} %get-tuple-element.31.refs_8_), channel_id=1, source_target_pairs={{0,1},{1,0},{2,3},{3,2},{4,5},{5,4},{6,7},{7,6},{8,9},{9,8},{10,11... | collective-permute-start | bytes 36872 | tf_op jit(solution)/shard_map/ppermute | solution.py:464
  34.1 2.5 %collective-permute-start.11 = (f32[24,128]{1,0:T(8,128)S(1)}, f32[24,128]{1,0:T(8,128)S(1)}, u32[]{:S(2)}, u32[]{:S(2)}) collective-permute-start(f32[24,128]{1,0:T(8,128)S(1)} %get-tuple-element.31.refs_8_), channel_id=1, source_target_pairs={{0,2},{1,3},{2,0},{3,1},{4,6},{5,7},{6,4},{7,5},{8,10},{9,11},{10,... | collective-permute-start | bytes 36872 | tf_op jit(solution)/shard_map/ppermute | solution.py:464
  35.4 3.4 %collective-permute-start.12 = (f32[24,128]{1,0:T(8,128)S(1)}, f32[24,128]{1,0:T(8,128)S(1)}, u32[]{:S(2)}, u32[]{:S(2)}) collective-permute-start(f32[24,128]{1,0:T(8,128)S(1)} %get-tuple-element.31.refs_8_), channel_id=1, source_target_pairs={{0,3},{1,2},{2,1},{3,0},{4,7},{5,6},{6,5},{7,4},{8,11},{9,10},{10,... | collective-permute-start | bytes 36872 | tf_op jit(solution)/shard_map/ppermute | solution.py:464
  38.8 7.7 %collective-permute-start.13 = (f32[96,128]{1,0:T(8,128)S(1)}, f32[96,128]{1,0:T(8,128)S(1)}, u32[]{:S(2)}, u32[]{:S(2)}) collective-permute-start(f32[96,128]{1,0:T(8,128)S(1)} %constant_dynamic-update-slice_fusion.4), channel_id=1, source_target_pairs={{0,4},{4,0},{8,12},{12,8},{16,20},{20,16},{24,28},{28,24},{1,5},{5... | collective-permute-start | bytes 147464 | tf_op jit(solution)/shard_map/ppermute | solution.py:473
  40.5 6.1 %collective-permute-start.14 = (f32[96,128]{1,0:T(8,128)S(1)}, f32[96,128]{1,0:T(8,128)S(1)}, u32[]{:S(2)}, u32[]{:S(2)}) collective-permute-start(f32[96,128]{1,0:T(8,128)S(1)} %constant_dynamic-update-slice_fusion.4), channel_id=1, source_target_pairs={{0,1},{1,0},{2,3},{3,2},{4,8},{5,9},{6,10},{7,11},{8,4},{9,5},{10,... | collective-permute-start | bytes 147464 | tf_op jit(solution)/shard_map/ppermute | solution.py:474
